TPU v7x, 32 devices: a whole 2x2x4 slice. The times are simulated.
32 devices in a mesh: dp: 8 (over z, y), tensor: 4 (over x, core).
Axes of the slice: x: 2, y: 2, z: 4, core: 2. Of those that a mesh axis runs over, the one named last changes fastest.
Arguments:
- block_input: bfloat16 [8192, 1536], P('dp'), may hold values from -6 to 6
- segments: int32 [8192], P('dp'), may hold values from 0 to 31, never falling along the last dimension, each value on 1 to 2048 neighbouring positions
- positions: int32 [8192], P('dp'), may hold values from 0 to 1023
- norm1_gain: float32 [1536], P('dp'), may hold values from 0.5 to 1.5
- q_norm_gain: float32 [64], P('dp'), may hold values from 0.5 to 1.5
- k_norm_gain: float32 [64], P('dp'), may hold values from 0.5 to 1.5
- w_q: float32 [1536, 1536], P('dp', 'tensor'), may hold values from -0.15625 to 0.15625
- w_k: float32 [1536, 512], P('dp', 'tensor'), may hold values from -0.15625 to 0.15625
- w_v: float32 [1536, 512], P('dp', 'tensor'), may hold values from -0.15625 to 0.15625
- w_o: float32 [1536, 1536], P('tensor', 'dp'), may hold values from -0.625 to 0.625
- norm2_gain: float32 [1536], P('dp'), may hold values from 0.5 to 1.5
- w_gate: float32 [1536, 6912], P('dp', 'tensor'), may hold values from -0.15625 to 0.15625
- w_up: float32 [1536, 6912], P('dp', 'tensor'), may hold values from -0.15625 to 0.15625
- w_down: float32 [6912, 1536], P('tensor', 'dp'), may hold values from -0.078125 to 0.078125
- cotangent: bfloat16 [8192, 1536], P('dp'), may hold values from -6 to 6
Outputs:
- block_output: bfloat16 [8192, 1536], P('dp')
- input_grad: float32 [8192, 1536], P('dp')
- norm1_gain_grad: float32 [1536], P('dp')
- q_norm_gain_grad: float32 [64], P('dp')
- k_norm_gain_grad: float32 [64], P('dp')
- w_q_grad: float32 [1536, 1536], P('dp', 'tensor')
- w_k_grad: float32 [1536, 512], P('dp', 'tensor')
- w_v_grad: float32 [1536, 512], P('dp', 'tensor')
- w_o_grad: float32 [1536, 1536], P('tensor', 'dp')
- norm2_gain_grad: float32 [1536], P('dp')
- w_gate_grad: float32 [1536, 6912], P('dp', 'tensor')
- w_up_grad: float32 [1536, 6912], P('dp', 'tensor')
- w_down_grad: float32 [6912, 1536], P('tensor', 'dp')
Inputs may be any that keep to these rules, and one draw needn't show every extreme that they name: `segments`: segment numbers never fall along the tokens; a document holds at most 2048 tokens, and some document holds exactly that many; a document that runs across the end of a 1024-token sequence is attended only within each sequence.
All inputs are finite; a program needn't handle non-finite values.
Results may differ from a plain program's by a relative error of at most 0.014.
The roundings to bfloat16 on the way count: a program that leaves them out, or rounds other values in their place, can miss the bound.
Values may be sent and summed in bfloat16 or wider, within the bound.
A program may use at most 192 MiB of HBM per device.

v0:
```python
import jax
import jax.numpy as jnp
from jax import lax
from jax.sharding import PartitionSpec as P

EPSILON = 1e-05
ROPE_BASE = 1000000.0
MASKED = -1e30


def rotation_tables(positions, head_dim):
    half_dim = head_dim // 2
    frequency = ROPE_BASE ** (-jnp.arange(half_dim, dtype=jnp.float32) * 2.0 / head_dim)
    angles = positions.astype(jnp.float32)[:, None] * frequency[None, :]
    return (jnp.cos(angles)[:, None, :], jnp.sin(angles)[:, None, :])


def rotate(values, cosine, sine):
    half_dim = values.shape[-1] // 2
    first_half = values[..., :half_dim]
    second_half = values[..., half_dim:]
    return jnp.concatenate(
        [first_half * cosine - second_half * sine, second_half * cosine + first_half * sine],
        axis=-1,
    )


def rotate_back(grads, cosine, sine):
    half_dim = grads.shape[-1] // 2
    first_half = grads[..., :half_dim]
    second_half = grads[..., half_dim:]
    return jnp.concatenate(
        [first_half * cosine + second_half * sine, second_half * cosine - first_half * sine],
        axis=-1,
    )


def norm_forward(values, gain):
    inverse = lax.rsqrt(jnp.mean(values * values, axis=-1, keepdims=True) + EPSILON)
    return (values * inverse * gain, inverse)


def norm_backward(values, inverse, gain, grad_out):
    scaled = grad_out * gain
    inner_mean = jnp.mean(scaled * values, axis=-1, keepdims=True)
    return inverse * scaled - values * (inverse * inverse * inverse) * inner_mean


def matmul(left_op, right_op):
    return jnp.dot(left_op, right_op, preferred_element_type=jnp.float32)


def matmul_tn(left_op, right_op):
    return lax.dot_general(
        left_op, right_op, (((0,), (0,)), ((), ())), preferred_element_type=jnp.float32
    )


def matmul_nt(left_op, right_op):
    return lax.dot_general(
        left_op, right_op, (((1,), (1,)), ((), ())), preferred_element_type=jnp.float32
    )


def gather_attention(norm1_gain, q_norm_gain, k_norm_gain, w_q, w_k, w_v, w_o):
    return (
        lax.all_gather(norm1_gain.astype(jnp.bfloat16), "dp", axis=0, tiled=True),
        lax.all_gather(q_norm_gain.astype(jnp.bfloat16), "dp", axis=0, tiled=True),
        lax.all_gather(k_norm_gain.astype(jnp.bfloat16), "dp", axis=0, tiled=True),
        lax.all_gather(w_q.astype(jnp.bfloat16), "dp", axis=0, tiled=True),
        lax.all_gather(w_k.astype(jnp.bfloat16), "dp", axis=0, tiled=True),
        lax.all_gather(w_v.astype(jnp.bfloat16), "dp", axis=0, tiled=True),
        lax.all_gather(w_o.astype(jnp.bfloat16), "dp", axis=1, tiled=True),
    )


def gather_mlp(norm2_gain, w_gate, w_up, w_down):
    return (
        lax.all_gather(norm2_gain.astype(jnp.bfloat16), "dp", axis=0, tiled=True),
        lax.all_gather(w_gate.astype(jnp.bfloat16), "dp", axis=0, tiled=True),
        lax.all_gather(w_up.astype(jnp.bfloat16), "dp", axis=0, tiled=True),
        lax.all_gather(w_down.astype(jnp.bfloat16), "dp", axis=1, tiled=True),
    )


def block_logits(query_part, key_part, segments, first_row, last_row, scale):
    raw_scores = (
        jnp.einsum("qkgd,skd->kgqs", query_part, key_part, preferred_element_type=jnp.float32)
        * scale
    )
    row_ids = jnp.arange(first_row, last_row)
    col_ids = jnp.arange(last_row)
    allowed = (segments[first_row:last_row][:, None] == segments[:last_row][None, :]) & (
        row_ids[:, None] >= col_ids[None, :]
    )
    return jnp.where(allowed[None, None], raw_scores, MASKED)


def attention_forward(query_b, key_b, value_b, segments, scale):
    seq_len = query_b.shape[0]
    block_rows = min(512, seq_len)
    pieces = []
    logsums = []
    for block_index in range(seq_len // block_rows):
        first_row = block_index * block_rows
        last_row = first_row + block_rows
        logits = block_logits(
            query_b[first_row:last_row], key_b[:last_row], segments, first_row, last_row, scale
        )
        maxima = jnp.max(logits, axis=-1, keepdims=True)
        expo_terms = jnp.exp(logits - maxima)
        totals = jnp.sum(expo_terms, axis=-1, keepdims=True)
        probs_low = (expo_terms / totals).astype(jnp.bfloat16)
        pieces.append(
            jnp.einsum(
                "kgqs,skd->qkgd", probs_low, value_b[:last_row], preferred_element_type=jnp.float32
            )
        )
        logsums.append(maxima + jnp.log(totals))
    return (jnp.concatenate(pieces, axis=0), logsums)


def attention_backward(query_b, key_b, value_b, grad_context, logsums, segments, scale):
    seq_len = query_b.shape[0]
    block_rows = min(512, seq_len)
    grad_query = []
    grad_key = jnp.zeros(key_b.shape, jnp.float32)
    grad_value = jnp.zeros(value_b.shape, jnp.float32)
    for block_index in range(seq_len // block_rows):
        first_row = block_index * block_rows
        last_row = first_row + block_rows
        query_part = query_b[first_row:last_row]
        grad_part = grad_context[first_row:last_row]
        logits = block_logits(query_part, key_b[:last_row], segments, first_row, last_row, scale)
        probs_soft = jnp.exp(logits - logsums[block_index])
        grad_probs = jnp.einsum(
            "qkgd,skd->kgqs", grad_part, value_b[:last_row], preferred_element_type=jnp.float32
        )
        row_inner = jnp.sum(probs_soft * grad_probs, axis=-1, keepdims=True)
        grad_scores = (probs_soft * (grad_probs - row_inner)).astype(jnp.bfloat16)
        grad_query.append(
            jnp.einsum(
                "kgqs,skd->qkgd", grad_scores, key_b[:last_row], preferred_element_type=jnp.float32
            )
            * scale
        )
        grad_key = grad_key.at[:last_row].add(
            jnp.einsum(
                "kgqs,qkgd->skd", grad_scores, query_part, preferred_element_type=jnp.float32
            )
            * scale
        )
        grad_value = grad_value.at[:last_row].add(
            jnp.einsum(
                "kgqs,qkgd->skd",
                probs_soft.astype(jnp.bfloat16),
                grad_part,
                preferred_element_type=jnp.float32,
            )
        )
    return (jnp.concatenate(grad_query, axis=0), grad_key, grad_value)


def shards(
    block_input,
    segments,
    positions,
    norm1_gain,
    q_norm_gain,
    k_norm_gain,
    w_q,
    w_k,
    w_v,
    w_o,
    norm2_gain,
    w_gate,
    w_up,
    w_down,
    cotangent,
):
    attn_full = gather_attention(norm1_gain, q_norm_gain, k_norm_gain, w_q, w_k, w_v, w_o)
    mlp_full = gather_mlp(norm2_gain, w_gate, w_up, w_down)
    gain_one, gain_query, gain_key, weight_q, weight_k, weight_v, weight_o = attn_full
    gain_two, weight_gate, weight_up, weight_down = mlp_full
    seq_len = block_input.shape[0]
    head_dim = gain_query.shape[0]
    local_heads = weight_q.shape[1] // head_dim
    local_kv = weight_k.shape[1] // head_dim
    group_size = local_heads // local_kv
    scale = head_dim ** (-0.5)
    cosine, sine = rotation_tables(positions, head_dim)
    rows_in = block_input.astype(jnp.float32)
    normed, inverse_one = norm_forward(rows_in, gain_one.astype(jnp.float32))
    normed_b = normed.astype(jnp.bfloat16)
    query = matmul(normed_b, weight_q).reshape(seq_len, local_heads, head_dim)
    keyed = matmul(normed_b, weight_k).reshape(seq_len, local_kv, head_dim)
    value_b = matmul(normed_b, weight_v).astype(jnp.bfloat16).reshape(seq_len, local_kv, head_dim)
    query_normed, query_inverse = norm_forward(query, gain_query.astype(jnp.float32))
    key_normed, key_inverse = norm_forward(keyed, gain_key.astype(jnp.float32))
    query_b = (
        rotate(query_normed, cosine, sine)
        .astype(jnp.bfloat16)
        .reshape(seq_len, local_kv, group_size, head_dim)
    )
    key_b = rotate(key_normed, cosine, sine).astype(jnp.bfloat16)
    context, logsums = attention_forward(query_b, key_b, value_b, segments, scale)
    context_b = context.reshape(seq_len, local_heads * head_dim).astype(jnp.bfloat16)
    attn_total = lax.psum(matmul(context_b, weight_o), "tensor")
    residual = rows_in + attn_total
    normed_two, inverse_two = norm_forward(residual, gain_two.astype(jnp.float32))
    normed_two_b = normed_two.astype(jnp.bfloat16)
    gated = matmul(normed_two_b, weight_gate)
    upward = matmul(normed_two_b, weight_up)
    sigmoid_gate = jax.nn.sigmoid(gated)
    inner_b = (gated * sigmoid_gate * upward).astype(jnp.bfloat16)
    mlp_total = lax.psum(matmul(inner_b, weight_down).astype(jnp.bfloat16), "tensor").astype(
        jnp.float32
    )
    output_rows = (residual + mlp_total).astype(jnp.bfloat16)
    gain_two, weight_gate, weight_up, weight_down = mlp_full
    grad_out = cotangent.astype(jnp.float32)
    grad_down = matmul_tn(inner_b, cotangent)
    grad_inner = matmul_nt(cotangent, weight_down)
    grad_up_b = (grad_inner * gated * sigmoid_gate).astype(jnp.bfloat16)
    grad_gate_b = (
        grad_inner * upward * sigmoid_gate * (1.0 + gated * (1.0 - sigmoid_gate))
    ).astype(jnp.bfloat16)
    grad_gate_w = matmul_tn(normed_two_b, grad_gate_b)
    grad_up_w = matmul_tn(normed_two_b, grad_up_b)
    grad_normed_two = lax.psum(
        matmul_nt(grad_gate_b, weight_gate) + matmul_nt(grad_up_b, weight_up), "tensor"
    )
    grad_gain_two = jnp.sum(grad_normed_two * residual * inverse_two, axis=0)
    grad_residual = grad_out + norm_backward(
        residual, inverse_two, gain_two.astype(jnp.float32), grad_normed_two
    )
    gain_one, gain_query, gain_key, weight_q, weight_k, weight_v, weight_o = attn_full
    grad_res_b = grad_residual.astype(jnp.bfloat16)
    grad_out_w = matmul_tn(context_b, grad_res_b)
    grad_context = (
        matmul_nt(grad_res_b, weight_o)
        .astype(jnp.bfloat16)
        .reshape(seq_len, local_kv, group_size, head_dim)
    )
    grad_query, grad_key, grad_value = attention_backward(
        query_b, key_b, value_b, grad_context, logsums, segments, scale
    )
    grad_query = rotate_back(grad_query.reshape(seq_len, local_heads, head_dim), cosine, sine)
    grad_key = rotate_back(grad_key, cosine, sine)
    grad_gain_q = jnp.sum(grad_query * query * query_inverse, axis=(0, 1))
    grad_gain_k = jnp.sum(grad_key * keyed * key_inverse, axis=(0, 1))
    grad_q_low = (
        norm_backward(query, query_inverse, gain_query.astype(jnp.float32), grad_query)
        .astype(jnp.bfloat16)
        .reshape(seq_len, local_heads * head_dim)
    )
    grad_k_low = (
        norm_backward(keyed, key_inverse, gain_key.astype(jnp.float32), grad_key)
        .astype(jnp.bfloat16)
        .reshape(seq_len, local_kv * head_dim)
    )
    grad_v_low = grad_value.astype(jnp.bfloat16).reshape(seq_len, local_kv * head_dim)
    grad_wq = matmul_tn(normed_b, grad_q_low)
    grad_wk = matmul_tn(normed_b, grad_k_low)
    grad_wv = matmul_tn(normed_b, grad_v_low)
    normed_part = (
        matmul_nt(grad_q_low, weight_q)
        + matmul_nt(grad_k_low, weight_k)
        + matmul_nt(grad_v_low, weight_v)
    )
    grad_normed, grad_gain_q, grad_gain_k = lax.psum(
        (normed_part, grad_gain_q, grad_gain_k), "tensor"
    )
    grad_gain_one = jnp.sum(grad_normed * rows_in * inverse_one, axis=0)
    grad_input = grad_residual + norm_backward(
        rows_in, inverse_one, gain_one.astype(jnp.float32), grad_normed
    )
    shares = tuple(
        (
            lax.psum_scatter(grad_gain_one, "dp", scatter_dimension=0, tiled=True),
            lax.psum_scatter(grad_gain_q, "dp", scatter_dimension=0, tiled=True),
            lax.psum_scatter(grad_gain_k, "dp", scatter_dimension=0, tiled=True),
            lax.psum_scatter(grad_wq, "dp", scatter_dimension=0, tiled=True),
            lax.psum_scatter(grad_wk, "dp", scatter_dimension=0, tiled=True),
            lax.psum_scatter(grad_wv, "dp", scatter_dimension=0, tiled=True),
            lax.psum_scatter(grad_out_w, "dp", scatter_dimension=1, tiled=True),
            lax.psum_scatter(grad_gain_two, "dp", scatter_dimension=0, tiled=True),
            lax.psum_scatter(grad_gate_w, "dp", scatter_dimension=0, tiled=True),
            lax.psum_scatter(grad_up_w, "dp", scatter_dimension=0, tiled=True),
            lax.psum_scatter(grad_down, "dp", scatter_dimension=1, tiled=True),
        )
    )
    return (
        output_rows,
        grad_input,
        shares[0],
        shares[1],
        shares[2],
        shares[3],
        shares[4],
        shares[5],
        shares[6],
        shares[7],
        shares[8],
        shares[9],
        shares[10],
    )


def solution(mesh):
    placed = (
        P("dp", None),
        P("dp"),
        P("dp"),
        P("dp"),
        P("dp"),
        P("dp"),
        P("dp", "tensor"),
        P("dp", "tensor"),
        P("dp", "tensor"),
        P("tensor", "dp"),
        P("dp"),
        P("dp", "tensor"),
        P("dp", "tensor"),
        P("tensor", "dp"),
        P("dp", None),
    )
    return jax.shard_map(
        shards,
        mesh=mesh,
        in_specs=placed,
        out_specs=(
            P("dp", None),
            P("dp", None),
            P("dp"),
            P("dp"),
            P("dp"),
            P("dp", "tensor"),
            P("dp", "tensor"),
            P("dp", "tensor"),
            P("tensor", "dp"),
            P("dp"),
            P("dp", "tensor"),
            P("dp", "tensor"),
            P("tensor", "dp"),
        ),
        check_vma=False,
    )
```

profile of v0, /device:TPU:0, one launch (start us, length us, event | category | flops | bytes accessed | tf_op | source)
XLA Modules:
  0.0 1790.7 jit_solution(7389086550737440357)
XLA Ops:
  20.2 24.5 %all-reduce.12 = (bf16[1536]{0:T(1024)(128)(2,1)S(1)}, bf16[64]{0:T(256)(128)(2,1)S(1)}, bf16[64]{0:T(256)(128)(2,1)S(1)}, bf16[1536]{0:T(1024)(128)(2,1)}) all-reduce(bf16[1536]{0:T(1024)(128)(2,1)S(1)} %dynamic-update-slice.10, bf16[64]{0:T(256)(128)(2,1)S(1)} %dynamic-update-slice.12, ...), channel_id=1, replica_groups=mesh['dp'=8,'tensor'=4] {'dp'}, use_global_device_ids=true, to_apply=%add.2 | all-reduce | flops 3200 | bytes 12800
  48.8 31.0 %all_gather.34 = bf16[1536,128]{1,0:T(8,128)(2,1)S(1)} all-gather(bf16[192,128]{1,0:T(8,128)(2,1)S(1)} %convert_element_type.130), channel_id=1, replica_groups=mesh['dp'=8,'tensor'=4] {'dp'}, dimensions={0}, use_global_device_ids=true | all-gather | bytes 442368 | tf_op jit(solution)/shard_map/all_gather | solution.py:72
  79.8 32.0 %all_gather.35 = bf16[1536,128]{1,0:T(8,128)(2,1)S(1)} all-gather(bf16[192,128]{1,0:T(8,128)(2,1)S(1)} %convert_element_type.132), channel_id=1, replica_groups=mesh['dp'=8,'tensor'=4] {'dp'}, dimensions={0}, use_global_device_ids=true | all-gather | bytes 442368 | tf_op jit(solution)/shard_map/all_gather | solution.py:71
  132.3 13.2 fusion.3
  163.1 108.4 %all-reduce.18.cloned.1.call-done = f32[1024,1536]{1,0:T(8,128)} async-done(((f32[1024,1536]{1,0:T(8,128)}), f32[1024,1536]{1,0:T(8,128)}) %all-reduce.18.cloned.1.call-update) | async-done | bytes 6291472 | tf_op jit(solution)/shard_map/psum | solution.py:208
  278.5 85.3 %all-gather.12.cloned.1.call-done = bf16[1536,1728]{1,0:T(8,128)(2,1)} async-done(((bf16[192,1728]{1,0:T(8,128)(2,1)}), bf16[1536,1728]{1,0:T(8,128)(2,1)}) %all-gather.12.cloned.1.call-update) | async-done | bytes 5308432 | tf_op jit(solution)/shard_map/all_gather | solution.py:81
  363.8 10.4 fusion.85
  374.2 79.9 %all-gather.10.cloned.1.call-done = bf16[1536,1728]{1,0:T(8,128)(2,1)} async-done(((bf16[192,1728]{1,0:T(8,128)(2,1)}), bf16[1536,1728]{1,0:T(8,128)(2,1)}) %all-gather.10.cloned.1.call-update) | async-done | bytes 5308432 | tf_op jit(solution)/shard_map/all_gather | solution.py:80
  454.1 10.8 fusion.84
  464.8 79.5 %all-gather.14.cloned.1.call-done = bf16[1728,1536]{0,1:T(8,128)(2,1)} async-done(((bf16[1728,192]{0,1:T(8,128)(2,1)}), bf16[1728,1536]{0,1:T(8,128)(2,1)}) %all-gather.14.cloned.1.call-update) | async-done | bytes 5308432 | tf_op jit(solution)/shard_map/all_gather | solution.py:82
  544.4 16.2 multiply_convert_fusion
  560.5 9.7 fusion.86
  570.3 9.8 convolution_add_fusion
  580.2 10.2 convolution_convert_fusion
  592.5 105.5 %all-reduce.22.cloned.1.call-done = f32[1024,1536]{1,0:T(8,128)} async-done(((f32[1024,1536]{1,0:T(8,128)}), f32[1024,1536]{1,0:T(8,128)}) %all-reduce.22.cloned.1.call-update) | async-done | bytes 6291472 | tf_op jit(solution)/shard_map/psum | solution.py:230
  698.0 6.5 multiply_reduce_fusion
  704.5 65.2 %all-reduce.20.cloned.1.call-done = bf16[1024,1536]{1,0:T(8,128)(2,1)} async-done(((bf16[1024,1536]{1,0:T(8,128)(2,1)}), bf16[1024,1536]{1,0:T(8,128)(2,1)}) %all-reduce.20.cloned.1.call-update) | async-done | bytes 3145744 | tf_op jit(solution)/shard_map/psum | solution.py:216
  769.7 9.4 subtract_add_fusion
  801.2 7.0 fusion.2
  839.9 11.1 fusion.94
  852.9 10.7 fusion.93
  863.9 10.6 fusion.92
  875.5 66.2 %all-reduce.24.cloned.1.call-done = f32[1024,1536]{1,0:T(8,128)} async-done(((f32[1024,1536]{1,0:T(8,128)}), f32[1024,1536]{1,0:T(8,128)}) %all-reduce.24.cloned.1.call-update) | async-done | bytes 6291472 | tf_op jit(solution)/shard_map/psum | solution.py:271
  945.9 37.2 %all-reduce.10 = (f32[1536]{0:T(1024)S(1)}, f32[64]{0:T(128)S(1)}, f32[64]{0:T(128)S(1)}, f32[1536]{0:T(1024)S(1)}) all-reduce(f32[1536]{0:T(1024)S(1)} %get-tuple-element.79, f32[64]{0:T(128)S(1)} %reduce_sum.173, f32[64]{0:T(128)S(1)} %reduce_sum.176, f32[1536]{0:T(1024)S(1)} %copy-done.62), channel_id=2, replica_groups=mesh['dp'=8,'tensor'=4] {'dp'}, use_global_device_ids=true, to_apply=%region_19.20.clone | all-reduce | flops 3200 | bytes 25600
  991.4 7.2 fusion.12
  998.6 9.6 reduce-scatter.12.cloned.1.call-done
  1008.2 65.8 %reduce-scatter.10.cloned.1.call-done = f32[192,128]{1,0:T(8,128)} async-done(((f32[1536,128]{1,0:T(8,128)}), f32[192,128]{1,0:T(8,128)}) %reduce-scatter.10.cloned.1.call-update) | async-done | bytes 98320 | tf_op jit(solution)/shard_map/reduce_scatter | solution.py:284
  1073.9 72.1 %reduce-scatter.14.cloned.1.call-done = f32[384,192]{0,1:T(8,128)} async-done(((f32[384,1536]{0,1:T(8,128)}), f32[384,192]{0,1:T(8,128)}) %reduce-scatter.14.cloned.1.call-update) | async-done | bytes 294928 | tf_op jit(solution)/shard_map/reduce_scatter | solution.py:286
  1146.1 72.3 %reduce-scatter.8.cloned.1.call-done = f32[192,384]{1,0:T(8,128)} async-done(((f32[1536,384]{1,0:T(8,128)}), f32[192,384]{1,0:T(8,128)}) %reduce-scatter.8.cloned.1.call-update) | async-done | bytes 294928 | tf_op jit(solution)/shard_map/reduce_scatter | solution.py:283
  1218.4 188.5 %reduce-scatter.20.cloned.1.call-done = f32[1728,192]{0,1:T(8,128)} async-done(((f32[1728,1536]{0,1:T(8,128)}), f32[1728,192]{0,1:T(8,128)}) %reduce-scatter.20.cloned.1.call-update) | async-done | bytes 1327120 | tf_op jit(solution)/shard_map/reduce_scatter | solution.py:290
  1406.9 188.6 %reduce-scatter.18.cloned.1.call-done = f32[192,1728]{1,0:T(8,128)} async-done(((f32[1536,1728]{1,0:T(8,128)}), f32[192,1728]{1,0:T(8,128)}) %reduce-scatter.18.cloned.1.call-update) | async-done | bytes 1327120 | tf_op jit(solution)/shard_map/reduce_scatter | solution.py:289
  1595.5 188.5 %reduce-scatter.16.cloned.1.call-done = f32[192,1728]{1,0:T(8,128)} async-done(((f32[1536,1728]{1,0:T(8,128)}), f32[192,1728]{1,0:T(8,128)}) %reduce-scatter.16.cloned.1.call-update) | async-done | bytes 1327120 | tf_op jit(solution)/shard_map/reduce_scatter | solution.py:288
  (300 shorter events, 129.9 us)
Async XLA Ops:
  7.2 114.7 %all-gather.6.cloned.1.call-start = ((), (), s32[]{:S(2)}) async-start(), calls=%async_computation.7 | async-start | bytes 1327104 | tf_op jit(solution)/shard_map/all_gather | solution.py:70
  8.9 139.2 %all-gather.8.cloned.1.call-start = ((), (), s32[]{:S(2)}) async-start(), calls=%async_computation.8 | async-start | bytes 1327104 | tf_op jit(solution)/shard_map/all_gather | solution.py:73
  10.6 260.9 %all-reduce.18.cloned.1.call-start = ((), (), s32[]{:S(2)}) async-start(), calls=%async_computation.9 | async-start | bytes 12582912 | tf_op jit(solution)/shard_map/psum | solution.py:208
  44.7 80.8 %copy-start.69 = (f32[64]{0:T(128)}, f32[64]{0:T(128)S(1)}, u32[]{:S(2)}) copy-start(f32[64]{0:T(128)S(1)} %convert_element_type.138) | copy-start | bytes 772
  44.7 76.3 %copy-start.67 = (f32[64]{0:T(128)}, f32[64]{0:T(128)S(1)}, u32[]{:S(2)}) copy-start(f32[64]{0:T(128)S(1)} %convert_element_type.134) | copy-start | bytes 772
  44.7 73.7 %copy-start.45 = (f32[1536]{0:T(1024)}, f32[1536]{0:T(1024)S(1)}, u32[]{:S(2)}) copy-start(f32[1536]{0:T(1024)S(1)} %convert_element_type.128) | copy-start | bytes 18436
  45.3 73.1 %copy-start.59 = (f32[1024]{0:T(1024)}, f32[1024]{0:T(1024)S(1)}, u32[]{:S(2)}) copy-start(f32[1024]{0:T(1024)S(1)} %get-tuple-element.125) | copy-start | bytes 12292
  154.1 117.3 %copy-start.6 = (bf16[1024,1536]{1,0:T(8,128)(2,1)S(1)}, bf16[1024,1536]{1,0:T(8,128)(2,1)}, u32[]{:S(2)}) copy-start(bf16[1024,1536]{1,0:T(8,128)(2,1)} %param.27) | copy-start | bytes 9437188
  154.2 209.6 %all-gather.12.cloned.1.call-start = ((), (), s32[]{:S(2)}) async-start(), calls=%async_computation.11 | async-start | bytes 6193152 | tf_op jit(solution)/shard_map/all_gather | solution.py:81
  156.7 297.4 %all-gather.10.cloned.1.call-start = ((), (), s32[]{:S(2)}) async-start(), calls=%async_computation.10 | async-start | bytes 6193152 | tf_op jit(solution)/shard_map/all_gather | solution.py:80
  159.4 385.0 %all-gather.14.cloned.1.call-start = ((), (), s32[]{:S(2)}) async-start(), calls=%async_computation.12 | async-start | bytes 6193152 | tf_op jit(solution)/shard_map/all_gather | solution.py:82
  161.7 536.3 %all-reduce.22.cloned.1.call-start = ((), (), s32[]{:S(2)}) async-start(), calls=%async_computation.14 | async-start | bytes 12582912 | tf_op jit(solution)/shard_map/psum | solution.py:230
  278.5 85.3 %copy-start.24 = (bf16[1024,1536]{1,0:T(8,128)(2,1)}, bf16[1024,1536]{1,0:T(8,128)(2,1)S(1)}, u32[]{:S(2)}) copy-start(bf16[1024,1536]{1,0:T(8,128)(2,1)S(1)} %multiply_convert_fusion.3) | copy-start | bytes 9437188
  374.2 170.2 %copy-start.23 = (bf16[1024,1536]{1,0:T(8,128)(2,1)S(1)}, bf16[1024,1536]{1,0:T(8,128)(2,1)}, u32[]{:S(2)}) copy-start(bf16[1024,1536]{1,0:T(8,128)(2,1)} %param.41) | copy-start | bytes 9437188
  580.1 189.6 %all-reduce.20.cloned.1.call-start = ((), (), s32[]{:S(2)}) async-start(), calls=%async_computation.13 | async-start | bytes 6291456 | tf_op jit(solution)/shard_map/psum | solution.py:216
  580.2 117.8 %copy-start.48 = (f32[1536]{0:T(1024)S(1)}, f32[1536]{0:T(1024)}, u32[]{:S(2)}) copy-start(f32[1536]{0:T(1024)} %convert_element_type.144) | copy-start | bytes 18436
  580.2 117.8 %copy-start.52 = (f32[1024]{0:T(1024)S(1)}, f32[1024]{0:T(1024)}, u32[]{:S(2)}) copy-start(f32[1024]{0:T(1024)} %copy-done.51) | copy-start | bytes 12292
  590.5 351.2 %all-reduce.24.cloned.1.call-start = ((), (), s32[]{:S(2)}) async-start(), calls=%async_computation.15 | async-start | bytes 12582912 | tf_op jit(solution)/shard_map/psum | solution.py:271
  592.5 177.1 %copy-start.63 = (f32[1024]{0:T(1024)S(1)}, f32[1024]{0:T(1024)}, u32[]{:S(2)}) copy-start(f32[1024]{0:T(1024)} %get-tuple-element.126) | copy-start | bytes 12292
  698.0 82.5 %slice-start.3 = ((s8[6291456]{0:T(1024)(128)(4,1)}), s8[2097152]{0:T(1024)(128)(4,1)S(1)}, s32[]{:S(2)}) async-start(s8[6291456]{0:T(1024)(128)(4,1)} %bitcast.213), calls=%async_computation.26 | async-start | bytes 4194304
  821.8 186.4 %reduce-scatter.12.cloned.1.call-start = ((), (), s32[]{:S(2)}) async-start(), calls=%async_computation.18 | async-start | bytes 884736 | tf_op jit(solution)/shard_map/reduce_scatter | solution.py:285
  826.5 247.4 %reduce-scatter.10.cloned.1.call-start = ((), (), s32[]{:S(2)}) async-start(), calls=%async_computation.17 | async-start | bytes 884736 | tf_op jit(solution)/shard_map/reduce_scatter | solution.py:284
  828.5 317.5 %reduce-scatter.14.cloned.1.call-start = ((), (), s32[]{:S(2)}) async-start(), calls=%async_computation.19 | async-start | bytes 2654208 | tf_op jit(solution)/shard_map/reduce_scatter | solution.py:286
  835.4 383.0 %reduce-scatter.8.cloned.1.call-start = ((), (), s32[]{:S(2)}) async-start(), calls=%async_computation.16 | async-start | bytes 2654208 | tf_op jit(solution)/shard_map/reduce_scatter | solution.py:283
  839.9 567.0 %reduce-scatter.20.cloned.1.call-start = ((), (), s32[]{:S(2)}) async-start(), calls=%async_computation.22 | async-start | bytes 12386304 | tf_op jit(solution)/shard_map/reduce_scatter | solution.py:290
  851.1 744.4 %reduce-scatter.18.cloned.1.call-start = ((), (), s32[]{:S(2)}) async-start(), calls=%async_computation.21 | async-start | bytes 12386304 | tf_op jit(solution)/shard_map/reduce_scatter | solution.py:289
  863.6 920.3 %reduce-scatter.16.cloned.1.call-start = ((), (), s32[]{:S(2)}) async-start(), calls=%async_computation.20 | async-start | bytes 12386304 | tf_op jit(solution)/shard_map/reduce_scatter | solution.py:288
  874.4 67.2 %copy-start.7 = (bf16[1024,1536]{1,0:T(8,128)(2,1)S(1)}, bf16[1024,1536]{1,0:T(8,128)(2,1)}, u32[]{:S(2)}) copy-start(bf16[1024,1536]{1,0:T(8,128)(2,1)} %param.27) | copy-start | bytes 9437188
  874.4 67.2 %copy-start.46 = (f32[1536]{0:T(1024)S(1)}, f32[1536]{0:T(1024)}, u32[]{:S(2)}) copy-start(f32[1536]{0:T(1024)} %copy-done.45) | copy-start | bytes 18436
  874.4 67.2 %copy-start.60 = (f32[1024]{0:T(1024)S(1)}, f32[1024]{0:T(1024)}, u32[]{:S(2)}) copy-start(f32[1024]{0:T(1024)} %copy-done.59) | copy-start | bytes 12292
  874.5 71.4 %copy-start.62 = (f32[1536]{0:T(1024)S(1)}, f32[1536]{0:T(1024)}, u32[]{:S(2)}) copy-start(f32[1536]{0:T(1024)} %get-tuple-element.77) | copy-start | bytes 18436
  874.5 116.9 %copy-start.65 = (f32[1024]{0:T(1024)S(1)}, f32[1024]{0:T(1024)}, u32[]{:S(2)}) copy-start(f32[1024]{0:T(1024)} %get-tuple-element.124) | copy-start | bytes 12292
  (66 other events, 470.0 us)
Sparse Core Ops, SparseCore 0:
  10.8 44.1 all-gather.5
  57.7 42.0 all-gather.7
  154.3 117.1 all-reduce.17
  274.1 89.6 all-gather.11
  366.4 87.6 all-gather.9
  456.7 87.6 all-gather.13
  580.2 117.7 all-reduce.21
  701.0 68.6 all-reduce.19
  821.9 119.6 all-reduce.23
  945.4 62.7 reduce-scatter.11
  1012.4 61.5 reduce-scatter.9
  1077.9 68.1 reduce-scatter.13
  1150.2 68.1 reduce-scatter.7
  1222.5 184.3 reduce-scatter.19
  1411.0 184.4 reduce-scatter.17
  1599.6 184.3 reduce-scatter.15
where the time goes:
time: 1790 us
  waiting for transfers between devices  1380 us (77%)
  matrix products  159 us (9%)
  blocking collectives  131 us (7%)
  other arithmetic  90.3 us (5%)
  between operations  18 us (1%)
    reduce_scatter x1, waiting for transfers between devices, shards(): lax.psum_scatter(grad_up_w, 'dp', scatter_dimension=0, tiled=True)  189 us
    reduce_scatter x1, waiting for transfers between devices, shards(): lax.psum_scatter(grad_down, 'dp', scatter_dimension=1, tiled=True)  189 us
    reduce_scatter x1, waiting for transfers between devices, shards(): lax.psum_scatter(grad_gate_w, 'dp', scatter_dimension=0, tiled=True)  188 us
    psum x1, waiting for transfers between devices, shards(): attn_total = lax.psum(matmul(context_b, weight_o), 'tensor')  108 us
    psum x1, waiting for transfers between devices, shards(): lax.psum(matmul_nt(grad_gate_b, weight_gate) + matmul_nt(grad_up_b, weigh...  105 us
    all_gather x1, waiting for transfers between devices, gather_mlp(): lax.all_gather(w_up.astype(jnp.bfloat16), 'dp', axis=0, tiled=True)  85.3 us
    all_gather x1, waiting for transfers between devices, gather_mlp(): lax.all_gather(w_gate.astype(jnp.bfloat16), 'dp', axis=0, tiled=True)  79.9 us
    all_gather x1, waiting for transfers between devices, gather_mlp(): lax.all_gather(w_down.astype(jnp.bfloat16), 'dp', axis=1, tiled=True)  79.5 us
  transfers between devices with their start and end apart: 16, of which 14 were waited for; matrix products, arithmetic and copies ran while one was open for 9% of the time, Pallas kernels for 0%

commit v1 on v0

v1 whole, which is shorter than its diff:
```python
import functools

import jax
import jax.numpy as jnp
from jax import lax
from jax.experimental import pallas as pl
from jax.experimental.pallas import tpu as pltpu
from jax.sharding import PartitionSpec as P

EPSILON = 1e-05
ROPE_BASE = 1000000.0
MASKED = -1e30


def rotation_tables(positions, head_dim):
    half_dim = head_dim // 2
    frequency = ROPE_BASE ** (-jnp.arange(half_dim, dtype=jnp.float32) * 2.0 / head_dim)
    angles = positions.astype(jnp.float32)[:, None] * frequency[None, :]
    return (jnp.cos(angles)[:, None, :], jnp.sin(angles)[:, None, :])


def rotate(values, cosine, sine):
    half_dim = values.shape[-1] // 2
    first_half = values[..., :half_dim]
    second_half = values[..., half_dim:]
    return jnp.concatenate(
        [first_half * cosine - second_half * sine, second_half * cosine + first_half * sine],
        axis=-1,
    )


def rotate_back(grads, cosine, sine):
    half_dim = grads.shape[-1] // 2
    first_half = grads[..., :half_dim]
    second_half = grads[..., half_dim:]
    return jnp.concatenate(
        [first_half * cosine + second_half * sine, second_half * cosine - first_half * sine],
        axis=-1,
    )


def norm_forward(values, gain):
    inverse = lax.rsqrt(jnp.mean(values * values, axis=-1, keepdims=True) + EPSILON)
    return (values * inverse * gain, inverse)


def norm_backward(values, inverse, gain, grad_out):
    scaled = grad_out * gain
    inner_mean = jnp.mean(scaled * values, axis=-1, keepdims=True)
    return inverse * scaled - values * (inverse * inverse * inverse) * inner_mean


def matmul(left_op, right_op):
    return jnp.dot(left_op, right_op, preferred_element_type=jnp.float32)


def matmul_tn(left_op, right_op):
    return lax.dot_general(
        left_op, right_op, (((0,), (0,)), ((), ())), preferred_element_type=jnp.float32
    )


def matmul_nt(left_op, right_op):
    return lax.dot_general(
        left_op, right_op, (((1,), (1,)), ((), ())), preferred_element_type=jnp.float32
    )


def place(parts, places, rows):
    count = len(parts)
    width = parts[0].shape[1]

    def kernel(*refs):
        ins, out, sems = refs[:count], refs[count], refs[count + 1]
        copies = []
        for index, (ref, spot) in enumerate(zip(ins, places())):
            start = pl.multiple_of(spot * rows, 16)
            copies.append(
                pltpu.make_async_copy(ref, out.at[pl.ds(start, rows), :], sems.at[index])
            )
        for copy in copies:
            copy.start()
        for copy in copies:
            copy.wait()

    size = count * rows * width * 2
    return pl.pallas_call(
        kernel,
        out_shape=jax.ShapeDtypeStruct((count * rows, width), parts[0].dtype),
        in_specs=[pl.BlockSpec(memory_space=pl.ANY)] * count,
        out_specs=pl.BlockSpec(memory_space=pl.ANY),
        scratch_shapes=[pltpu.SemaphoreType.DMA((count,))],
        cost_estimate=pl.CostEstimate(flops=0, bytes_accessed=2 * size, transcendentals=0),
    )(*parts)


class Ring:
    def __init__(self, count):
        self.count = count
        self.depth = count // 2
        self.flip = [(d, d ^ 1) for d in range(count)]

    def hop(self, values, step):
        pairs = [
            (d, ((d // 2 + step) % self.depth) * 2 + d % 2) for d in range(self.count)
        ]
        return lax.ppermute(values, "dp", pairs)

    def swap(self, values):
        return lax.ppermute(values, "dp", self.flip)

    def gather(self, shard):
        column = [shard] + [self.hop(shard, step) for step in range(1, self.depth)]
        beside = [self.swap(piece) for piece in column]

        def places():
            me = lax.axis_index("dp")
            far, near = me // 2, me % 2
            rows = [lax.rem(far + self.depth - step, self.depth) * 2 for step in range(self.depth)]
            return [row + near for row in rows] + [row + 1 - near for row in rows]

        return place(column + beside, places, shard.shape[0])

    def scatter(self, partial):
        me = lax.axis_index("dp")
        far, near = me // 2, me % 2
        rows = partial.shape[0] // self.count
        total = None
        for step in list(range(1, self.depth)) + [0]:
            there = lax.rem(far + step, self.depth) * 2
            out = lax.dynamic_slice_in_dim(partial, (there + 1 - near) * rows, rows, 0)
            came = self.swap(out).astype(jnp.float32)
            keep = lax.dynamic_slice_in_dim(partial, (there + near) * rows, rows, 0)
            both = keep.astype(jnp.float32) + came
            if step:
                arrived = self.hop(both.astype(jnp.bfloat16), step).astype(jnp.float32)
            else:
                arrived = both
            total = arrived if total is None else total + arrived
        return total


def tensor_sum(partial, count):
    if count != 4:
        return lax.psum(partial.astype(jnp.bfloat16), "tensor")
    me = lax.axis_index("tensor")
    core = lax.rem(me, 2)
    half = partial.shape[0] // 2
    mate = [(t, t ^ 1) for t in range(count)]
    across = [(t, t ^ 2) for t in range(count)]
    out = lax.dynamic_slice_in_dim(partial, (1 - core) * half, half, 0).astype(jnp.bfloat16)
    keep = lax.dynamic_slice_in_dim(partial, core * half, half, 0)
    chip = (keep + lax.ppermute(out, "tensor", mate).astype(jnp.float32)).astype(jnp.bfloat16)
    other = lax.ppermute(chip, "tensor", across)
    mine = (chip.astype(jnp.float32) + other.astype(jnp.float32)).astype(jnp.bfloat16)
    theirs = lax.ppermute(mine, "tensor", mate)
    first = jnp.where(core == 0, mine, theirs)
    second = jnp.where(core == 0, theirs, mine)
    return jnp.concatenate([first, second], axis=0)


def block_logits(query_part, key_part, segments, first_row, last_row, scale):
    raw_scores = (
        jnp.einsum("qkgd,skd->kgqs", query_part, key_part, preferred_element_type=jnp.float32)
        * scale
    )
    row_ids = jnp.arange(first_row, last_row)
    col_ids = jnp.arange(last_row)
    allowed = (segments[first_row:last_row][:, None] == segments[:last_row][None, :]) & (
        row_ids[:, None] >= col_ids[None, :]
    )
    return jnp.where(allowed[None, None], raw_scores, MASKED)


def attention_forward(query_b, key_b, value_b, segments, scale):
    seq_len = query_b.shape[0]
    block_rows = min(512, seq_len)
    pieces = []
    logsums = []
    for block_index in range(seq_len // block_rows):
        first_row = block_index * block_rows
        last_row = first_row + block_rows
        logits = block_logits(
            query_b[first_row:last_row], key_b[:last_row], segments, first_row, last_row, scale
        )
        maxima = jnp.max(logits, axis=-1, keepdims=True)
        expo_terms = jnp.exp(logits - maxima)
        totals = jnp.sum(expo_terms, axis=-1, keepdims=True)
        probs_low = (expo_terms / totals).astype(jnp.bfloat16)
        pieces.append(
            jnp.einsum(
                "kgqs,skd->qkgd", probs_low, value_b[:last_row], preferred_element_type=jnp.float32
            )
        )
        logsums.append(maxima + jnp.log(totals))
    return (jnp.concatenate(pieces, axis=0), logsums)


def attention_backward(query_b, key_b, value_b, grad_context, logsums, segments, scale):
    seq_len = query_b.shape[0]
    block_rows = min(512, seq_len)
    grad_query = []
    grad_key = jnp.zeros(key_b.shape, jnp.float32)
    grad_value = jnp.zeros(value_b.shape, jnp.float32)
    for block_index in range(seq_len // block_rows):
        first_row = block_index * block_rows
        last_row = first_row + block_rows
        query_part = query_b[first_row:last_row]
        grad_part = grad_context[first_row:last_row]
        logits = block_logits(query_part, key_b[:last_row], segments, first_row, last_row, scale)
        probs_soft = jnp.exp(logits - logsums[block_index])
        grad_probs = jnp.einsum(
            "qkgd,skd->kgqs", grad_part, value_b[:last_row], preferred_element_type=jnp.float32
        )
        row_inner = jnp.sum(probs_soft * grad_probs, axis=-1, keepdims=True)
        grad_scores = (probs_soft * (grad_probs - row_inner)).astype(jnp.bfloat16)
        grad_query.append(
            jnp.einsum(
                "kgqs,skd->qkgd", grad_scores, key_b[:last_row], preferred_element_type=jnp.float32
            )
            * scale
        )
        grad_key = grad_key.at[:last_row].add(
            jnp.einsum(
                "kgqs,qkgd->skd", grad_scores, query_part, preferred_element_type=jnp.float32
            )
            * scale
        )
        grad_value = grad_value.at[:last_row].add(
            jnp.einsum(
                "kgqs,qkgd->skd",
                probs_soft.astype(jnp.bfloat16),
                grad_part,
                preferred_element_type=jnp.float32,
            )
        )
    return (jnp.concatenate(grad_query, axis=0), grad_key, grad_value)


def shards(
    block_input,
    segments,
    positions,
    norm1_gain,
    q_norm_gain,
    k_norm_gain,
    w_q,
    w_k,
    w_v,
    w_o,
    norm2_gain,
    w_gate,
    w_up,
    w_down,
    cotangent,
    *,
    n_dp,
    n_tensor,
):
    ring = Ring(n_dp)
    bf16 = jnp.bfloat16
    rows = w_q.shape[0]
    q_cols, kv_cols, ff_cols = w_q.shape[1], w_k.shape[1], w_gate.shape[1]
    small_gain = q_norm_gain.shape[0]

    def column(gain):
        return jnp.pad(gain.astype(bf16), (0, rows - gain.shape[0]))[:, None]

    gains = jnp.concatenate(
        [column(norm1_gain), column(norm2_gain), column(q_norm_gain), column(k_norm_gain)], axis=1
    )
    gains = jnp.pad(gains, ((0, 0), (0, 124)))
    pack_attn = jnp.concatenate(
        [w_q.astype(bf16), w_k.astype(bf16), w_v.astype(bf16), w_o.T.astype(bf16), gains], axis=1
    )
    pack_gates = jnp.concatenate([w_gate.astype(bf16), w_up.astype(bf16)], axis=1)
    pack_down = w_down.T.astype(bf16)
    full_attn = ring.gather(pack_attn)
    full_gates = ring.gather(pack_gates)
    full_down = ring.gather(pack_down)

    qkv_cols = q_cols + 2 * kv_cols
    weight_qkv = full_attn[:, :qkv_cols]
    weight_ot = full_attn[:, qkv_cols : qkv_cols + q_cols]
    gain_block = full_attn[:, qkv_cols + q_cols : qkv_cols + q_cols + 4].astype(jnp.float32).T
    gain_one, gain_two = gain_block[0], gain_block[1]
    gain_query = gain_block[2].reshape(n_dp, rows)[:, :small_gain].reshape(-1)
    gain_key = gain_block[3].reshape(n_dp, rows)[:, :small_gain].reshape(-1)

    seq_len = block_input.shape[0]
    head_dim = gain_query.shape[0]
    local_heads = q_cols // head_dim
    local_kv = kv_cols // head_dim
    group_size = local_heads // local_kv
    scale = head_dim ** (-0.5)
    cosine, sine = rotation_tables(positions, head_dim)
    rows_in = block_input.astype(jnp.float32)
    normed, inverse_one = norm_forward(rows_in, gain_one)
    normed_b = normed.astype(bf16)
    qkv = matmul(normed_b, weight_qkv)
    query = qkv[:, :q_cols].reshape(seq_len, local_heads, head_dim)
    keyed = qkv[:, q_cols : q_cols + kv_cols].reshape(seq_len, local_kv, head_dim)
    value_b = qkv[:, q_cols + kv_cols :].astype(bf16).reshape(seq_len, local_kv, head_dim)
    query_normed, query_inverse = norm_forward(query, gain_query)
    key_normed, key_inverse = norm_forward(keyed, gain_key)
    query_b = (
        rotate(query_normed, cosine, sine)
        .astype(bf16)
        .reshape(seq_len, local_kv, group_size, head_dim)
    )
    key_b = rotate(key_normed, cosine, sine).astype(bf16)
    context, logsums = attention_forward(query_b, key_b, value_b, segments, scale)
    context_b = context.reshape(seq_len, local_heads * head_dim).astype(bf16)
    attn_total = tensor_sum(matmul_nt(context_b, weight_ot), n_tensor)
    residual = rows_in + attn_total.astype(jnp.float32)
    normed_two, inverse_two = norm_forward(residual, gain_two)
    normed_two_b = normed_two.astype(bf16)
    weight_gate = full_gates[:, :ff_cols]
    weight_up = full_gates[:, ff_cols:]
    gated = matmul(normed_two_b, weight_gate)
    upward = matmul(normed_two_b, weight_up)
    sigmoid_gate = jax.nn.sigmoid(gated)
    inner_b = (gated * sigmoid_gate * upward).astype(bf16)
    grad_down = ring.scatter(matmul_tn(cotangent, inner_b).astype(bf16)).T
    mlp_total = tensor_sum(matmul_nt(inner_b, full_down), n_tensor)
    output_rows = (residual + mlp_total.astype(jnp.float32)).astype(bf16)
    grad_out = cotangent.astype(jnp.float32)
    grad_inner = matmul(cotangent, full_down)
    grad_up_b = (grad_inner * gated * sigmoid_gate).astype(bf16)
    grad_gate_b = (
        grad_inner * upward * sigmoid_gate * (1.0 + gated * (1.0 - sigmoid_gate))
    ).astype(bf16)
    grad_gate_w = ring.scatter(matmul_tn(normed_two_b, grad_gate_b).astype(bf16))
    grad_up_w = ring.scatter(matmul_tn(normed_two_b, grad_up_b).astype(bf16))
    grad_normed_two = tensor_sum(
        matmul_nt(grad_gate_b, weight_gate) + matmul_nt(grad_up_b, weight_up), n_tensor
    ).astype(jnp.float32)
    grad_gain_two = jnp.sum(grad_normed_two * residual * inverse_two, axis=0)
    grad_residual = grad_out + norm_backward(residual, inverse_two, gain_two, grad_normed_two)
    grad_res_b = grad_residual.astype(bf16)
    grad_out_w = ring.scatter(matmul_tn(grad_res_b, context_b).astype(bf16)).T
    grad_context = (
        matmul(grad_res_b, weight_ot).astype(bf16).reshape(seq_len, local_kv, group_size, head_dim)
    )
    grad_query, grad_key, grad_value = attention_backward(
        query_b, key_b, value_b, grad_context, logsums, segments, scale
    )
    grad_query = rotate_back(grad_query.reshape(seq_len, local_heads, head_dim), cosine, sine)
    grad_key = rotate_back(grad_key, cosine, sine)
    grad_gain_q = jnp.sum(grad_query * query * query_inverse, axis=(0, 1))
    grad_gain_k = jnp.sum(grad_key * keyed * key_inverse, axis=(0, 1))
    grad_q_low = (
        norm_backward(query, query_inverse, gain_query, grad_query)
        .astype(bf16)
        .reshape(seq_len, local_heads * head_dim)
    )
    grad_k_low = (
        norm_backward(keyed, key_inverse, gain_key, grad_key)
        .astype(bf16)
        .reshape(seq_len, local_kv * head_dim)
    )
    grad_v_low = grad_value.astype(bf16).reshape(seq_len, local_kv * head_dim)
    grad_low = jnp.concatenate([grad_q_low, grad_k_low, grad_v_low], axis=1)
    grad_qkv = ring.scatter(matmul_tn(normed_b, grad_low).astype(bf16))
    grad_normed = tensor_sum(matmul_nt(grad_low, weight_qkv), n_tensor).astype(jnp.float32)
    grad_gain_one = jnp.sum(grad_normed * rows_in * inverse_one, axis=0)
    grad_input = grad_residual + norm_backward(rows_in, inverse_one, gain_one, grad_normed)
    share = 1.0 / n_tensor
    small = lax.psum(
        jnp.concatenate([grad_gain_one * share, grad_gain_two * share, grad_gain_q, grad_gain_k]),
        ("dp", "tensor"),
    )
    me = lax.axis_index("dp")
    width = gain_one.shape[0]

    def own(start, size):
        return lax.dynamic_slice_in_dim(small, start + me * size, size, 0)

    return (
        output_rows,
        grad_input,
        own(0, rows),
        own(2 * width, small_gain),
        own(2 * width + head_dim, small_gain),
        grad_qkv[:, :q_cols],
        grad_qkv[:, q_cols : q_cols + kv_cols],
        grad_qkv[:, q_cols + kv_cols :],
        grad_out_w,
        own(width, rows),
        grad_gate_w,
        grad_up_w,
        grad_down,
    )


def solution(mesh):
    placed = (
        P("dp", None),
        P("dp"),
        P("dp"),
        P("dp"),
        P("dp"),
        P("dp"),
        P("dp", "tensor"),
        P("dp", "tensor"),
        P("dp", "tensor"),
        P("tensor", "dp"),
        P("dp"),
        P("dp", "tensor"),
        P("dp", "tensor"),
        P("tensor", "dp"),
        P("dp", None),
    )
    return jax.shard_map(
        functools.partial(shards, n_dp=mesh.shape["dp"], n_tensor=mesh.shape["tensor"]),
        mesh=mesh,
        in_specs=placed,
        out_specs=(
            P("dp", None),
            P("dp", None),
            P("dp"),
            P("dp"),
            P("dp"),
            P("dp", "tensor"),
            P("dp", "tensor"),
            P("dp", "tensor"),
            P("tensor", "dp"),
            P("dp"),
            P("dp", "tensor"),
            P("dp", "tensor"),
            P("tensor", "dp"),
        ),
        check_vma=False,
    )
```

time: 1790 us -> 1480 us (0.83)
  waiting for transfers between devices: 1380 us -> 421 us
  Pallas kernels: 0 us -> 599 us
  starting transfers between devices: 1.24 us -> 101 us
  blocking collectives: 131 us -> 37.9 us
  local copies, waits for them, and re-layouts: 15.2 us -> 44.3 us
  other arithmetic: 90.3 us -> 115 us
    reduce_scatter x7 -> x0, waiting for transfers between devices: 785 us -> none  [the longest x1 189 us: shards(): lax.psum_scatter(grad_up_w, 'dp', scatter_dimension=0, tiled=True)]
    pallas_call x0 -> x3, Pallas kernels: none -> 599 us  [place(): pl.pallas_call(kernel, out_shape=jax.ShapeDtypeStruct((count * rows, widt...]
    ppermute x0 -> x68, waiting for transfers between devices: none -> 421 us  [the longest x24 297 us: hop(): return lax.ppermute(values, 'dp', pairs)]
    psum x4 -> x0, waiting for transfers between devices: 345 us -> none  [the longest x1 108 us: shards(): attn_total = lax.psum(matmul(context_b, weight_o), 'tensor')]
    all_gather x5 -> x0, waiting for transfers between devices: 245 us -> none  [the longest x1 85.3 us: gather_mlp(): lax.all_gather(w_up.astype(jnp.bfloat16), 'dp', axis=0, tiled=True)]
    ppermute x0 -> x68, starting transfers between devices: none -> 101 us  [the longest x24 62 us: hop(): return lax.ppermute(values, 'dp', pairs)]
    all_gather x2 -> x0, blocking collectives: 63 us -> none  [the longest x1 32 us: gather_attention(): lax.all_gather(w_k.astype(jnp.bfloat16), 'dp', axis=0, tiled=True)]
    unnamed x2 -> x0, blocking collectives: 61.7 us -> none
  transfers between devices with their start and end apart: 16 -> 68, of which waited for: 14 -> 26; matrix products, arithmetic and copies ran while one was open for 9% -> 11% of each run, Pallas kernels for 0% -> 33%
where the time goes in v1:
time: 1480 us; the launch traced here: 1470 us
  Pallas kernels  599 us (40%)
  waiting for transfers between devices  421 us (28%)
  matrix products  148 us (10%)
  other arithmetic  115 us (8%)
  starting transfers between devices  101 us (7%)
  local copies, waits for them, and re-layouts  44.3 us (3%)
  blocking collectives  37.9 us (3%)
    pallas_call x3, Pallas kernels, place(): pl.pallas_call(kernel, out_shape=jax.ShapeDtypeStruct((count * rows, widt...  599 us
    ppermute x24, waiting for transfers between devices, hop(): return lax.ppermute(values, 'dp', pairs)  297 us
    ppermute x32, waiting for transfers between devices, swap(): return lax.ppermute(values, 'dp', self.flip)  124 us
    ppermute x24, starting transfers between devices, hop(): return lax.ppermute(values, 'dp', pairs)  62 us
    dot_general x5, matrix products, matmul(): return jnp.dot(left_op, right_op, preferred_element_type=jnp.float32)  47.6 us
    dot_general x5, matrix products, matmul_nt(): lax.dot_general(left_op, right_op, (((1,), (1,)), ((), ())), preferred_el...  39.6 us
    psum x1, blocking collectives, shards(): lax.psum(jnp.concatenate([grad_gain_one * share, grad_gain_two * share, g...  37.9 us
    ppermute x32, starting transfers between devices, swap(): return lax.ppermute(values, 'dp', self.flip)  33 us
  transfers between devices with their start and end apart: 68, of which 26 were waited for; matrix products, arithmetic and copies ran while one was open for 11% of the time, Pallas kernels for 33%

profile of v1, /device:TPU:0, one launch (start us, length us, event | category | flops | bytes accessed | tf_op | source)
XLA Modules:
  0.0 1468.9 jit_solution(8102670321899764902)
XLA Ops:
  25.2 26.3 %collective-permute-done.1.refs_2_ = bf16[192,1152]{1,0:T(8,128)(2,1)S(1)} collective-permute-done((bf16[192,1152]{1,0:T(8,128)(2,1)S(1)}, bf16[192,1152]{1,0:T(8,128)(2,1)S(1)}, u32[]{:S(2)}, u32[]{:S(2)}) %collective-permute-start.1) | collective-permute-done | bytes 442400 | tf_op jit(solution)/shard_map/ppermute | solution.py:107
  55.4 9.2 collective-permute-done.5.refs_6_
  71.9 108.4 %shard_map.256 = bf16[1536,1152]{1,0:T(8,128)(2,1)} custom-call(bf16[192,1152]{1,0:T(8,128)(2,1)} %copy-done.42, bf16[192,1152]{1,0:T(8,128)(2,1)} %copy-done.56, bf16[192,1152]{1,0:T(8,128)(2,1)} %copy-done.55, bf16[192,1152]{1,0:T(8,128)(2,1)} %copy-done.54, bf16[192,1152]{1,0:T(8,128)(2,1)} %copy-done.53, ...), custom_call_target="tpu_custom_call" | custom-call | bytes 7077888 | tf_op jit(solution)/shard_map/pallas_call | solution.py:87
  237.0 12.4 collective-permute-done.19.refs_3_
  249.9 40.3 %collective-permute-done.18.refs_2_ = bf16[192,1728]{1,0:T(8,128)(2,1)} collective-permute-done((bf16[192,1728]{1,0:T(8,128)(2,1)}, bf16[192,1728]{1,0:T(8,128)(2,1)}, u32[]{:S(2)}, u32[]{:S(2)}) %collective-permute-start.18) | collective-permute-done | bytes 663584 | tf_op jit(solution)/shard_map/ppermute | solution.py:107
  299.8 8.0 collective-permute-done.22.refs_6_
  310.8 13.7 collective-permute-done.21.refs_5_
  331.1 80.3 %collective-permute-done.11.refs_2_ = bf16[192,3456]{1,0:T(8,128)(2,1)} collective-permute-done((bf16[192,3456]{1,0:T(8,128)(2,1)}, bf16[192,3456]{1,0:T(8,128)(2,1)}, u32[]{:S(2)}, u32[]{:S(2)}) %collective-permute-start.11) | collective-permute-done | bytes 1327136 | tf_op jit(solution)/shard_map/ppermute | solution.py:107
  413.4 167.9 %shard_map.258 = bf16[1536,1728]{1,0:T(8,128)(2,1)} custom-call(bf16[192,1728]{1,0:T(8,128)(2,1)} %convert_bitcast_fusion.1.refs_0_, bf16[192,1728]{1,0:T(8,128)(2,1)} %collective-permute-done.17.refs_1_, bf16[192,1728]{1,0:T(8,128)(2,1)} %collective-permute-done.18.refs_2_, bf16[192,1728]{1,0:T(8,128)(2,1)} %collective-permute-done.19.refs_3_, ...), custom_call_target="tpu_custom_call" | custom-call | bytes 10616832 | tf_op jit(solution)/shard_map/pallas_call | solution.py:87
  584.9 10.7 fusion.125
  595.6 322.8 %shard_map.257 = bf16[1536,3456]{1,0:T(8,128)(2,1)} custom-call(bf16[192,3456]{1,0:T(8,128)(2,1)} %pad_maximum_fusion.5.refs_0_, bf16[192,3456]{1,0:T(8,128)(2,1)} %collective-permute-done.10.refs_1_, bf16[192,3456]{1,0:T(8,128)(2,1)} %collective-permute-done.11.refs_2_, bf16[192,3456]{1,0:T(8,128)(2,1)} %collective-permute-done.12.refs_3_, ...), custom_call_target="tpu_custom_call" | custom-call | bytes 21233664 | tf_op jit(solution)/shard_map/pallas_call | solution.py:87
  935.8 21.4 %fusion.10 = (bf16[1024,1728]{0,1:T(8,128)(2,1)}, bf16[1024,1728]{0,1:T(8,128)(2,1)}, bf16[1024,1728]{0,1:T(8,128)(2,1)}) fusion(f32[1728,1024]{1,0:T(8,128)} %fusion.125, f32[1024,1728]{0,1:T(8,128)} %fusion.41, bf16[1024,1536]{1,0:T(8,128)(2,1)} %copy-done.27, bf16[1536,3456]{1,0:T(8,128)(2,1)} %shard_map.257), kind=kOutput, calls=%fused_computation.30 | convolution fusion | flops 5464129536 | bytes 33423360 | tf_op jit(solution)/shard_map/dot_general | solution.py:54
  957.3 9.2 fusion.124
  966.6 12.4 fusion.35
  979.0 9.5 fusion.44
  991.3 8.2 convolution_convert_fusion
  1003.8 8.4 convolution_convert_fusion.2
  1017.1 8.6 convolution_convert_fusion.1
  1035.7 9.7 collective-permute-done.61
  1046.9 13.2 collective-permute-done.65
  1063.5 11.3 collective-permute-done.63
  1076.5 13.1 collective-permute-done.54
  1091.1 13.2 collective-permute-done.58
  1105.9 13.2 collective-permute-done.56
  1130.9 9.7 fusion.16
  1203.5 29.7 %collective-permute-start.57 = (bf16[192,1728]{1,0:T(8,128)(2,1)S(1)}, bf16[192,1728]{1,0:T(8,128)(2,1)S(1)}, u32[]{:S(2)}, u32[]{:S(2)}) collective-permute-start(bf16[192,1728]{1,0:T(8,128)(2,1)S(1)} %copy-done.45), channel_id=1, source_target_pairs={{0,16},{4,20},{8,24},{12,28},{16,0},{20,4},{24,8},{28,12},{1,17},{... | collective-permute-start | bytes 1990664 | tf_op jit(solution)/shard_map/ppermute | solution.py:107
  1233.2 30.1 %collective-permute-done.64 = bf16[192,1728]{1,0:T(8,128)(2,1)S(1)} collective-permute-done((bf16[192,1728]{1,0:T(8,128)(2,1)S(1)}, bf16[192,1728]{1,0:T(8,128)(2,1)S(1)}, u32[]{:S(2)}, u32[]{:S(2)}) %collective-permute-start.64) | collective-permute-done | bytes 663584 | tf_op jit(solution)/shard_map/ppermute | solution.py:107
  1276.6 45.7 %collective-permute-done.57 = bf16[192,1728]{1,0:T(8,128)(2,1)S(1)} collective-permute-done((bf16[192,1728]{1,0:T(8,128)(2,1)S(1)}, bf16[192,1728]{1,0:T(8,128)(2,1)S(1)}, u32[]{:S(2)}, u32[]{:S(2)}) %collective-permute-start.57) | collective-permute-done | bytes 663584 | tf_op jit(solution)/shard_map/ppermute | solution.py:107
  1327.1 23.0 %collective-permute-done.50 = bf16[192,1728]{1,0:T(8,128)(2,1)S(1)} collective-permute-done((bf16[192,1728]{1,0:T(8,128)(2,1)S(1)}, bf16[192,1728]{1,0:T(8,128)(2,1)S(1)}, u32[]{:S(2)}, u32[]{:S(2)}) %collective-permute-start.50) | collective-permute-done | bytes 663584 | tf_op jit(solution)/shard_map/ppermute | solution.py:107
  1390.8 9.4 collective-permute-done.43
  1403.9 11.3 collective-permute-done.36
  1422.7 37.9 %psum.7 = f32[3200]{0:T(1024)S(1)} all-reduce(f32[3200]{0:T(1024)S(1)} %concatenate.76), channel_id=1, replica_groups=mesh['dp'=8,'tensor'=4] {'dp','tensor'}, use_global_device_ids=true, to_apply=%region_20.21 | all-reduce | flops 3200 | bytes 25600 | tf_op jit(solution)/shard_map/psum | solution.py:369
  (454 shorter events, 318.1 us)
Async XLA Ops:
  229.0 61.6 %collective-permute-start.7 = (bf16[512,1536]{1,0:T(8,128)(2,1)}, bf16[512,1536]{1,0:T(8,128)(2,1)}, u32[]{:S(2)}, u32[]{:S(2)}) collective-permute-start(bf16[512,1536]{1,0:T(8,128)(2,1)} %dynamic-slice_convert_fusion.3), channel_id=1, source_target_pairs={{0,1},{1,0},{2,3},{3,2},{4,5},{5,4},{6,7},{7,6},{8,9},{9,8},{10,11... | collective-permute-start | bytes 4718600 | tf_op jit(solution)/shard_map/ppermute | solution.py:153
  230.0 60.2 %collective-permute-start.18 = (bf16[192,1728]{1,0:T(8,128)(2,1)}, bf16[192,1728]{1,0:T(8,128)(2,1)}, u32[]{:S(2)}, u32[]{:S(2)}) collective-permute-start(bf16[192,1728]{1,0:T(8,128)(2,1)} %convert_bitcast_fusion.1.refs_0_), channel_id=1, source_target_pairs={{0,16},{4,20},{8,24},{12,28},{16,0},{20,4},{24,8},{28,12},{1,17},{... | collective-permute-start | bytes 1990664 | tf_op jit(solution)/shard_map/ppermute | solution.py:107
  230.0 67.5 %collective-permute-start.20 = (bf16[192,1728]{1,0:T(8,128)(2,1)}, bf16[192,1728]{1,0:T(8,128)(2,1)}, u32[]{:S(2)}, u32[]{:S(2)}) collective-permute-start(bf16[192,1728]{1,0:T(8,128)(2,1)} %convert_bitcast_fusion.1.refs_0_), channel_id=1, source_target_pairs={{0,4},{4,0},{8,12},{12,8},{16,20},{20,16},{24,28},{28,24},{1,5},{5... | collective-permute-start | bytes 1990664 | tf_op jit(solution)/shard_map/ppermute | solution.py:110
  230.5 67.0 %collective-permute-start.17 = (bf16[192,1728]{1,0:T(8,128)(2,1)}, bf16[192,1728]{1,0:T(8,128)(2,1)}, u32[]{:S(2)}, u32[]{:S(2)}) collective-permute-start(bf16[192,1728]{1,0:T(8,128)(2,1)} %convert_bitcast_fusion.1.refs_0_), channel_id=1, source_target_pairs={{0,8},{4,12},{8,16},{12,20},{16,24},{20,28},{24,0},{28,4},{1,9},{5... | collective-permute-start | bytes 1990664 | tf_op jit(solution)/shard_map/ppermute | solution.py:107
  294.6 286.7 %collective-permute-start.8 = (bf16[512,1536]{1,0:T(8,128)(2,1)}, bf16[512,1536]{1,0:T(8,128)(2,1)}, u32[]{:S(2)}, u32[]{:S(2)}) collective-permute-start(bf16[512,1536]{1,0:T(8,128)(2,1)} %add_convert_fusion.8), channel_id=1, source_target_pairs={{0,2},{1,3},{2,0},{3,1},{4,6},{5,7},{6,4},{7,5},{8,10},{9,11},{10,... | collective-permute-start | bytes 4718600 | tf_op jit(solution)/shard_map/ppermute | solution.py:154
  297.5 113.8 %collective-permute-start.11 = (bf16[192,3456]{1,0:T(8,128)(2,1)}, bf16[192,3456]{1,0:T(8,128)(2,1)}, u32[]{:S(2)}, u32[]{:S(2)}) collective-permute-start(bf16[192,3456]{1,0:T(8,128)(2,1)} %pad_maximum_fusion.5.refs_0_), channel_id=1, source_target_pairs={{0,16},{4,20},{8,24},{12,28},{16,0},{20,4},{24,8},{28,12},{1,17},{... | collective-permute-start | bytes 3981320 | tf_op jit(solution)/shard_map/ppermute | solution.py:107
  297.6 115.3 %collective-permute-start.10 = (bf16[192,3456]{1,0:T(8,128)(2,1)}, bf16[192,3456]{1,0:T(8,128)(2,1)}, u32[]{:S(2)}, u32[]{:S(2)}) collective-permute-start(bf16[192,3456]{1,0:T(8,128)(2,1)} %pad_maximum_fusion.5.refs_0_), channel_id=1, source_target_pairs={{0,8},{4,12},{8,16},{12,20},{16,24},{20,28},{24,0},{28,4},{1,9},{5... | collective-permute-start | bytes 3981320 | tf_op jit(solution)/shard_map/ppermute | solution.py:107
  324.5 271.1 %collective-permute-start.13 = (bf16[192,3456]{1,0:T(8,128)(2,1)}, bf16[192,3456]{1,0:T(8,128)(2,1)}, u32[]{:S(2)}, u32[]{:S(2)}) collective-permute-start(bf16[192,3456]{1,0:T(8,128)(2,1)} %pad_maximum_fusion.5.refs_0_), channel_id=1, source_target_pairs={{0,4},{4,0},{8,12},{12,8},{16,20},{20,16},{24,28},{28,24},{1,5},{5... | collective-permute-start | bytes 3981320 | tf_op jit(solution)/shard_map/ppermute | solution.py:110
  329.5 266.1 %collective-permute-start.16 = (bf16[192,3456]{1,0:T(8,128)(2,1)}, bf16[192,3456]{1,0:T(8,128)(2,1)}, u32[]{:S(2)}, u32[]{:S(2)}) collective-permute-start(bf16[192,3456]{1,0:T(8,128)(2,1)} %collective-permute-done.12.refs_3_), channel_id=1, source_target_pairs={{0,4},{4,0},{8,12},{12,8},{16,20},{20,16},{24,28},{28,24},{1,5},{5... | collective-permute-start | bytes 3981320 | tf_op jit(solution)/shard_map/ppermute | solution.py:110
  411.3 184.3 %collective-permute-start.15 = (bf16[192,3456]{1,0:T(8,128)(2,1)}, bf16[192,3456]{1,0:T(8,128)(2,1)}, u32[]{:S(2)}, u32[]{:S(2)}) collective-permute-start(bf16[192,3456]{1,0:T(8,128)(2,1)} %collective-permute-done.11.refs_2_), channel_id=1, source_target_pairs={{0,4},{4,0},{8,12},{12,8},{16,20},{20,16},{24,28},{28,24},{1,5},{5... | collective-permute-start | bytes 3981320 | tf_op jit(solution)/shard_map/ppermute | solution.py:110
  412.9 182.8 %collective-permute-start.14 = (bf16[192,3456]{1,0:T(8,128)(2,1)}, bf16[192,3456]{1,0:T(8,128)(2,1)}, u32[]{:S(2)}, u32[]{:S(2)}) collective-permute-start(bf16[192,3456]{1,0:T(8,128)(2,1)} %collective-permute-done.10.refs_1_), channel_id=1, source_target_pairs={{0,4},{4,0},{8,12},{12,8},{16,20},{20,16},{24,28},{28,24},{1,5},{5... | collective-permute-start | bytes 3981320 | tf_op jit(solution)/shard_map/ppermute | solution.py:110
  584.9 333.5 %collective-permute-start.9 = (bf16[512,1536]{1,0:T(8,128)(2,1)}, bf16[512,1536]{1,0:T(8,128)(2,1)}, u32[]{:S(2)}, u32[]{:S(2)}) collective-permute-start(bf16[512,1536]{1,0:T(8,128)(2,1)} %add_convert_fusion.7), channel_id=1, source_target_pairs={{0,1},{1,0},{2,3},{3,2},{4,5},{5,4},{6,7},{7,6},{8,9},{9,8},{10,11... | collective-permute-start | bytes 4718600 | tf_op jit(solution)/shard_map/ppermute | solution.py:156
  1033.3 56.3 %collective-permute-start.54 = (bf16[192,1728]{1,0:T(8,128)(2,1)S(1)}, bf16[192,1728]{1,0:T(8,128)(2,1)S(1)}, u32[]{:S(2)}, u32[]{:S(2)}) collective-permute-start(bf16[192,1728]{1,0:T(8,128)(2,1)S(1)} %get-tuple-element.152), channel_id=1, source_target_pairs={{0,4},{4,0},{8,12},{12,8},{16,20},{20,16},{24,28},{28,24},{1,5},{5... | collective-permute-start | bytes 1990664 | tf_op jit(solution)/shard_map/ppermute | solution.py:110
  1045.4 59.0 %collective-permute-start.58 = (bf16[192,1728]{1,0:T(8,128)(2,1)S(1)}, bf16[192,1728]{1,0:T(8,128)(2,1)S(1)}, u32[]{:S(2)}, u32[]{:S(2)}) collective-permute-start(bf16[192,1728]{1,0:T(8,128)(2,1)S(1)} %get-tuple-element.154), channel_id=1, source_target_pairs={{0,4},{4,0},{8,12},{12,8},{16,20},{20,16},{24,28},{28,24},{1,5},{5... | collective-permute-start | bytes 1990664 | tf_op jit(solution)/shard_map/ppermute | solution.py:110
  1060.1 59.0 %collective-permute-start.56 = (bf16[192,1728]{1,0:T(8,128)(2,1)S(1)}, bf16[192,1728]{1,0:T(8,128)(2,1)S(1)}, u32[]{:S(2)}, u32[]{:S(2)}) collective-permute-start(bf16[192,1728]{1,0:T(8,128)(2,1)S(1)} %get-tuple-element.155), channel_id=1, source_target_pairs={{0,4},{4,0},{8,12},{12,8},{16,20},{20,16},{24,28},{28,24},{1,5},{5... | collective-permute-start | bytes 1990664 | tf_op jit(solution)/shard_map/ppermute | solution.py:110
  1061.6 60.7 %collective-permute-start.25 = (bf16[512,1536]{1,0:T(8,128)(2,1)S(1)}, bf16[512,1536]{1,0:T(8,128)(2,1)S(1)}, u32[]{:S(2)}, u32[]{:S(2)}) collective-permute-start(bf16[512,1536]{1,0:T(8,128)(2,1)S(1)} %add_convert_fusion.6), channel_id=1, source_target_pairs={{0,2},{1,3},{2,0},{3,1},{4,6},{5,7},{6,4},{7,5},{8,10},{9,11},{10,... | collective-permute-start | bytes 4718600 | tf_op jit(solution)/shard_map/ppermute | solution.py:154
  1074.9 48.4 %collective-permute-start.29 = (bf16[512,1536]{1,0:T(8,128)(2,1)S(1)}, bf16[512,1536]{1,0:T(8,128)(2,1)S(1)}, u32[]{:S(2)}, u32[]{:S(2)}) collective-permute-start(bf16[512,1536]{1,0:T(8,128)(2,1)S(1)} %add_convert_fusion.3), channel_id=1, source_target_pairs={{0,1},{1,0},{2,3},{3,2},{4,5},{5,4},{6,7},{7,6},{8,9},{9,8},{10,11... | collective-permute-start | bytes 4718600 | tf_op jit(solution)/shard_map/ppermute | solution.py:156
  1089.6 94.3 %collective-permute-start.67 = (bf16[192,1728]{1,0:T(8,128)(2,1)}, bf16[192,1728]{1,0:T(8,128)(2,1)}, u32[]{:S(2)}, u32[]{:S(2)}) collective-permute-start(bf16[192,1728]{1,0:T(8,128)(2,1)} %get-tuple-element.146), channel_id=1, source_target_pairs={{0,4},{4,0},{8,12},{12,8},{16,20},{20,16},{24,28},{28,24},{1,5},{5... | collective-permute-start | bytes 1990664 | tf_op jit(solution)/shard_map/ppermute | solution.py:110
  1104.4 82.5 %collective-permute-start.47 = (bf16[192,1728]{1,0:T(8,128)(2,1)}, bf16[192,1728]{1,0:T(8,128)(2,1)}, u32[]{:S(2)}, u32[]{:S(2)}) collective-permute-start(bf16[192,1728]{1,0:T(8,128)(2,1)} %get-tuple-element.159), channel_id=1, source_target_pairs={{0,4},{4,0},{8,12},{12,8},{16,20},{20,16},{24,28},{28,24},{1,5},{5... | collective-permute-start | bytes 1990664 | tf_op jit(solution)/shard_map/ppermute | solution.py:110
  1119.1 71.8 %collective-permute-start.51 = (bf16[192,1728]{1,0:T(8,128)(2,1)}, bf16[192,1728]{1,0:T(8,128)(2,1)}, u32[]{:S(2)}, u32[]{:S(2)}) collective-permute-start(bf16[192,1728]{1,0:T(8,128)(2,1)} %get-tuple-element.161), channel_id=1, source_target_pairs={{0,4},{4,0},{8,12},{12,8},{16,20},{20,16},{24,28},{28,24},{1,5},{5... | collective-permute-start | bytes 1990664 | tf_op jit(solution)/shard_map/ppermute | solution.py:110
  1122.3 69.9 %collective-permute-start.49 = (bf16[192,1728]{1,0:T(8,128)(2,1)}, bf16[192,1728]{1,0:T(8,128)(2,1)}, u32[]{:S(2)}, u32[]{:S(2)}) collective-permute-start(bf16[192,1728]{1,0:T(8,128)(2,1)} %get-tuple-element.162), channel_id=1, source_target_pairs={{0,4},{4,0},{8,12},{12,8},{16,20},{20,16},{24,28},{28,24},{1,5},{5... | collective-permute-start | bytes 1990664 | tf_op jit(solution)/shard_map/ppermute | solution.py:110
  1129.6 63.2 %collective-permute-start.62 = (bf16[192,1728]{1,0:T(8,128)(2,1)}, bf16[192,1728]{1,0:T(8,128)(2,1)}, u32[]{:S(2)}, u32[]{:S(2)}) collective-permute-start(bf16[192,1728]{1,0:T(8,128)(2,1)} %get-tuple-element.142), channel_id=1, source_target_pairs={{0,8},{4,12},{8,16},{12,20},{16,24},{20,28},{24,0},{28,4},{1,9},{5... | collective-permute-start | bytes 1990664 | tf_op jit(solution)/shard_map/ppermute | solution.py:107
  1186.8 76.5 %collective-permute-start.64 = (bf16[192,1728]{1,0:T(8,128)(2,1)S(1)}, bf16[192,1728]{1,0:T(8,128)(2,1)S(1)}, u32[]{:S(2)}, u32[]{:S(2)}) collective-permute-start(bf16[192,1728]{1,0:T(8,128)(2,1)S(1)} %copy-done.47), channel_id=1, source_target_pairs={{0,16},{4,20},{8,24},{12,28},{16,0},{20,4},{24,8},{28,12},{1,17},{... | collective-permute-start | bytes 1990664 | tf_op jit(solution)/shard_map/ppermute | solution.py:107
  1191.7 76.7 %collective-permute-start.60 = (bf16[192,1728]{1,0:T(8,128)(2,1)S(1)}, bf16[192,1728]{1,0:T(8,128)(2,1)S(1)}, u32[]{:S(2)}, u32[]{:S(2)}) collective-permute-start(bf16[192,1728]{1,0:T(8,128)(2,1)S(1)} %copy-done.44), channel_id=1, source_target_pairs={{0,4},{4,0},{8,12},{12,8},{16,20},{20,16},{24,28},{28,24},{1,5},{5... | collective-permute-start | bytes 1990664 | tf_op jit(solution)/shard_map/ppermute | solution.py:110
  1192.3 76.7 %collective-permute-start.55 = (bf16[192,1728]{1,0:T(8,128)(2,1)S(1)}, bf16[192,1728]{1,0:T(8,128)(2,1)S(1)}, u32[]{:S(2)}, u32[]{:S(2)}) collective-permute-start(bf16[192,1728]{1,0:T(8,128)(2,1)S(1)} %copy-done.48), channel_id=1, source_target_pairs={{0,8},{4,12},{8,16},{12,20},{16,24},{20,28},{24,0},{28,4},{1,9},{5... | collective-permute-start | bytes 1990664 | tf_op jit(solution)/shard_map/ppermute | solution.py:107
  1192.8 83.6 %collective-permute-start.59 = (bf16[192,1728]{1,0:T(8,128)(2,1)S(1)}, bf16[192,1728]{1,0:T(8,128)(2,1)S(1)}, u32[]{:S(2)}, u32[]{:S(2)}) collective-permute-start(bf16[192,1728]{1,0:T(8,128)(2,1)S(1)} %copy-done.46), channel_id=1, source_target_pairs={{0,24},{4,28},{8,0},{12,4},{16,8},{20,12},{24,16},{28,20},{1,25},{... | collective-permute-start | bytes 1990664 | tf_op jit(solution)/shard_map/ppermute | solution.py:107
  1203.5 118.9 %collective-permute-start.57 = (bf16[192,1728]{1,0:T(8,128)(2,1)S(1)}, bf16[192,1728]{1,0:T(8,128)(2,1)S(1)}, u32[]{:S(2)}, u32[]{:S(2)}) collective-permute-start(bf16[192,1728]{1,0:T(8,128)(2,1)S(1)} %copy-done.45), channel_id=1, source_target_pairs={{0,16},{4,20},{8,24},{12,28},{16,0},{20,4},{24,8},{28,12},{1,17},{... | collective-permute-start | bytes 1990664 | tf_op jit(solution)/shard_map/ppermute | solution.py:107
  1263.3 61.8 %collective-permute-start.30 = (bf16[512,1536]{1,0:T(8,128)(2,1)S(1)}, bf16[512,1536]{1,0:T(8,128)(2,1)S(1)}, u32[]{:S(2)}, u32[]{:S(2)}) collective-permute-start(bf16[512,1536]{1,0:T(8,128)(2,1)S(1)} %dynamic-slice_convert_fusion), channel_id=1, source_target_pairs={{0,1},{1,0},{2,3},{3,2},{4,5},{5,4},{6,7},{7,6},{8,9},{9,8},{10,11... | collective-permute-start | bytes 4718600 | tf_op jit(solution)/shard_map/ppermute | solution.py:153
  1268.5 58.6 %collective-permute-start.53 = (bf16[192,1728]{1,0:T(8,128)(2,1)S(1)}, bf16[192,1728]{1,0:T(8,128)(2,1)S(1)}, u32[]{:S(2)}, u32[]{:S(2)}) collective-permute-start(bf16[192,1728]{1,0:T(8,128)(2,1)S(1)} %copy-done.43), channel_id=1, source_target_pairs={{0,4},{4,0},{8,12},{12,8},{16,20},{20,16},{24,28},{28,24},{1,5},{5... | collective-permute-start | bytes 1990664 | tf_op jit(solution)/shard_map/ppermute | solution.py:110
  1269.0 58.1 %collective-permute-start.48 = (bf16[192,1728]{1,0:T(8,128)(2,1)S(1)}, bf16[192,1728]{1,0:T(8,128)(2,1)S(1)}, u32[]{:S(2)}, u32[]{:S(2)}) collective-permute-start(bf16[192,1728]{1,0:T(8,128)(2,1)S(1)} %get-tuple-element.156), channel_id=1, source_target_pairs={{0,8},{4,12},{8,16},{12,20},{16,24},{20,28},{24,0},{28,4},{1,9},{5... | collective-permute-start | bytes 1990664 | tf_op jit(solution)/shard_map/ppermute | solution.py:107
  1276.4 50.7 %collective-permute-start.52 = (bf16[192,1728]{1,0:T(8,128)(2,1)S(1)}, bf16[192,1728]{1,0:T(8,128)(2,1)S(1)}, u32[]{:S(2)}, u32[]{:S(2)}) collective-permute-start(bf16[192,1728]{1,0:T(8,128)(2,1)S(1)} %get-tuple-element.157), channel_id=1, source_target_pairs={{0,24},{4,28},{8,0},{12,4},{16,8},{20,12},{24,16},{28,20},{1,25},{... | collective-permute-start | bytes 1990664 | tf_op jit(solution)/shard_map/ppermute | solution.py:107
  1362.8 54.1 %collective-permute-start.32 = (bf16[512,1536]{1,0:T(8,128)(2,1)}, bf16[512,1536]{1,0:T(8,128)(2,1)}, u32[]{:S(2)}, u32[]{:S(2)}) collective-permute-start(bf16[512,1536]{1,0:T(8,128)(2,1)} %add_convert_fusion.1), channel_id=1, source_target_pairs={{0,1},{1,0},{2,3},{3,2},{4,5},{5,4},{6,7},{7,6},{8,9},{9,8},{10,11... | collective-permute-start | bytes 4718600 | tf_op jit(solution)/shard_map/ppermute | solution.py:156
  (132 other events, 2684.6 us)

commit v2 on v0

v2 whole, which is shorter than its diff:
```python
import functools

import jax
import jax.numpy as jnp
from jax import lax
from jax.experimental import pallas as pl
from jax.experimental.pallas import tpu as pltpu
from jax.sharding import PartitionSpec as P

EPSILON = 1e-05
ROPE_BASE = 1000000.0
MASKED = -1e30


MESH = pl.DeviceIdType.MESH
NEAR = 2
HALF = 64
LANES = 128
HIGHEST = lax.Precision.HIGHEST
BF16 = jnp.bfloat16
F32 = jnp.float32


def whole_block():
    return pl.BlockSpec(memory_space=pltpu.VMEM)


def in_place():
    return pl.BlockSpec(memory_space=pl.ANY)


def remote(src, dst, send, recv, dp, tensor):
    return pltpu.make_async_remote_copy(
        src_ref=src,
        dst_ref=dst,
        send_sem=send,
        recv_sem=recv,
        device_id=(dp, tensor),
        device_id_type=MESH,
    )


def dot_nn(left, right):
    return jnp.dot(left, right, preferred_element_type=F32)


def dot_nt(left, right):
    return lax.dot_general(left, right, (((1,), (1,)), ((), ())), preferred_element_type=F32)


def dot_tn(left, right):
    return lax.dot_general(left, right, (((0,), (0,)), ((), ())), preferred_element_type=F32)


class Place:
    def __init__(self, count):
        self.count = count
        self.depth = count // NEAR
        self.me = lax.axis_index("dp")
        self.tensor = lax.axis_index("tensor")
        self.far = self.me // NEAR
        self.near = lax.rem(self.me, NEAR)
        self.core = lax.rem(self.tensor, 2)
        self.mate = self.tensor + 1 - 2 * self.core
        self.across = lax.rem(self.tensor + 2, 4)
        self.beside = self.me + 1 - 2 * self.near

    def ahead(self, step):
        return lax.rem(self.far + step, self.depth)

    def behind(self, step):
        return lax.rem(self.far + self.depth - step, self.depth)

    def greet(self, everyone, tensor):
        barrier = pltpu.get_barrier_semaphore()
        peers = []
        if everyone:
            peers += [(lax.rem(self.me + d, self.count), self.tensor) for d in range(1, self.count)]
        else:
            peers += [
                (self.ahead(step) * NEAR + self.near, self.tensor) for step in range(1, self.depth)
            ]
            peers.append((self.beside, self.tensor))
        if tensor:
            peers += [(self.me, self.mate), (self.me, self.across)]
        for peer in peers:
            pl.semaphore_signal(barrier, 1, device_id=peer, device_id_type=MESH)
        pl.semaphore_wait(barrier, len(peers))


class Gather:
    def __init__(self, place, shard, full, sems):
        self.place, self.shard, self.full = place, shard, full
        self.rows = shard.shape[0]
        late = self.late_rows(self.rows)
        self.cuts = [(0, self.rows - late)] + ([(self.rows - late, late)] if late else [])
        self.zsend, self.zrecv, self.ysend, self.yrecv, self.own = sems
        self.sent = []

    @staticmethod
    def late_rows(rows):
        return rows // 6 // 16 * 16

    @staticmethod
    def sems(count):
        depth = count // NEAR
        dma = pltpu.SemaphoreType.DMA
        return [dma((2, depth - 1, 3)), dma((2, depth - 1, 3)), dma((2 * depth - 1, 2)), dma((2 * depth - 1, 2)), dma]

    def spot(self, block, cut):
        start, size = self.cuts[cut]
        return self.full.at[pl.ds(pl.multiple_of(block * self.rows + start, 16), size), :]

    def mine(self, cut):
        start, size = self.cuts[cut]
        return self.shard.at[pl.ds(start, size), :]

    def block(self, way, step, other):
        far = self.place.far - step if way == 0 else self.place.far + step
        return far * NEAR + (1 - self.place.near if other else self.place.near)

    def valid(self, way, step):
        return self.place.far >= step if way == 0 else self.place.far + step < self.place.depth

    def emit(self, copy, when):
        if when is None:
            copy.start()
        else:
            pl.when(when)(copy.start)
        self.sent.append((copy, when))

    def along(self, way, step, cut, other, valid=None):
        place = self.place
        if step >= place.depth - 1:
            return
        more = place.far < place.depth - 1 if way == 0 else place.far > 0
        spot = self.spot(self.block(way, step, other), cut)
        goal = place.me + (NEAR if way == 0 else -NEAR)
        self.emit(
            remote(
                self.mine(cut) if step == 0 and not other else spot, spot,
                self.zsend.at[way, step, cut + other], self.zrecv.at[way, step, cut + other], goal, place.tensor,
            ),
            more if valid is None else more & valid,
        )

    def over(self, way, step, cut, valid=None):
        place = self.place
        spot = self.spot(self.block(way, step, 0), cut)
        slot = step if way == 0 else step + place.depth - 1
        self.emit(
            remote(
                self.mine(cut) if step == 0 else spot, spot,
                self.ysend.at[slot, cut], self.yrecv.at[slot, cut], place.beside, place.tensor,
            ),
            valid,
        )

    def came_over(self, way, step, cut):
        place = self.place
        spot = self.spot(self.block(way, step, 1), cut)
        slot = step if way == 0 else step + place.depth - 1
        copy = remote(
            spot, spot, self.ysend.at[slot, cut], self.yrecv.at[slot, cut], place.beside, place.tensor
        )
        if step == 0:
            copy.wait_recv()
        else:
            pl.when(self.valid(way, step))(copy.wait_recv)

    def start(self):
        place = self.place
        self.local = pltpu.make_async_copy(
            self.shard, self.full.at[pl.ds(pl.multiple_of(place.me * self.rows, 16), self.rows), :], self.own
        )
        self.local.start()
        for cut in reversed(range(len(self.cuts))):
            self.over(0, 0, cut)
        for cut in range(len(self.cuts)):
            for way in range(2):
                self.along(way, 0, cut, 0)

    def steps(self):
        place = self.place
        if len(self.cuts) > 1:
            self.came_over(0, 0, 1)
            for way in range(2):
                self.along(way, 0, 1, 1)
            yield
        for step in range(1, place.depth):
            for cut in range(len(self.cuts)):
                for other in range(cut + 1):
                    for way in range(2):
                        valid = self.valid(way, step)
                        spot = self.spot(self.block(way, step, other), cut)
                        copy = remote(
                            spot, spot, self.zsend.at[way, step - 1, cut + other],
                            self.zrecv.at[way, step - 1, cut + other], place.me, place.tensor,
                        )
                        pl.when(valid)(copy.wait_recv)
                        self.along(way, step, cut, other, valid)
                        if cut == 0:
                            self.over(way, step, cut, valid)
                        yield

    def finish(self):
        self.came_over(0, 0, 0)
        for step in range(1, self.place.depth):
            for way in range(2):
                self.came_over(way, step, 0)
        self.local.wait()

    def settle(self):
        for copy, when in self.sent:
            if when is None:
                copy.wait_send()
            else:
                pl.when(when)(copy.wait_send)


class TensorSum:
    def __init__(self, place, part, total, tiles, scratch):
        self.place, self.part, self.total, self.tiles = place, part, total, tiles
        self.tile = part.shape[0] // tiles
        self.half = self.tile // 2
        self.near, self.chip, self.far, self.sems = scratch
        self.sent = []

    @staticmethod
    def scratch(rows, width, tiles, kind):
        half = (rows // 2, width)
        return [
            pltpu.VMEM(half, kind), pltpu.VMEM(half, BF16), pltpu.VMEM(half, BF16), pltpu.SemaphoreType.DMA((6, tiles))
        ]

    def half_rows(self, index, which):
        return pl.ds(pl.multiple_of(index * self.tile + which * self.half, 16), self.half)

    def slot(self, index):
        return pl.ds(index * self.half, self.half)

    def send_core(self, index):
        place = self.place
        copy = remote(
            self.part.at[self.half_rows(index, 1 - place.core), :], self.near.at[self.slot(index), :],
            self.sems.at[0, index], self.sems.at[1, index], place.me, place.mate,
        )
        copy.start()
        self.sent.append(copy)

    def send_across(self, index):
        place = self.place
        spot = self.near.at[self.slot(index), :]
        remote(spot, spot, self.sems.at[0, index], self.sems.at[1, index], place.me, place.mate).wait_recv()
        mine = self.part[self.half_rows(index, place.core), :].astype(F32)
        self.chip[self.slot(index), :] = (mine + self.near[self.slot(index), :].astype(F32)).astype(BF16)
        copy = remote(
            self.chip.at[self.slot(index), :], self.far.at[self.slot(index), :],
            self.sems.at[2, index], self.sems.at[3, index], place.me, place.across,
        )
        copy.start()
        self.sent.append(copy)

    def send_back(self, index):
        place = self.place
        spot = self.far.at[self.slot(index), :]
        remote(spot, spot, self.sems.at[2, index], self.sems.at[3, index], place.me, place.across).wait_recv()
        both = self.chip[self.slot(index), :].astype(F32) + self.far[self.slot(index), :].astype(F32)
        rows = self.half_rows(index, place.core)
        self.total[rows, :] = both.astype(self.total.dtype)
        copy = remote(
            self.total.at[rows, :], self.total.at[rows, :],
            self.sems.at[4, index], self.sems.at[5, index], place.me, place.mate,
        )
        copy.start()
        self.sent.append(copy)

    def finish(self, index):
        place = self.place
        spot = self.total.at[self.half_rows(index, 1 - place.core), :]
        remote(spot, spot, self.sems.at[4, index], self.sems.at[5, index], place.me, place.mate).wait_recv()

    def settle(self):
        for copy in self.sent:
            copy.wait_send()


def lane_ids(width=LANES):
    return lax.broadcasted_iota(jnp.int32, (1, width), 1)


def head_mean(values):
    row = lax.broadcasted_iota(jnp.int32, (LANES, LANES), 0)
    col = lax.broadcasted_iota(jnp.int32, (LANES, LANES), 1)
    groups = jnp.where(row // HALF == col // HALF, 1.0 / HALF, 0.0).astype(F32)
    return jnp.dot(values, groups, precision=HIGHEST, preferred_element_type=F32)


def turn(values, cosine, sine):
    ahead = pltpu.roll(values, LANES - HALF // 2, 1)
    back = pltpu.roll(values, HALF // 2, 1)
    first = lax.rem(lane_ids(), HALF) < HALF // 2
    return values * cosine + jnp.where(first, ahead, back) * sine


def bias_block(seg_col, seg_row, bias, first, tile):
    last = first + tile
    rows = lax.broadcasted_iota(jnp.int32, (tile, last), 0) + first
    cols = lax.broadcasted_iota(jnp.int32, (tile, last), 1)
    allowed = (seg_col[pl.ds(first, tile), :] == seg_row[:, pl.ds(0, last)]) & (rows >= cols)
    bias[:, pl.ds(0, last)] = jnp.where(allowed, 0.0, MASKED)


def forward_kernel(count, *refs):
    (
        x_ref, seg_col, seg_row, cos_ref, sin_ref, gain_ref, pack_attn, pack_gates,
        full_attn, full_gates, n1_ref, qk_ref, qm_ref, kb_ref, vb_ref, lse_ref, ctx_ref, h_ref, n2_ref,
        gains_out,
        w0, bias, gain_slots, part, total, tmp_near, tmp_chip, tmp_far, sum_sems, gain_send, gain_recv, out_sem,
        *gather_sems,
    ) = refs
    place = Place(count)
    seq, width = x_ref.shape
    q_cols = ctx_ref.shape[1]
    kv_cols = kb_ref.shape[1]
    pairs = q_cols // LANES
    group = (q_cols // HALF) // (kv_cols // HALF)
    tile = seq // 4
    place.greet(True, True)
    first = Gather(place, pack_attn, w0, gather_sems[:5])
    second = Gather(place, pack_gates, full_gates, gather_sems[5:])
    gain_copies = []
    for step in range(1, count):
        copy = remote(
            gain_ref, gain_slots.at[step], gain_send.at[step], gain_recv.at[step],
            lax.rem(place.me + step, count), place.tensor,
        )
        copy.start()
        gain_copies.append(copy)
    first.start()
    for qb in range(4):
        bias_block(seg_col, seg_row, bias.at[qb], qb * tile, tile)
    gains = gain_ref[...]
    for copy in gain_copies:
        copy.wait_recv()
    for step in range(1, count):
        gains = gains + gain_slots[step]
    gains_out[...] = gains
    for _ in first.steps():
        pass
    second.start()
    moves = second.steps()
    g1 = gains_out[pl.ds(0, 1), :]
    g2 = gains_out[pl.ds(1, 1), :]

    def norm_one(index, carry):
        rows = pl.ds(pl.multiple_of(index * LANES, LANES), LANES)
        x = x_ref[rows, :].astype(F32)
        inverse = lax.rsqrt(jnp.mean(x * x, axis=1, keepdims=True) + EPSILON)
        n1_ref[rows, :] = (x * inverse * g1).astype(BF16)
        return carry

    lax.fori_loop(0, seq // LANES, norm_one, 0)
    first.finish()
    save = pltpu.make_async_copy(w0, full_attn, out_sem)
    save.start()
    gq = gains_out[pl.ds(2, 1), pl.ds(0, LANES)]
    gk = gains_out[pl.ds(3, 1), pl.ds(0, LANES)]
    lanes = lane_ids()

    def project(index, carry):
        rows = pl.ds(pl.multiple_of(index * tile, tile), tile)
        qkv = dot_nn(n1_ref[rows, :], w0[:, pl.ds(0, q_cols + 2 * kv_cols)])
        qk_ref[rows, :] = qkv[:, : q_cols + kv_cols]
        vb_ref[rows, :] = qkv[:, q_cols + kv_cols :].astype(BF16)
        cosine, sine = cos_ref[rows, :], sin_ref[rows, :]
        for pair in range(pairs + 1):
            raw = qkv[:, pair * LANES : (pair + 1) * LANES]
            inverse = lax.rsqrt(head_mean(raw * raw) + EPSILON)
            turned = turn(raw * inverse * (gk if pair == pairs else gq), cosine, sine)
            if pair == pairs:
                kb_ref[rows, :] = turned.astype(BF16)
                continue
            swapped = pltpu.roll(turned, HALF, 1)
            for side in range(2):
                head = 2 * pair + side
                kv = head // group
                keep = (turned if side == kv else swapped).astype(BF16) * 0.125
                qm_ref[head, rows, :] = jnp.where(lanes // HALF == kv, keep, jnp.zeros_like(keep))
        return carry

    lax.fori_loop(0, 4, project, 0)
    next(moves, None)

    for qb in range(4):
        last = (qb + 1) * tile
        rows = pl.ds(qb * tile, tile)

        def attend(pair, carry, last=last, rows=rows, qb=qb):
            halves, sums = [], []
            for side in range(2):
                head = 2 * pair + side
                kv = head // group
                logits = dot_nt(qm_ref[head, rows, :], kb_ref[pl.ds(0, last), :]) + bias[qb, :, pl.ds(0, last)]
                top = jnp.max(logits, axis=1, keepdims=True)
                expo = jnp.exp(logits - top)
                total = jnp.sum(expo, axis=1, keepdims=True)
                probs = (expo * (1.0 / total)).astype(BF16)
                got = dot_nn(probs, vb_ref[pl.ds(0, last), :])
                halves.append(jnp.where(kv == side, got, pltpu.roll(got, HALF, 1)))
                sums.append(top + jnp.log(total))
            ctx_ref[rows, pl.ds(pl.multiple_of(pair * LANES, LANES), LANES)] = jnp.where(
                lanes < HALF, halves[0], halves[1]
            ).astype(BF16)
            carry = jnp.where(lanes == 2 * pair, sums[0], carry)
            return jnp.where(lanes == 2 * pair + 1, sums[1], carry)

        lse_ref[rows, :] = lax.fori_loop(0, pairs, attend, jnp.zeros((tile, LANES), F32))
        next(moves, None)
        next(moves, None)

    summed = TensorSum(place, part, total, 4, (tmp_near, tmp_chip, tmp_far, sum_sems))
    for index in range(4):
        rows = pl.ds(index * tile, tile)
        part[rows, :] = dot_nt(
            ctx_ref[rows, :], w0[:, pl.ds(q_cols + 2 * kv_cols, q_cols)]
        )
        summed.send_core(index)
    for index in range(4):
        summed.send_across(index)
    next(moves, None)
    for index in range(4):
        summed.send_back(index)
        next(moves, None)
    for index in range(4):
        summed.finish(index)

        def norm_two(sub, carry, index=index):
            rows = pl.ds(pl.multiple_of(index * tile + sub * LANES, LANES), LANES)
            h = x_ref[rows, :].astype(F32) + total[rows, :]
            h_ref[rows, :] = h
            inverse = lax.rsqrt(jnp.mean(h * h, axis=1, keepdims=True) + EPSILON)
            n2_ref[rows, :] = (h * inverse * g2).astype(BF16)
            return carry

        lax.fori_loop(0, tile // LANES, norm_two, 0)
        next(moves, None)
    for _ in moves:
        pass
    second.finish()
    save.wait()
    for copy in gain_copies:
        copy.wait_send()
    first.settle()
    second.settle()
    summed.settle()


def forward_call(count, x, seg_col, seg_row, cosine, sine, gains, pack_attn, pack_gates):
    seq, width = x.shape
    rows = pack_attn.shape[0]
    shape = jax.ShapeDtypeStruct
    q_cols, kv_cols = 384, LANES
    outs = [
        shape((count * rows, pack_attn.shape[1]), BF16),
        shape((count * rows, pack_gates.shape[1]), BF16),
        shape((seq, width), BF16),
        shape((seq, q_cols + kv_cols), F32),
        shape((q_cols // HALF, seq, LANES), BF16),
        shape((seq, LANES), BF16),
        shape((seq, LANES), BF16),
        shape((seq, LANES), F32),
        shape((seq, q_cols), BF16),
        shape((seq, width), F32),
        shape((seq, width), BF16),
        shape(gains.shape, F32),
    ]
    dma = pltpu.SemaphoreType.DMA
    return pl.pallas_call(
        functools.partial(forward_kernel, count),
        out_shape=outs,
        in_specs=[whole_block()] * 6 + [in_place()] * 2,
        out_specs=[in_place()] * 2 + [whole_block()] * 10,
        scratch_shapes=[
            pltpu.VMEM((count * rows, pack_attn.shape[1]), BF16),
            pltpu.VMEM((4, seq // 4, seq), F32),
            pltpu.VMEM((count,) + gains.shape, F32),
            pltpu.VMEM((seq, width), F32),
            pltpu.VMEM((seq, width), F32),
            *TensorSum.scratch(seq, width, 4, F32),
            dma((count,)),
            dma((count,)),
            dma,
            *Gather.sems(count),
            *Gather.sems(count),
        ],
        compiler_params=pltpu.CompilerParams(
            collective_id=1, has_side_effects=True, vmem_limit_bytes=60 << 20
        ),
    )(x, seg_col, seg_row, cosine, sine, gains, pack_attn, pack_gates)


class Scatter:
    def __init__(self, place, partial, result, scratch):
        self.place, self.partial, self.result = place, partial, result
        self.rows = partial.shape[0] // place.count
        self.late = Gather.late_rows(self.rows)
        self.early = self.rows - self.late
        self.over_in, self.far_in, self.far_late, self.late_in = scratch[:4]
        self.zsend, self.zrecv, self.ysend, self.yrecv, self.lsend, self.lrecv = scratch[4:]
        self.sent = []

    @staticmethod
    def scratch(count, rows, width):
        depth = count // NEAR
        late = Gather.late_rows(rows)
        early = rows - late
        dma = pltpu.SemaphoreType.DMA
        return [
            pltpu.VMEM((depth, early, width), BF16),
            pltpu.VMEM((depth + 1, early, width), BF16),
            pltpu.VMEM((2, depth + 1, max(late, 16), width), BF16),
            pltpu.VMEM((max(late, 16), width), BF16),
            dma((2, depth - 1, 3)),
            dma((2, depth - 1, 3)),
            dma((2 * depth - 1,)),
            dma((2 * depth - 1,)),
            dma,
            dma,
        ]

    def spot(self, far, other, late):
        near = 1 - self.place.near if other else self.place.near
        start = (far * NEAR + near) * self.rows + (self.early if late else 0)
        return pl.ds(pl.multiple_of(start, 16), self.late if late else self.early)

    def valid(self, way, step):
        return self.place.far + step < self.place.depth if way == 0 else self.place.far >= step

    def fed(self, way):
        return self.place.far > 0 if way == 0 else self.place.far < self.place.depth - 1

    def goal(self, way, step):
        return self.place.far + step if way == 0 else self.place.far - step

    def slot(self, way, step):
        return step if way == 0 else step + self.place.depth - 1

    def emit(self, copy, when=None):
        if when is None:
            copy.start()
        else:
            pl.when(when)(copy.start)
        self.sent.append((copy, when))

    def over(self, far, slot):
        place = self.place
        return remote(
            self.partial.at[self.spot(far, True, False), :], self.over_in.at[far],
            self.ysend.at[slot], self.yrecv.at[slot], place.beside, place.tensor,
        )

    def start(self):
        place = self.place
        for step in reversed(range(1, place.depth)):
            for way in range(2):
                self.emit(self.over(self.goal(way, step), self.slot(way, step)), self.valid(way, step))
        self.emit(self.over(place.far, 0))

    def add(self, spot, sources):
        size = sources[0].shape[0]
        part = 32 if size % 32 == 0 else 16

        def body(index, carry):
            start = pl.multiple_of(index * part, 16)
            rows = pl.ds(pl.multiple_of(spot.start + start, 16), part)
            total = self.partial[rows, :].astype(F32)
            for source in sources:
                total = total + source[pl.ds(start, part), :].astype(F32)
            self.partial[rows, :] = total.astype(BF16)
            return carry

        lax.fori_loop(0, size // part, body, 0)

    def incoming(self, way, step, item):
        place = self.place
        index = place.depth if way == 1 and step == 0 else self.goal(way, step)
        return self.far_in.at[index] if item == 0 else self.far_late.at[item - 1, index]

    def wait_far(self, way, step, item):
        place = self.place
        into = self.incoming(way, step, item)
        remote(
            into, into, self.zsend.at[way, step, item], self.zrecv.at[way, step, item], place.me, place.tensor
        ).wait_recv()
        return into

    def pass_on(self, way, step, item):
        place = self.place
        far = self.goal(way, step)
        spot = self.spot(far, item == 2, item > 0)
        if item == 0:
            copy = self.over(far, self.slot(way, step))
            pl.when(self.valid(way, step))(copy.wait_recv)
        base = [self.over_in.at[far]] if item == 0 else []
        valid = self.valid(way, step)
        if step < place.depth - 1:

            @pl.when(valid & self.fed(way))
            def _():
                self.add(spot, base + [self.wait_far(way, step, item)])

        if base:

            @pl.when(valid & jnp.logical_not(self.fed(way)))
            def _():
                self.add(spot, base)

        index = place.depth if way == 1 and step == 1 else far
        into = self.far_in.at[index] if item == 0 else self.far_late.at[item - 1, index]
        self.emit(
            remote(
                self.partial.at[spot, :], into,
                self.zsend.at[way, step - 1, item], self.zrecv.at[way, step - 1, item],
                place.me + (NEAR if way == 0 else -NEAR), place.tensor,
            ),
            valid,
        )

    def steps(self):
        place = self.place
        for step in reversed(range(1, place.depth)):
            for item in ((1, 2) if self.late else ()):
                for way in range(2):
                    self.pass_on(way, step, item)
                yield
            for way in range(2):
                self.pass_on(way, step, 0)
                yield
        far = place.far
        if self.late:
            for item in (2, 1):
                spot = self.spot(far, item == 2, True)
                for way in range(2):

                    @pl.when(self.fed(way))
                    def _(way=way, item=item, spot=spot):
                        self.add(spot, [self.wait_far(way, 0, item)])

                if item == 2:
                    copy = remote(
                        self.partial.at[spot, :], self.late_in, self.lsend, self.lrecv, place.beside, place.tensor
                    )
                    self.emit(copy)
            yield
        self.over(far, 0).wait_recv()
        spot = self.spot(far, False, False)
        self.add(spot, [self.over_in.at[far]])
        yield
        for way in range(2):

            @pl.when(self.fed(way))
            def _(way=way, spot=spot):
                self.add(spot, [self.wait_far(way, 0, 0)])

        own = self.spot(far, False, False)
        self.result[pl.ds(0, self.early), :] = self.partial[own, :].astype(F32)
        yield
        if self.late:
            copy.wait_recv()
            own = self.spot(far, False, True)
            self.result[pl.ds(self.early, self.late), :] = (
                self.partial[own, :].astype(F32) + self.late_in[...].astype(F32)
            )
        yield

    def settle(self):
        for copy, when in self.sent:
            if when is None:
                copy.wait_send()
            else:
                pl.when(when)(copy.wait_send)


def drain(*moves):
    for one in moves:
        for _ in one:
            pass


def ahead(moves, count=1):
    for _ in range(count):
        next(moves, None)


def blocks(total, size, body):
    def step(index, carry):
        body(pl.multiple_of(index * size, size))
        return carry

    lax.fori_loop(0, total // size, step, 0)


def mlp_kernel(count, *refs):
    (
        n2_ref, cot_ref, gates_hbm, pack_down,
        first_out, second_out, dn2_ref, part_ref, down_ref,
        w1, w2, ab, hid, partial, load_sem, save_sems, *rest,
    ) = refs
    place = Place(count)
    seq, width = n2_ref.shape
    both = w1.shape[1]
    even = both // (2 * LANES)
    split = first_out.shape[1]
    lanes = lane_ids()
    place.greet(False, False)
    gather = Gather(place, pack_down, w2, rest[:5])
    scatter = Scatter(place, partial, down_ref, rest[5:])
    load = pltpu.make_async_copy(gates_hbm, w1, load_sem)
    load.start()
    gather.start()
    moves = gather.steps()
    load.wait()

    def gate_up(index, carry):
        cols = pl.ds(pl.multiple_of(index * 2 * LANES, 2 * LANES), 2 * LANES)
        got = dot_nn(n2_ref[...], w1[:, cols])
        gate, up = got[:, :LANES], got[:, LANES:]
        sig = jax.nn.sigmoid(gate)
        act = gate * sig
        hid[:, pl.ds(pl.multiple_of(index * LANES, LANES), LANES)] = (act * up).astype(BF16)
        slope = up * sig * (1.0 + gate * (1.0 - sig))
        ab[:, cols] = jnp.concatenate([slope, act], axis=1).astype(BF16)
        return carry

    third = even // 3
    for piece in range(3):
        lax.fori_loop(piece * third, even if piece == 2 else (piece + 1) * third, gate_up, 0)
        ahead(moves, 2)
    tail = pl.ds(2 * even * LANES, LANES)
    got = dot_nn(n2_ref[...], w1[:, tail])
    up = pltpu.roll(got, HALF, 1)
    sig = jax.nn.sigmoid(got)
    act = got * sig
    hid[:, pl.ds(even * LANES, LANES)] = jnp.where(lanes < HALF, act * up, 0.0).astype(BF16)
    slope = up * sig * (1.0 + got * (1.0 - sig))
    ab[:, tail] = jnp.where(lanes < HALF, slope, pltpu.roll(act, HALF, 1)).astype(BF16)
    ahead(moves, 2)

    def down_grad(start):
        partial[pl.ds(start, 384), :] = dot_tn(cot_ref[:, pl.ds(start, 384)], hid[...]).astype(BF16)

    blocks(width, 384, down_grad)
    scatter.start()
    sums = scatter.steps()
    drain(moves)
    ahead(sums, 4)
    gather.finish()

    def inner_grad(index, carry):
        got = dot_nn(cot_ref[...], w2[:, pl.ds(pl.multiple_of(index * 2 * LANES, 2 * LANES), 2 * LANES)])
        for side in range(2):
            piece = got[:, side * LANES : (side + 1) * LANES]
            cols = pl.ds(pl.multiple_of(index * 4 * LANES + side * 2 * LANES, 2 * LANES), 2 * LANES)
            ab[:, cols] = (ab[:, cols].astype(F32) * jnp.concatenate([piece, piece], axis=1)).astype(BF16)
        return carry

    lax.fori_loop(0, even // 2, inner_grad, 0)
    got = dot_nn(cot_ref[...], w2[:, pl.ds((even - 1) * LANES, 2 * LANES)])
    piece = got[:, :LANES]
    cols = pl.ds(2 * (even - 1) * LANES, 2 * LANES)
    ab[:, cols] = (ab[:, cols].astype(F32) * jnp.concatenate([piece, piece], axis=1)).astype(BF16)
    piece = got[:, LANES:]
    piece = jnp.where(lanes < HALF, piece, pltpu.roll(piece, HALF, 1))
    ab[:, tail] = (ab[:, tail].astype(F32) * piece).astype(BF16)
    ahead(sums, 2)

    def normed_grad(start):
        dn2_ref[:, pl.ds(start, 256)] = dot_nt(ab[...], w1[pl.ds(start, 256), :]).astype(dn2_ref.dtype)

    blocks(width, 256, normed_grad)
    ahead(sums, 2)

    def output_part(start):
        part_ref[:, pl.ds(start, 256)] = dot_nt(hid[...], w2[pl.ds(start, 256), :]).astype(BF16)

    blocks(width, 256, output_part)
    ahead(sums, 2)

    def gates_grad(start):
        rows = pl.ds(start, 384)
        for low, high in ((0, split), (split, both)):
            w1[rows, pl.ds(low, high - low)] = dot_tn(
                n2_ref[:, pl.ds(start, 384)], ab[:, pl.ds(low, high - low)]
            ).astype(BF16)

    blocks(width, 384, gates_grad)
    saves = [
        pltpu.make_async_copy(w1.at[:, pl.ds(0, split)], first_out, save_sems.at[0]),
        pltpu.make_async_copy(w1.at[:, pl.ds(split, both - split)], second_out, save_sems.at[1]),
    ]
    for save in saves:
        save.start()
    drain(sums)
    for save in saves:
        save.wait()
    gather.settle()
    scatter.settle()


def mlp_call(count, n2, cot, full_gates, pack_down):
    seq, width = n2.shape
    rows, down = pack_down.shape
    both = full_gates.shape[1]
    split = 14 * LANES
    shape = jax.ShapeDtypeStruct
    dma = pltpu.SemaphoreType.DMA
    return pl.pallas_call(
        functools.partial(mlp_kernel, count),
        out_shape=[
            shape((width, split), BF16),
            shape((width, both - split), BF16),
            shape((seq, width), BF16),
            shape((seq, width), BF16),
            shape((rows, down), F32),
        ],
        in_specs=[whole_block()] * 2 + [in_place()] * 2,
        out_specs=[in_place()] * 2 + [whole_block()] * 3,
        scratch_shapes=[
            pltpu.VMEM((width, both), BF16),
            pltpu.VMEM((width, down), BF16),
            pltpu.VMEM((seq, both), BF16),
            pltpu.VMEM((seq, down), BF16),
            pltpu.VMEM((width, down), BF16),
            dma,
            dma((2,)),
            *Gather.sems(count),
            *Scatter.scratch(count, rows, down),
        ],
        compiler_params=pltpu.CompilerParams(
            collective_id=2, has_side_effects=True, vmem_limit_bytes=61 << 20
        ),
    )(n2, cot, full_gates, pack_down)


def middle_kernel(count, *refs):
    (
        part_in, dn2_ref, h_ref, cot_ref, w0_ref, ctx_ref, gain_ref,
        gates_ref, dh_ref, dm_ref, dwo_ref, small_ref,
        partial, dhb, near, chip, far, sum_sems, load_sem, *rest,
    ) = refs
    place = Place(count)
    seq, width = dn2_ref.shape
    q_cols = ctx_ref.shape[1]
    heads = q_cols // HALF
    group = heads // 2
    tile = seq // 4
    lanes = lane_ids()
    load = pltpu.make_async_copy(part_in, partial, load_sem)
    load.start()
    place.greet(False, True)
    scatter = Scatter(place, partial, gates_ref, rest)
    summed = TensorSum(place, dn2_ref, dh_ref, 4, (near, chip, far, sum_sems))
    for index in range(4):
        summed.send_core(index)
    load.wait()
    scatter.start()
    sums = scatter.steps()
    for index in range(4):
        summed.send_across(index)
    ahead(sums, 2)
    for index in range(4):
        summed.send_back(index)
        ahead(sums, 1)
    g2 = gain_ref[pl.ds(1, 1), :]
    summed.settle()
    gain_sum = jnp.zeros((8, width), F32)
    for index in range(4):
        summed.finish(index)

        def residual_grad(sub, carry, index=index):
            rows = pl.ds(pl.multiple_of(index * tile + sub * 64, 64), 64)
            grad = dh_ref[rows, :]
            h = h_ref[rows, :]
            inverse = lax.rsqrt(jnp.mean(h * h, axis=1, keepdims=True) + EPSILON)
            scaled = grad * g2
            inner = jnp.mean(scaled * h, axis=1, keepdims=True)
            dh = cot_ref[rows, :].astype(F32) + inverse * scaled - h * (inverse * inverse * inverse * inner)
            dh_ref[rows, :] = dh
            dhb[rows, :] = dh.astype(BF16)
            return carry + jnp.sum((grad * h * inverse).reshape(8, 8, width), axis=0)

        gain_sum = lax.fori_loop(0, tile // 64, residual_grad, gain_sum)
        rows = pl.ds(index * tile, tile)
        dctx = dot_nn(dhb[rows, :], w0_ref[:, pl.ds(w0_ref.shape[1] - q_cols, q_cols)])
        for pair in range(heads // 2):
            value = dctx[:, pair * LANES : (pair + 1) * LANES]
            swapped = pltpu.roll(value, HALF, 1)
            for side in range(2):
                head = 2 * pair + side
                keep = value if side == head // group else swapped
                dm_ref[head, rows, :] = jnp.where(lanes // HALF == head // group, keep, 0.0).astype(BF16)
        ahead(sums, 1)
    small_ref[...] = gain_sum

    def out_grad(start):
        dwo_ref[pl.ds(start, 384), :] = dot_tn(dhb[:, pl.ds(start, 384)], ctx_ref[...]).astype(BF16)

    blocks(width, 384, out_grad)
    drain(sums)
    scatter.settle()


def middle_call(count, part, dn2, h, cot, w0, ctx, gains):
    seq, width = dn2.shape
    q_cols = ctx.shape[1]
    rows = width // count
    shape = jax.ShapeDtypeStruct
    dma = pltpu.SemaphoreType.DMA
    return pl.pallas_call(
        functools.partial(middle_kernel, count),
        out_shape=[
            shape((rows, part.shape[1]), F32),
            shape((seq, width), F32),
            shape((q_cols // HALF, seq, LANES), BF16),
            shape((width, q_cols), BF16),
            shape((8, width), F32),
        ],
        in_specs=[in_place()] + [whole_block()] * 6,
        out_specs=[whole_block()] * 5,
        scratch_shapes=[
            pltpu.VMEM(part.shape, BF16),
            pltpu.VMEM((seq, width), BF16),
            *TensorSum.scratch(seq, width, 4, BF16),
            dma,
            *Scatter.scratch(count, rows, part.shape[1]),
        ],
        compiler_params=pltpu.CompilerParams(
            collective_id=3, has_side_effects=True, vmem_limit_bytes=61 << 20
        ),
    )(part, dn2, h, cot, w0, ctx, gains)


def last_kernel(count, *refs):
    (
        part_in, dwo_in, mlp_ref, dm_ref, qm_ref, kb_ref, vb_ref, lse_ref, qk_ref, cos_ref, sin_ref,
        seg_col, seg_row, n1_ref, w0_ref, gain_ref,
        gates_ref, out_ref, qkv_ref, dn1_ref, mlp_total, small_ref,
        partial, partial_o, partial_qkv, bias, dk, dv, dlow, part1,
        near1, chip1, far1, sems1, near2, chip2, far2, sems2, load_sems, *rest,
    ) = refs
    place = Place(count)
    seq, width = n1_ref.shape
    kv_cols = kb_ref.shape[1]
    q_cols = qk_ref.shape[1] - kv_cols
    pairs = q_cols // LANES
    group = (q_cols // HALF) // (kv_cols // HALF)
    tile = seq // 4
    lanes = lane_ids()
    loads = [
        pltpu.make_async_copy(part_in, partial, load_sems.at[0]),
        pltpu.make_async_copy(dwo_in, partial_o, load_sems.at[1]),
    ]
    for load in loads:
        load.start()
    place.greet(False, True)
    third = len(rest) // 3
    scatter = Scatter(place, partial, gates_ref, rest[:third])
    scatter_o = Scatter(place, partial_o, out_ref, rest[third : 2 * third])
    scatter_qkv = Scatter(place, partial_qkv, qkv_ref, rest[2 * third :])
    summed = TensorSum(place, mlp_ref, mlp_total, 4, (near1, chip1, far1, sems1))
    for index in range(4):
        summed.send_core(index)
    for load in loads:
        load.wait()
    scatter.start()
    scatter_o.start()
    sums, sums_o = scatter.steps(), scatter_o.steps()
    for index in range(4):
        summed.send_across(index)
    dk[...] = jnp.zeros_like(dk)
    dv[...] = jnp.zeros_like(dv)
    gq = gain_ref[pl.ds(2, 1), pl.ds(0, LANES)]
    gk = gain_ref[pl.ds(3, 1), pl.ds(0, LANES)]

    def head_back(grad, raw, cosine, sine, gain):
        back = turn(grad, cosine, -sine)
        inverse = lax.rsqrt(head_mean(raw * raw) + EPSILON)
        scaled = back * gain
        inner = head_mean(scaled * raw)
        low = inverse * scaled - raw * (inverse * inverse * inverse * inner)
        return low.astype(BF16), jnp.sum((back * raw * inverse).reshape(-1, 8, LANES), axis=0)

    gain_q = jnp.zeros((8, LANES), F32)
    for qb in range(4):
        last = (qb + 1) * tile
        rows = pl.ds(qb * tile, tile)
        bias_block(seg_col, seg_row, bias, qb * tile, tile)

        def attend_back(pair, carry, last=last, rows=rows):
            keys = pl.ds(0, last)
            sides = []
            for side in range(2):
                head = 2 * pair + side
                kv = head // group
                query, grad = qm_ref[head, rows, :], dm_ref[head, rows, :]
                logsum = jnp.sum(jnp.where(lanes == head, lse_ref[rows, :], 0.0), axis=1, keepdims=True)
                logits = dot_nt(query, kb_ref[keys, :]) + bias[:, keys]
                probs = jnp.exp(logits - logsum)
                dprob = dot_nt(grad, vb_ref[keys, :])
                inner = jnp.sum(probs * dprob, axis=1, keepdims=True)
                ds = (probs * (dprob - inner)).astype(BF16)
                got = dot_nn(ds, kb_ref[keys, :]) * 0.125
                sides.append(jnp.where(kv == side, got, pltpu.roll(got, HALF, 1)))
                dk[keys, :] += dot_tn(ds, query)
                dv[keys, :] += dot_tn(probs.astype(BF16), grad)
            cols = pl.ds(pl.multiple_of(pair * LANES, LANES), LANES)
            low, terms = head_back(
                jnp.where(lanes < HALF, sides[0], sides[1]), qk_ref[rows, cols], cos_ref[rows, :], sin_ref[rows, :], gq
            )
            dlow[rows, cols] = low
            return carry + terms

        gain_q = lax.fori_loop(0, pairs, attend_back, gain_q)
        summed.send_back(qb)
        ahead(sums, 2)
        ahead(sums_o, 1)
    gain_k = jnp.zeros((8, LANES), F32)
    for qb in range(4):
        rows = pl.ds(qb * tile, tile)
        low, terms = head_back(
            dk[rows, :], qk_ref[rows, pl.ds(q_cols, LANES)], cos_ref[rows, :], sin_ref[rows, :], gk
        )
        dlow[rows, pl.ds(q_cols, LANES)] = low
        dlow[rows, pl.ds(q_cols + LANES, LANES)] = dv[rows, :].astype(BF16)
        gain_k = gain_k + terms
    small_ref[pl.ds(0, 8), :] = gain_q
    small_ref[pl.ds(8, 8), :] = gain_k
    final = TensorSum(place, part1, dn1_ref, 4, (near2, chip2, far2, sems2))
    for index in range(4):
        rows = pl.ds(index * tile, tile)
        part1[rows, :] = dot_nt(dlow[rows, :], w0_ref[:, pl.ds(0, dlow.shape[1])]).astype(BF16)
        final.send_core(index)
    ahead(sums, 1)
    for index in range(4):
        final.send_across(index)

    def qkv_grad(start):
        partial_qkv[pl.ds(start, 384), :] = dot_tn(n1_ref[:, pl.ds(start, 384)], dlow[...]).astype(BF16)

    blocks(width, 384, qkv_grad)
    scatter_qkv.start()
    sums_qkv = scatter_qkv.steps()
    drain(sums, sums_o)
    for index in range(4):
        final.send_back(index)
        ahead(sums_qkv, 2)
    for index in range(4):
        summed.finish(index)
        final.finish(index)
        ahead(sums_qkv, 2)
    drain(sums_qkv)
    for one in (scatter, scatter_o, scatter_qkv, summed, final):
        one.settle()


def last_call(count, part, dwo, mlp, dm, qm, kb, vb, lse, qk, cosine, sine, seg_col, seg_row, n1, w0, gains):
    seq, width = n1.shape
    rows = width // count
    q_cols = dwo.shape[1]
    low = qk.shape[1] + LANES
    shape = jax.ShapeDtypeStruct
    dma = pltpu.SemaphoreType.DMA
    return pl.pallas_call(
        functools.partial(last_kernel, count),
        out_shape=[
            shape((rows, part.shape[1]), F32),
            shape((rows, q_cols), F32),
            shape((rows, low), F32),
            shape((seq, width), BF16),
            shape((seq, width), BF16),
            shape((16, LANES), F32),
        ],
        in_specs=[in_place()] * 2 + [whole_block()] * 14,
        out_specs=[whole_block()] * 6,
        scratch_shapes=[
            pltpu.VMEM(part.shape, BF16),
            pltpu.VMEM(dwo.shape, BF16),
            pltpu.VMEM((width, low), BF16),
            pltpu.VMEM((seq // 4, seq), F32),
            pltpu.VMEM((seq, LANES), F32),
            pltpu.VMEM((seq, LANES), F32),
            pltpu.VMEM((seq, low), BF16),
            pltpu.VMEM((seq, width), BF16),
            *TensorSum.scratch(seq, width, 4, BF16),
            *TensorSum.scratch(seq, width, 4, BF16),
            dma((2,)),
            *Scatter.scratch(count, rows, part.shape[1]),
            *Scatter.scratch(count, rows, q_cols),
            *Scatter.scratch(count, rows, low),
        ],
        compiler_params=pltpu.CompilerParams(
            collective_id=4, has_side_effects=True, vmem_limit_bytes=61 << 20
        ),
    )(part, dwo, mlp, dm, qm, kb, vb, lse, qk, cosine, sine, seg_col, seg_row, n1, w0, gains)


def rotation_tables(positions, head_dim):
    half_dim = head_dim // 2
    frequency = ROPE_BASE ** (-jnp.arange(half_dim, dtype=jnp.float32) * 2.0 / head_dim)
    angles = positions.astype(jnp.float32)[:, None] * frequency[None, :]
    return (jnp.cos(angles)[:, None, :], jnp.sin(angles)[:, None, :])


def lay(gate, up):
    rows, cols = gate.shape
    even = cols // LANES * LANES
    pairs = jnp.stack(
        [gate[:, :even].reshape(rows, -1, LANES), up[:, :even].reshape(rows, -1, LANES)], axis=2
    ).reshape(rows, 2 * even)
    return jnp.concatenate([pairs, gate[:, even:], up[:, even:]], axis=1)


def unlay(both):
    rows, cols = both.shape
    even = cols // 2 // LANES * LANES
    pairs = both[:, : 2 * even].reshape(rows, -1, 2, LANES)
    rest = both[:, 2 * even :]
    size = rest.shape[1] // 2
    return (
        jnp.concatenate([pairs[:, :, 0].reshape(rows, even), rest[:, :size]], axis=1),
        jnp.concatenate([pairs[:, :, 1].reshape(rows, even), rest[:, size:]], axis=1),
    )


def spread(gain, me, width):
    full = jnp.zeros((width,), F32)
    return lax.dynamic_update_slice(full, gain.astype(BF16).astype(F32), (me * gain.shape[0],))


def gain_rows(norm1_gain, norm2_gain, q_gain, k_gain, count):
    me = lax.axis_index("dp")
    width = norm1_gain.shape[0] * count
    head = q_gain.shape[0] * count
    rows = [spread(norm1_gain, me, width), spread(norm2_gain, me, width)]
    for gain in (q_gain, k_gain):
        one = spread(gain, me, head)
        rows.append(jnp.pad(jnp.concatenate([one, one]), (0, width - 2 * head)))
    return jnp.pad(jnp.stack(rows), ((0, 4), (0, 0)))


def rotation_lanes(positions):
    cosine, sine = rotation_tables(positions, HALF)
    cosine, sine = cosine[:, 0], sine[:, 0]
    return (
        jnp.concatenate([cosine] * 4, axis=1),
        jnp.concatenate([-sine, sine, -sine, sine], axis=1),
    )


def shards(
    block_input,
    segments,
    positions,
    norm1_gain,
    q_norm_gain,
    k_norm_gain,
    w_q,
    w_k,
    w_v,
    w_o,
    norm2_gain,
    w_gate,
    w_up,
    w_down,
    cotangent,
    *,
    n_dp,
    n_tensor,
):
    rows = w_q.shape[0]
    q_cols, kv_cols, ff_cols = w_q.shape[1], w_k.shape[1], w_gate.shape[1]
    small_gain = q_norm_gain.shape[0]
    head_dim = small_gain * n_dp
    seg_col, seg_row = segments[:, None], segments[None, :]
    gains = gain_rows(norm1_gain, norm2_gain, q_norm_gain, k_norm_gain, n_dp)
    pack_attn = jnp.concatenate(
        [w_q.astype(BF16), w_k.astype(BF16), w_v.astype(BF16), w_o.T.astype(BF16)], axis=1
    )
    pack_gates = lay(w_gate.astype(BF16), w_up.astype(BF16))
    pack_down = jnp.pad(w_down.T.astype(BF16), ((0, 0), (0, -ff_cols % LANES)))
    cosine, sine = rotation_lanes(positions)
    w0, w1, n1, qk, qm, kb, vb, lse, ctx, h, n2, gains = forward_call(
        n_dp, block_input, seg_col, seg_row, cosine, sine, gains, pack_attn, pack_gates
    )
    first, second, dn2, mlp, down = mlp_call(n_dp, n2, cotangent, w1, pack_down)
    gates_one, dh, dm, dwo, small_two = middle_call(n_dp, first, dn2, h, cotangent, w0, ctx, gains)
    gates_two, grad_o, grad_qkv, dn1, mlp_total, small_heads = last_call(
        n_dp, second, dwo, mlp, dm, qm, kb, vb, lse, qk, cosine, sine, seg_col, seg_row, n1, w0, gains
    )
    output_rows = (h + mlp_total.astype(F32)).astype(BF16)
    x = block_input.astype(F32)
    grad = dn1.astype(F32)
    inverse = lax.rsqrt(jnp.mean(x * x, axis=-1, keepdims=True) + EPSILON)
    scaled = grad * gains[0]
    inner = jnp.mean(scaled * x, axis=-1, keepdims=True)
    grad_input = dh + inverse * scaled - x * (inverse * inverse * inverse) * inner
    grad_gain_one = jnp.sum(grad * x * inverse, axis=0)
    share = 1.0 / n_tensor
    heads = small_heads.reshape(2, 8, 2, head_dim).sum(axis=(1, 2))
    small = lax.psum(
        jnp.concatenate([grad_gain_one * share, small_two.sum(axis=0) * share, heads[0], heads[1]]),
        ("dp", "tensor"),
    )
    me = lax.axis_index("dp")
    width = block_input.shape[1]

    def own(start, size):
        return lax.dynamic_slice_in_dim(small, start + me * size, size, 0)

    grad_gate, grad_up = unlay(jnp.concatenate([gates_one, gates_two], axis=1))
    return (
        output_rows,
        grad_input,
        own(0, rows),
        own(2 * width, small_gain),
        own(2 * width + head_dim, small_gain),
        grad_qkv[:, :q_cols],
        grad_qkv[:, q_cols : q_cols + kv_cols],
        grad_qkv[:, q_cols + kv_cols :],
        grad_o.T,
        own(width, rows),
        grad_gate,
        grad_up,
        down[:, :ff_cols].T,
    )


def solution(mesh):
    placed = (
        P("dp", None),
        P("dp"),
        P("dp"),
        P("dp"),
        P("dp"),
        P("dp"),
        P("dp", "tensor"),
        P("dp", "tensor"),
        P("dp", "tensor"),
        P("tensor", "dp"),
        P("dp"),
        P("dp", "tensor"),
        P("dp", "tensor"),
        P("tensor", "dp"),
        P("dp", None),
    )
    return jax.shard_map(
        functools.partial(shards, n_dp=mesh.shape["dp"], n_tensor=mesh.shape["tensor"]),
        mesh=mesh,
        in_specs=placed,
        out_specs=(
            P("dp", None),
            P("dp", None),
            P("dp"),
            P("dp"),
            P("dp"),
            P("dp", "tensor"),
            P("dp", "tensor"),
            P("dp", "tensor"),
            P("tensor", "dp"),
            P("dp"),
            P("dp", "tensor"),
            P("dp", "tensor"),
            P("tensor", "dp"),
        ),
        check_vma=False,
    )
```

time: 1790 us -> 670 us (0.37)
  waiting for transfers between devices: 1380 us -> 0 us
  Pallas kernels: 0 us -> 560 us
  matrix products: 159 us -> 0 us
  blocking collectives: 131 us -> 39.4 us
  other arithmetic: 90.3 us -> 30.6 us
    reduce_scatter x7 -> x0, waiting for transfers between devices: 785 us -> none  [the longest x1 189 us: shards(): lax.psum_scatter(grad_up_w, 'dp', scatter_dimension=0, tiled=True)]
    pallas_call x0 -> x4, Pallas kernels: none -> 560 us  [the longest x1 178 us: forward_call(): pl.pallas_call(functools.partial(forward_kernel, count), out_shape=outs,...]
    psum x4 -> x0, waiting for transfers between devices: 345 us -> none  [the longest x1 108 us: shards(): attn_total = lax.psum(matmul(context_b, weight_o), 'tensor')]
    all_gather x5 -> x0, waiting for transfers between devices: 245 us -> none  [the longest x1 85.3 us: gather_mlp(): lax.all_gather(w_up.astype(jnp.bfloat16), 'dp', axis=0, tiled=True)]
    dot_general x33 -> x0, matrix products: 159 us -> none  [the longest x7 47.9 us: matmul_tn(): lax.dot_general(left_op, right_op, (((0,), (0,)), ((), ())), preferred_el...]
    all_gather x2 -> x0, blocking collectives: 63 us -> none  [the longest x1 32 us: gather_attention(): lax.all_gather(w_k.astype(jnp.bfloat16), 'dp', axis=0, tiled=True)]
    unnamed x2 -> x0, blocking collectives: 61.7 us -> none
    psum x1, blocking collectives: 6.17 us -> 39.4 us  [shards(): lax.psum(jnp.concatenate([grad_gain_one * share, small_two.sum(axis=0) *...]
  transfers between devices with their start and end apart: 16 -> 0, of which waited for: 14 -> 0; matrix products, arithmetic and copies ran while one was open for 9% -> 0% of each run, Pallas kernels for 0% -> 0%
where the time goes in v2:
time: 670 us; the launch traced here: 661 us
  Pallas kernels  560 us (84%)
  blocking collectives  39.4 us (6%)
  other arithmetic  30.6 us (5%)
  local copies, waits for them, and re-layouts  28.8 us (4%)
    pallas_call x1, Pallas kernels, forward_call(): pl.pallas_call(functools.partial(forward_kernel, count), out_shape=outs,...  178 us
    pallas_call x1, Pallas kernels, mlp_call(): pl.pallas_call(functools.partial(mlp_kernel, count), out_shape=[shape((wi...  164 us
    pallas_call x1, Pallas kernels, last_call(): pl.pallas_call(functools.partial(last_kernel, count), out_shape=[shape((r...  135 us
    pallas_call x1, Pallas kernels, middle_call(): pl.pallas_call(functools.partial(middle_kernel, count), out_shape=[shape(...  83.7 us
    psum x1, blocking collectives, shards(): lax.psum(jnp.concatenate([grad_gain_one * share, small_two.sum(axis=0) *...  39.4 us

profile of v2, /device:TPU:0, one launch (start us, length us, event | category | flops | bytes accessed | tf_op | source)
XLA Modules:
  0.0 660.7 jit_solution(16467289586377903422)
XLA Ops:
  0.7 0.9 convert_dynamic-update-slice_fusion.1
  1.6 0.8 convert_dynamic-update-slice_fusion
  3.2 0.7 convert_convert_fusion
  4.7 0.7 convert_element_type.69
  5.4 1.9 fusion.8
  7.3 1.8 pad_maximum_fusion.4
  9.8 1.4 convert_element_type.82
  11.2 0.8 copy-done.3
  12.9 2.0 copy.33
  15.5 1.8 concatenate.35.refs_7_
  17.3 1.0 copy.34.refs_1_.refs_11_
  18.4 0.8 pad_maximum_fusion.6.refs_6_
  19.2 178.0 %shard_map.246 = (bf16[1536,1024]{1,0:T(8,128)(2,1)}, bf16[1536,3456]{1,0:T(8,128)(2,1)}, bf16[1024,1536]{1,0:T(8,128)(2,1)}, f32[1024,512]{1,0:T(8,128)}, bf16[...) custom-call(bf16[1024,1536]{1,0:T(8,128)(2,1)} %refs_0_.1, ...), custom_call_target="tpu_custom_call" | custom-call | tf_op jit(solution)/shard_map/pallas_call | solution.py:479
  197.3 0.9 pad.18.refs_3_
  198.2 164.2 %shard_map.247 = (bf16[1536,1792]{1,0:T(8,128)(2,1)}, bf16[1536,1664]{1,0:T(8,128)(2,1)}, bf16[1024,1536]{1,0:T(8,128)(2,1)}, bf16[1024,1536]{1,0:T(8,128)(2,1)}, f32[192,1792]{1,0:T(8,128)}) custom-call(bf16[1024,1536]{1,0:T(8,128)(2,1)} %get-tuple-element.42.refs_0_, bf16[1024,1536]{1,0:T(8,128)(2,1)} %refs_3_.1, ...), custom_call_target="tpu_custom_call" | custom-call | tf_op jit(solution)/shard_map/pallas_call | solution.py:818
  362.4 83.7 %shard_map.248 = (f32[192,1792]{1,0:T(8,128)}, f32[1024,1536]{1,0:T(8,128)}, bf16[6,1024,128]{2,1,0:T(8,128)(2,1)}, bf16[1536,384]{1,0:T(8,128)(2,1)}, f32[8,1536]{1,0:T(8,128)}) custom-call(bf16[1536,1792]{1,0:T(8,128)(2,1)} %get-tuple-element.45.refs_0_, bf16[1024,1536]{1,0:T(8,128)(2,1)} %get-tuple-element.46.refs_1_, ...), custom_call_target="tpu_custom_call" | custom-call | tf_op jit(solution)/shard_map/pallas_call | solution.py:920
  446.0 134.6 %shard_map.249 = (f32[192,1664]{1,0:T(8,128)}, f32[192,384]{1,0:T(8,128)}, f32[192,640]{1,0:T(8,128)}, bf16[1024,1536]{1,0:T(8,128)(2,1)}, bf16[1024,1536]{1,0:T(8,128)(2,1)}, /*index=5*/f32[16,128]{1,0:T(8,128)}) custom-call(bf16[1536,1664]{1,0:T(8,128)(2,1)} %get-tuple-element.44.refs_0_, bf16[1536,384]{1,0:T(8,128)(2,1)} %get-tuple-element.50.refs_1_, ...), custom_call_target="tpu_custom_call" | custom-call | tf_op jit(solution)/shard_map/pallas_call | solution.py:1074
  580.7 1.9 pad_maximum_fusion
  582.5 2.6 reshape.68
  585.1 9.6 %slice_reduce_fusion = (f32[192,13,128]{2,1,0:T(8,128)S(1)}, f32[192,13,128]{2,1,0:T(8,128)S(1)}) fusion(f32[192,13,2,128]{3,2,1,0:T(2,128)} %reshape.68), kind=kLoop, calls=%fused_computation.21 | loop fusion | bytes 5111808 | tf_op jit(solution)/shard_map/slice | solution.py:1132
  595.2 1.1 fusion.9
  596.3 1.2 pad_maximum_fusion.3
  598.0 1.2 pad_maximum_fusion.2
  599.1 1.5 slice_reduce_fusion.2
  601.4 2.6 fusion.7
  604.3 39.4 %psum.7 = f32[3200]{0:T(1024)S(1)} all-reduce(f32[3200]{0:T(1024)S(1)} %concatenate.36), channel_id=1, replica_groups=mesh['dp'=8,'tensor'=4] {'dp','tensor'}, use_global_device_ids=true, to_apply=%region_5.6 | all-reduce | flops 3200 | bytes 25600 | tf_op jit(solution)/shard_map/psum | solution.py:1211
  644.9 6.5 fusion.2
  651.4 5.6 add_convert_fusion
  657.0 0.7 slice.58
  657.7 0.7 fusion.10
  658.4 1.2 slice_bitcast_fusion
  659.6 0.7 copy.49
  (73 shorter events, 7.0 us)
Async XLA Ops:
  0.6 8.5 %copy-start.5 = (f32[192,1728]{1,0:T(8,128)S(1)}, f32[192,1728]{1,0:T(8,128)}, u32[]{:S(2)}) copy-start(f32[192,1728]{1,0:T(8,128)} %param.26) | copy-start | bytes 3981316
  11.2 0.8 copy-start.3
  12.9 2.6 slice-start
  14.9 2.4 copy-start.14
  14.9 3.5 copy-start.11
  14.9 3.5 copy-start.12
  15.5 2.9 copy-start.8
  15.5 2.9 copy-start.9
  19.2 178.0 %copy-start.6 = (f32[1728,192]{0,1:T(8,128)S(1)}, f32[1728,192]{0,1:T(8,128)}, u32[]{:S(2)}) copy-start(f32[1728,192]{0,1:T(8,128)} %param.28) | copy-start | bytes 3981316
  597.4 3.2 copy-start
  597.9 3.4 copy-start.1
  601.3 2.7 copy-start.15
  601.3 2.8 copy-start.13
  644.9 6.5 copy-start.2
  651.4 5.6 copy-start.7
  651.4 7.0 %copy-start.4 = (f32[192,1792]{1,0:T(8,128)S(1)}, f32[192,1792]{1,0:T(8,128)}, u32[]{:S(2)}) copy-start(f32[192,1792]{1,0:T(8,128)} %get-tuple-element.68) | copy-start | bytes 4128772
  657.0 2.6 copy-start.10

commit v3 on v2

v3 whole, which is shorter than its diff:
```python
import functools

import jax
import jax.numpy as jnp
from jax import lax
from jax.experimental import pallas as pl
from jax.experimental.pallas import tpu as pltpu
from jax.sharding import PartitionSpec as P

EPSILON = 1e-05
ROPE_BASE = 1000000.0
MASKED = -1e30


MESH = pl.DeviceIdType.MESH
NEAR = 2
HALF = 64
LANES = 128
HIGHEST = lax.Precision.HIGHEST
BF16 = jnp.bfloat16
F32 = jnp.float32


def whole_block():
    return pl.BlockSpec(memory_space=pltpu.VMEM)


def in_place():
    return pl.BlockSpec(memory_space=pl.ANY)


def remote(src, dst, send, recv, dp, tensor):
    return pltpu.make_async_remote_copy(
        src_ref=src,
        dst_ref=dst,
        send_sem=send,
        recv_sem=recv,
        device_id=(dp, tensor),
        device_id_type=MESH,
    )


def begin(src, dst, sem):
    copy = pltpu.make_async_copy(src, dst, sem)
    copy.start()
    return copy


def dot_nn(left, right):
    return jnp.dot(left, right, preferred_element_type=F32)


def dot_nt(left, right):
    return lax.dot_general(left, right, (((1,), (1,)), ((), ())), preferred_element_type=F32)


def dot_tn(left, right):
    return lax.dot_general(left, right, (((0,), (0,)), ((), ())), preferred_element_type=F32)


class Place:
    def __init__(self, count):
        self.count = count
        self.depth = count // NEAR
        self.me = lax.axis_index("dp")
        self.tensor = lax.axis_index("tensor")
        self.far = self.me // NEAR
        self.near = lax.rem(self.me, NEAR)
        self.core = lax.rem(self.tensor, 2)
        self.mate = self.tensor + 1 - 2 * self.core
        self.across = lax.rem(self.tensor + 2, 4)
        self.beside = self.me + 1 - 2 * self.near

    def ahead(self, step):
        return lax.rem(self.far + step, self.depth)

    def behind(self, step):
        return lax.rem(self.far + self.depth - step, self.depth)

    def greet(self, everyone, tensor):
        barrier = pltpu.get_barrier_semaphore()
        peers = []
        if everyone:
            peers += [(lax.rem(self.me + d, self.count), self.tensor) for d in range(1, self.count)]
        else:
            peers += [
                (self.ahead(step) * NEAR + self.near, self.tensor) for step in range(1, self.depth)
            ]
            peers.append((self.beside, self.tensor))
        if tensor:
            peers += [(self.me, lax.rem(self.tensor + t, 4)) for t in range(1, 4)]
        for peer in peers:
            pl.semaphore_signal(barrier, 1, device_id=peer, device_id_type=MESH)
        pl.semaphore_wait(barrier, len(peers))


class Gather:
    def __init__(self, place, shard, full, late, sems):
        self.place, self.shard, self.full = place, shard, full
        self.rows = shard.shape[0]
        self.cuts = [(0, self.rows - late)] + ([(self.rows - late, late)] if late else [])
        self.zsend, self.zrecv, self.ysend, self.yrecv, self.own = sems
        self.sent = []

    @staticmethod
    def sems(count):
        depth = count // NEAR
        dma = pltpu.SemaphoreType.DMA
        return [dma((2, depth - 1, 3)), dma((2, depth - 1, 3)), dma((2 * depth - 1, 2)), dma((2 * depth - 1, 2)), dma]

    def spot(self, block, cut):
        start, size = self.cuts[cut]
        return self.full.at[pl.ds(pl.multiple_of(block * self.rows + start, 16), size), :]

    def mine(self, cut):
        start, size = self.cuts[cut]
        return self.shard.at[pl.ds(start, size), :]

    def block(self, way, step, other):
        far = self.place.far - step if way == 0 else self.place.far + step
        return far * NEAR + (1 - self.place.near if other else self.place.near)

    def valid(self, way, step):
        return self.place.far >= step if way == 0 else self.place.far + step < self.place.depth

    def emit(self, make):
        copy, when = make()
        if when is None:
            copy.start()
        else:
            pl.when(when)(copy.start)
        self.sent.append(make)

    def along(self, way, step, cut, other):
        place = self.place
        if step >= place.depth - 1:
            return

        def make():
            more = place.far < place.depth - 1 if way == 0 else place.far > 0
            spot = self.spot(self.block(way, step, other), cut)
            copy = remote(
                self.mine(cut) if step == 0 and not other else spot, spot,
                self.zsend.at[way, step, cut + other], self.zrecv.at[way, step, cut + other],
                place.me + (NEAR if way == 0 else -NEAR), place.tensor,
            )
            return copy, more if step == 0 else more & self.valid(way, step)

        self.emit(make)

    def crossing(self, way, step, cut, other):
        place = self.place
        spot = self.spot(self.block(way, step, other), cut)
        slot = step if way == 0 else step + place.depth - 1
        return remote(
            self.mine(cut) if step == 0 and not other else spot, spot,
            self.ysend.at[slot, cut], self.yrecv.at[slot, cut], place.beside, place.tensor,
        ), (self.valid(way, step) if step else None)

    def over(self, way, step, cut):
        self.emit(lambda: self.crossing(way, step, cut, 0))

    def came_over(self, way, step, cut):
        copy, when = self.crossing(way, step, cut, 1)
        if when is None:
            copy.wait_recv()
        else:
            pl.when(when)(copy.wait_recv)

    def start(self):
        place = self.place
        self.local = lambda: pltpu.make_async_copy(
            self.shard, self.full.at[pl.ds(pl.multiple_of(place.me * self.rows, 16), self.rows), :], self.own
        )
        self.local().start()
        for cut in reversed(range(len(self.cuts))):
            self.over(0, 0, cut)
        for cut in range(len(self.cuts)):
            for way in range(2):
                self.along(way, 0, cut, 0)

    def steps(self):
        place = self.place
        if len(self.cuts) > 1:
            self.came_over(0, 0, 1)
            for way in range(2):
                self.along(way, 0, 1, 1)
            yield
        for step in range(1, place.depth):
            for cut in range(len(self.cuts)):
                for other in range(cut + 1):
                    for way in range(2):
                        spot = self.spot(self.block(way, step, other), cut)
                        copy = remote(
                            spot, spot, self.zsend.at[way, step - 1, cut + other],
                            self.zrecv.at[way, step - 1, cut + other], place.me, place.tensor,
                        )
                        pl.when(self.valid(way, step))(copy.wait_recv)
                        self.along(way, step, cut, other)
                        if cut == 0:
                            self.over(way, step, cut)
                    yield

    def finish(self):
        self.came_over(0, 0, 0)
        for step in range(1, self.place.depth):
            for way in range(2):
                self.came_over(way, step, 0)
        self.local().wait()

    def settle(self):
        for make in self.sent:
            copy, when = make()
            if when is None:
                copy.wait_send()
            else:
                pl.when(when)(copy.wait_send)


def late_share(rows, share):
    return int(rows * share) // 16 * 16


class TensorSum:
    def __init__(self, place, part, total, tiles, scratch):
        self.place, self.part, self.total, self.tiles = place, part, total, tiles
        self.tile = part.shape[0] // tiles
        self.half = self.tile // 2
        self.near, self.chip, self.far, self.sems = scratch
        self.sent = []

    @staticmethod
    def scratch(rows, width, tiles, kind):
        half = (rows // 2, width)
        return [
            pltpu.VMEM(half, kind), pltpu.VMEM(half, BF16), pltpu.VMEM(half, BF16), pltpu.SemaphoreType.DMA((6, tiles))
        ]

    def half_rows(self, index, which):
        return pl.ds(pl.multiple_of(index * self.tile + which * self.half, 16), self.half)

    def slot(self, index):
        return pl.ds(index * self.half, self.half)

    def core_copy(self, index):
        place = self.place
        return remote(
            self.part.at[self.half_rows(index, 1 - place.core), :], self.near.at[self.slot(index), :],
            self.sems.at[0, index], self.sems.at[1, index], place.me, place.mate,
        )

    def across_copy(self, index):
        place = self.place
        return remote(
            self.chip.at[self.slot(index), :], self.far.at[self.slot(index), :],
            self.sems.at[2, index], self.sems.at[3, index], place.me, place.across,
        )

    def back_copy(self, index, which):
        place = self.place
        rows = self.half_rows(index, which)
        return remote(
            self.total.at[rows, :], self.total.at[rows, :],
            self.sems.at[4, index], self.sems.at[5, index], place.me, place.mate,
        )

    def send_core(self, index):
        self.core_copy(index).start()
        self.sent.append(lambda: self.core_copy(index))

    def send_across(self, index):
        place = self.place
        self.core_copy(index).wait_recv()
        mine = self.part[self.half_rows(index, place.core), :].astype(F32)
        self.chip[self.slot(index), :] = (mine + self.near[self.slot(index), :].astype(F32)).astype(BF16)
        self.across_copy(index).start()
        self.sent.append(lambda: self.across_copy(index))

    def send_back(self, index):
        place = self.place
        self.across_copy(index).wait_recv()
        both = self.chip[self.slot(index), :].astype(F32) + self.far[self.slot(index), :].astype(F32)
        self.total[self.half_rows(index, place.core), :] = both.astype(self.total.dtype)
        self.back_copy(index, place.core).start()

    def finish(self, index):
        self.back_copy(index, 1 - self.place.core).wait_recv()
        self.back_copy(index, self.place.core).wait_send()

    def steps(self):
        for index in range(2):
            self.send_across(index)
            yield
        for index in range(self.tiles):
            self.send_back(index)
            if index + 2 < self.tiles:
                self.send_across(index + 2)
            yield

    def settle(self):
        for make in self.sent:
            make().wait_send()


def lane_ids(width=LANES):
    return lax.broadcasted_iota(jnp.int32, (1, width), 1)


def head_mean(values):
    row = lax.broadcasted_iota(jnp.int32, (LANES, LANES), 0)
    col = lax.broadcasted_iota(jnp.int32, (LANES, LANES), 1)
    groups = jnp.where(row // HALF == col // HALF, 1.0 / HALF, 0.0).astype(F32)
    return jnp.dot(values, groups, precision=HIGHEST, preferred_element_type=F32)


def turn(values, cosine, sine):
    ahead = pltpu.roll(values, LANES - HALF // 2, 1)
    back = pltpu.roll(values, HALF // 2, 1)
    first = lax.rem(lane_ids(), HALF) < HALF // 2
    return values * cosine + jnp.where(first, ahead, back) * sine


def bias_block(seg_col, seg_row, bias, first, tile):
    last = first + tile
    rows = lax.broadcasted_iota(jnp.int32, (tile, last), 0) + first
    cols = lax.broadcasted_iota(jnp.int32, (tile, last), 1)
    allowed = (seg_col[pl.ds(first, tile), :] == seg_row[:, pl.ds(0, last)]) & (rows >= cols)
    bias[:, pl.ds(0, last)] = jnp.where(allowed, 0.0, MASKED)


def drain(*moves):
    for one in moves:
        for _ in one:
            pass


def ahead(moves, count=1):
    for _ in range(count):
        next(moves, None)


def polled(count, body, *polls):
    def step(index, carry):
        body(index)
        for at in range(count):
            due = [(moves, times[at]) for moves, times in polls if at in times]
            if due:

                @pl.when(index == at)
                def _(due=due):
                    for moves, times in due:
                        ahead(moves, times)

        return carry

    lax.fori_loop(0, count, step, 0)


def every(count, times=1, first=0):
    return {index: times for index in range(first, count)}


def blocks(total, size, body):
    def step(index, carry):
        body(pl.multiple_of(index * size, size))
        return carry

    lax.fori_loop(0, total // size, step, 0)


def forward_kernel(count, *refs):
    (
        x_hbm, seg_col, seg_row, cos_ref, sin_ref, gain_ref, pack_attn, pack_gates,
        full_attn, full_gates, n1_out, qk_out, qm_out, kb_out, vb_out, lse_out, ctx_out, h_out, n2_out, gains_out,
        x_ref, w0, n1_ref, qk_ref, qm_ref, kb_ref, vb_ref, lse_ref, ctx_ref, h_ref, n2_ref,
        bias, gain_slots, part, total, tmp_near, tmp_chip, tmp_far, sum_sems, gain_send, gain_recv, copy_sems,
        *gather_sems,
    ) = refs
    place = Place(count)
    seq, width = x_ref.shape
    q_cols = ctx_ref.shape[1]
    kv_cols = kb_ref.shape[1]
    pairs = q_cols // LANES
    group = (q_cols // HALF) // (kv_cols // HALF)
    tile = seq // 4
    load = begin(x_hbm, x_ref, copy_sems.at[0])
    place.greet(True, True)
    first = Gather(place, pack_attn, w0, late_share(pack_attn.shape[0], 1 / 6), gather_sems[:5])
    second = Gather(place, pack_gates, full_gates, late_share(pack_gates.shape[0], 1 / 6), gather_sems[5:])
    gain_copies = []
    for step in range(1, count):
        copy = remote(
            gain_ref, gain_slots.at[step], gain_send.at[step], gain_recv.at[step],
            lax.rem(place.me + step, count), place.tensor,
        )
        copy.start()
        gain_copies.append(copy)
    first.start()
    for qb in range(4):
        bias_block(seg_col, seg_row, bias.at[qb], qb * tile, tile)
    gains = gain_ref[...]
    for copy in gain_copies:
        copy.wait_recv()
    for step in range(1, count):
        gains = gains + gain_slots[step]
    gains_out[...] = gains
    moves_first = first.steps()
    ahead(moves_first, 2)
    g1 = gains_out[pl.ds(0, 1), :]
    g2 = gains_out[pl.ds(1, 1), :]
    load.wait()

    def norm_one(index, carry):
        rows = pl.ds(pl.multiple_of(index * LANES, LANES), LANES)
        x = x_ref[rows, :].astype(F32)
        inverse = lax.rsqrt(jnp.mean(x * x, axis=1, keepdims=True) + EPSILON)
        n1_ref[rows, :] = (x * inverse * g1).astype(BF16)
        return carry

    lax.fori_loop(0, seq // LANES, norm_one, 0)
    saves = [begin(n1_ref, n1_out, copy_sems.at[1])]
    drain(moves_first)
    second.start()
    moves = second.steps()
    first.finish()
    saves.append(begin(w0, full_attn, copy_sems.at[2]))
    gq = gains_out[pl.ds(2, 1), pl.ds(0, LANES)]
    gk = gains_out[pl.ds(3, 1), pl.ds(0, LANES)]
    lanes = lane_ids()

    def project(index, carry):
        rows = pl.ds(pl.multiple_of(index * tile, tile), tile)
        qkv = dot_nn(n1_ref[rows, :], w0[:, pl.ds(0, q_cols + 2 * kv_cols)])
        qk_ref[rows, :] = qkv[:, : q_cols + kv_cols]
        vb_ref[rows, :] = qkv[:, q_cols + kv_cols :].astype(BF16)
        cosine, sine = cos_ref[rows, :], sin_ref[rows, :]
        for pair in range(pairs + 1):
            raw = qkv[:, pair * LANES : (pair + 1) * LANES]
            inverse = lax.rsqrt(head_mean(raw * raw) + EPSILON)
            turned = turn(raw * inverse * (gk if pair == pairs else gq), cosine, sine)
            if pair == pairs:
                kb_ref[rows, :] = turned.astype(BF16)
                continue
            swapped = pltpu.roll(turned, HALF, 1)
            for side in range(2):
                head = 2 * pair + side
                kv = head // group
                keep = (turned if side == kv else swapped).astype(BF16) * 0.125
                qm_ref[head, rows, :] = jnp.where(lanes // HALF == kv, keep, jnp.zeros_like(keep))
        return carry

    lax.fori_loop(0, 4, project, 0)
    for index, (src, dst) in enumerate(((qk_ref, qk_out), (qm_ref, qm_out), (kb_ref, kb_out), (vb_ref, vb_out))):
        saves.append(begin(src, dst, copy_sems.at[3 + index]))
    next(moves, None)

    for qb in range(4):
        last = (qb + 1) * tile
        rows = pl.ds(qb * tile, tile)

        def attend(pair, carry, last=last, rows=rows, qb=qb):
            halves, sums = [], []
            for side in range(2):
                head = 2 * pair + side
                kv = head // group
                logits = dot_nt(qm_ref[head, rows, :], kb_ref[pl.ds(0, last), :]) + bias[qb, :, pl.ds(0, last)]
                top = jnp.max(logits, axis=1, keepdims=True)
                expo = jnp.exp(logits - top)
                summed = jnp.sum(expo, axis=1, keepdims=True)
                probs = (expo * (1.0 / summed)).astype(BF16)
                got = dot_nn(probs, vb_ref[pl.ds(0, last), :])
                halves.append(jnp.where(kv == side, got, pltpu.roll(got, HALF, 1)))
                sums.append(top + jnp.log(summed))
            ctx_ref[rows, pl.ds(pl.multiple_of(pair * LANES, LANES), LANES)] = jnp.where(
                lanes < HALF, halves[0], halves[1]
            ).astype(BF16)
            carry = jnp.where(lanes == 2 * pair, sums[0], carry)
            return jnp.where(lanes == 2 * pair + 1, sums[1], carry)

        lse_ref[rows, :] = lax.fori_loop(0, pairs, attend, jnp.zeros((tile, LANES), F32))
        next(moves, None)
    saves.append(begin(lse_ref, lse_out, copy_sems.at[7]))
    saves.append(begin(ctx_ref, ctx_out, copy_sems.at[8]))

    summed = TensorSum(place, part, total, 4, (tmp_near, tmp_chip, tmp_far, sum_sems))
    for index in range(4):
        rows = pl.ds(index * tile, tile)
        part[rows, :] = dot_nt(ctx_ref[rows, :], w0[:, pl.ds(q_cols + 2 * kv_cols, q_cols)])
        summed.send_core(index)
    summed.send_across(0)
    summed.send_across(1)
    next(moves, None)
    for index in range(4):
        summed.send_back(index)
        if index < 2:
            summed.send_across(index + 2)
        next(moves, None)
        summed.finish(index)

        def norm_two(sub, carry, index=index):
            rows = pl.ds(pl.multiple_of(index * tile + sub * LANES, LANES), LANES)
            h = x_ref[rows, :].astype(F32) + total[rows, :]
            h_ref[rows, :] = h
            inverse = lax.rsqrt(jnp.mean(h * h, axis=1, keepdims=True) + EPSILON)
            n2_ref[rows, :] = (h * inverse * g2).astype(BF16)
            return carry

        lax.fori_loop(0, tile // LANES, norm_two, 0)
        next(moves, None)
    saves.append(begin(h_ref, h_out, copy_sems.at[9]))
    saves.append(begin(n2_ref, n2_out, copy_sems.at[10]))
    drain(moves)
    second.finish()
    for save in saves:
        save.wait()
    for copy in gain_copies:
        copy.wait_send()
    first.settle()
    second.settle()
    summed.settle()


def forward_call(count, x, seg_col, seg_row, cosine, sine, gains, pack_attn, pack_gates):
    seq, width = x.shape
    rows = pack_attn.shape[0]
    q_cols, kv_cols = 384, LANES
    kept = [
        ((seq, width), BF16),
        ((seq, q_cols + kv_cols), F32),
        ((q_cols // HALF, seq, LANES), BF16),
        ((seq, LANES), BF16),
        ((seq, LANES), BF16),
        ((seq, LANES), F32),
        ((seq, q_cols), BF16),
        ((seq, width), F32),
        ((seq, width), BF16),
    ]
    attn = ((count * rows, pack_attn.shape[1]), BF16)
    outs = [attn, ((count * rows, pack_gates.shape[1]), BF16), *kept, (gains.shape, F32)]
    dma = pltpu.SemaphoreType.DMA
    return pl.pallas_call(
        functools.partial(forward_kernel, count),
        out_shape=[jax.ShapeDtypeStruct(*out) for out in outs],
        in_specs=[in_place()] + [whole_block()] * 5 + [in_place()] * 2,
        out_specs=[in_place()] * 11 + [whole_block()],
        scratch_shapes=[
            pltpu.VMEM((seq, width), BF16),
            pltpu.VMEM(*attn),
            *[pltpu.VMEM(*one) for one in kept],
            pltpu.VMEM((4, seq // 4, seq), F32),
            pltpu.VMEM((count,) + gains.shape, F32),
            pltpu.VMEM((seq, width), F32),
            pltpu.VMEM((seq, width), F32),
            *TensorSum.scratch(seq, width, 4, F32),
            dma((count,)),
            dma((count,)),
            dma((11,)),
            *Gather.sems(count),
            *Gather.sems(count),
        ],
        compiler_params=pltpu.CompilerParams(
            collective_id=1, has_side_effects=True, vmem_limit_bytes=61 << 20
        ),
    )(x, seg_col, seg_row, cosine, sine, gains, pack_attn, pack_gates)


class Scatter:
    def __init__(self, place, partial, result, late, scratch):
        self.place, self.partial, self.result = place, partial, result
        self.rows = partial.shape[0] // place.count
        self.late = late
        early = self.rows - late
        half = (early // 2 + 15) // 16 * 16
        self.cuts = [(0, half), (half, early - half)] if early > half else [(0, early)]
        self.tail = (early, late)
        self.over_in, self.far_in, self.far_other, self.late_in = scratch[:4]
        self.zsend, self.zrecv, self.ysend, self.yrecv, self.lsend, self.lrecv = scratch[4:]
        self.sent = []
        depth = place.depth
        orders = [
            sorted(range(depth), key=lambda goal, far=far: (-abs(goal - far), -goal)) for far in range(depth)
        ]
        self.goals = []
        for index in range(depth):
            goal = jnp.int32(0)
            for far in range(depth):
                goal = goal + orders[far][index] * (place.far == far).astype(jnp.int32)
            self.goals.append(goal)
        self.pieces = [(index, cut) for index in range(depth) for cut in range(len(self.cuts))]

    @staticmethod
    def scratch(count, rows, width, late):
        depth = count // NEAR
        dma = pltpu.SemaphoreType.DMA
        return [
            pltpu.VMEM((depth, rows - late, width), BF16),
            pltpu.VMEM((depth + 2, rows, width), BF16),
            pltpu.VMEM((depth + 2, max(late, 16), width), BF16),
            pltpu.VMEM((max(late, 16), width), BF16),
            dma((depth - 1, 4)),
            dma((depth + 2, 4)),
            dma((depth, 2)),
            dma((depth, 2)),
            dma,
            dma,
        ]

    def spot(self, goal, other, start, size):
        near = 1 - self.place.near if other else self.place.near
        return pl.ds(pl.multiple_of((goal * NEAR + near) * self.rows + start, 16), size)

    def over(self, number):
        place = self.place
        index, cut = self.pieces[number]
        start, size = self.cuts[cut]
        return remote(
            self.partial.at[self.spot(self.goals[index], True, start, size), :],
            self.over_in.at[index, pl.ds(start, size), :],
            self.ysend.at[index, cut], self.yrecv.at[index, cut], place.beside, place.tensor,
        )

    def cross(self, number):
        if number < len(self.pieces):
            self.over(number).start()
            self.sent.append(lambda: self.over(number))

    def start(self):
        for number in range(len(self.cuts)):
            self.cross(number)

    def add(self, spot, sources):
        size = sources[0].shape[0]
        part = 32 if size % 32 == 0 else 16

        def body(index, carry):
            start = pl.multiple_of(index * part, 16)
            rows = pl.ds(pl.multiple_of(spot.start + start, 16), part)
            total = self.partial[rows, :].astype(F32)
            for source in sources:
                total = total + source[pl.ds(start, part), :].astype(F32)
            self.partial[rows, :] = total.astype(BF16)
            return carry

        lax.fori_loop(0, size // part, body, 0)

    def item(self, item):
        return (0, *self.cuts[item]) if item < 2 else (item - 2, *self.tail)

    def into(self, slot, item):
        other, start, size = self.item(item)
        return self.far_other.at[slot] if other else self.far_in.at[slot, pl.ds(start, size), :]

    def wait_far(self, slot, item):
        place = self.place
        into = self.into(slot, item)
        remote(
            into, into, self.zsend.at[0, item], self.zrecv.at[slot, item], place.me, place.tensor
        ).wait_recv()
        return into

    def hop(self, index, item):
        place = self.place
        goal = self.goals[index]
        sign = 2 * (goal > place.far).astype(jnp.int32) - 1
        ends = ((goal - place.far) * sign == 1).astype(jnp.int32)
        slot = goal + ends * (place.depth + (1 - sign) // 2 - goal)
        return remote(
            self.partial.at[self.spot(goal, *self.item(item)), :], self.into(slot, item),
            self.zsend.at[index, item], self.zrecv.at[slot, item], place.me + sign * NEAR, place.tensor,
        )

    def arrived(self, index, cut):
        number = index * len(self.cuts) + cut
        self.over(number).wait_recv()
        self.cross(number + len(self.cuts))
        start, size = self.cuts[cut]
        return self.over_in.at[index, pl.ds(start, size), :]

    def pass_on(self, index, item):
        place = self.place
        goal = self.goals[index]
        up = goal > place.far
        fed = (up & (place.far > 0)) | (jnp.logical_not(up) & (place.far < place.depth - 1))
        spot = self.spot(goal, *self.item(item))
        base = [self.arrived(index, item)] if item < 2 else []

        @pl.when(fed)
        def _():
            self.add(spot, base + [self.wait_far(goal, item)])

        if base:

            @pl.when(jnp.logical_not(fed))
            def _():
                self.add(spot, base)

        self.hop(index, item).start()
        self.sent.append(lambda: self.hop(index, item))

    def close(self, item):
        place = self.place
        spot = self.spot(place.far, *self.item(item))
        for way, comes in enumerate((place.far > 0, place.far < place.depth - 1)):

            @pl.when(comes)
            def _(way=way):
                self.add(spot, [self.wait_far(place.depth + way, item)])

    def last(self):
        place = self.place
        return remote(
            self.partial.at[self.spot(place.far, True, *self.tail), :], self.late_in,
            self.lsend, self.lrecv, place.beside, place.tensor,
        )

    def steps(self):
        place = self.place
        for index in range(place.depth - 1):
            if self.late:
                self.pass_on(index, 2)
                self.pass_on(index, 3)
                yield
            for cut in range(len(self.cuts)):
                self.pass_on(index, cut)
                yield
        if self.late:
            self.close(3)
            self.last().start()
            self.sent.append(self.last)
            self.close(2)
            yield
        for cut, (start, size) in enumerate(self.cuts):
            own = self.spot(place.far, 0, start, size)
            self.add(own, [self.arrived(place.depth - 1, cut)])
            self.close(cut)
            self.result[pl.ds(start, size), :] = self.partial[own, :].astype(F32)
            yield
        if self.late:
            start, size = self.tail
            self.last().wait_recv()
            self.result[pl.ds(start, size), :] = (
                self.partial[self.spot(place.far, 0, start, size), :].astype(F32) + self.late_in[...].astype(F32)
            )
            yield

    def settle(self):
        for make in self.sent:
            make().wait_send()


def mlp_kernel(count, share, *refs):
    (
        n2_hbm, cot_hbm, gates_hbm, pack_down,
        first_out, second_out, dn2_out, part_out, down_ref,
        n2_ref, cot_ref, dn2_part, dn2_ref, w1, w2, ab, hid, partial, near, chip, far, sum_sems, copy_sems, *rest,
    ) = refs
    place = Place(count)
    seq, width = n2_ref.shape
    both = w1.shape[1]
    even = both // (2 * LANES)
    split = first_out.shape[1]
    tile = seq // 4
    lanes = lane_ids()
    loads = [
        begin(src, dst, copy_sems.at[index])
        for index, (src, dst) in enumerate(((n2_hbm, n2_ref), (gates_hbm, w1), (cot_hbm, cot_ref)))
    ]
    place.greet(False, True)
    late = late_share(pack_down.shape[0], share)
    gather = Gather(place, pack_down, w2, late, rest[:5])
    scatter = Scatter(place, partial, down_ref, late, rest[5:])
    summed = TensorSum(place, dn2_part, dn2_ref, 4, (near, chip, far, sum_sems))
    gather.start()
    moves, sums, tensor = gather.steps(), scatter.steps(), summed.steps()
    loads[0].wait()
    loads[1].wait()

    def gate_up(index):
        cols = pl.ds(pl.multiple_of(index * 2 * LANES, 2 * LANES), 2 * LANES)
        got = dot_nn(n2_ref[...], w1[:, cols])
        gate, up = got[:, :LANES], got[:, LANES:]
        sig = jax.nn.sigmoid(gate)
        act = gate * sig
        hid[:, pl.ds(pl.multiple_of(index * LANES, LANES), LANES)] = (act * up).astype(BF16)
        slope = up * sig * (1.0 + gate * (1.0 - sig))
        ab[:, cols] = jnp.concatenate([slope, act], axis=1).astype(BF16)

    polled(even, gate_up, (moves, {8: 1, 12: 1}))
    tail = pl.ds(2 * even * LANES, LANES)
    got = dot_nn(n2_ref[...], w1[:, tail])
    up = pltpu.roll(got, HALF, 1)
    sig = jax.nn.sigmoid(got)
    act = got * sig
    hid[:, pl.ds(even * LANES, LANES)] = jnp.where(lanes < HALF, act * up, 0.0).astype(BF16)
    slope = up * sig * (1.0 + got * (1.0 - sig))
    ab[:, tail] = jnp.where(lanes < HALF, slope, pltpu.roll(act, HALF, 1)).astype(BF16)
    loads[2].wait()

    def down_grad(index):
        rows = pl.ds(pl.multiple_of(index * 384, 384), 384)
        partial[rows, :] = dot_tn(cot_ref[:, rows], hid[...]).astype(BF16)

    polled(width // 384, down_grad, (moves, {1: 1, 3: 1}))
    scatter.start()
    drain(moves)
    ahead(sums, 3)
    gather.finish()

    def inner_grad(index):
        got = dot_nn(cot_ref[...], w2[:, pl.ds(pl.multiple_of(index * 2 * LANES, 2 * LANES), 2 * LANES)])
        for side in range(2):
            piece = got[:, side * LANES : (side + 1) * LANES]
            cols = pl.ds(pl.multiple_of(index * 4 * LANES + side * 2 * LANES, 2 * LANES), 2 * LANES)
            ab[:, cols] = (ab[:, cols].astype(F32) * jnp.concatenate([piece, piece], axis=1)).astype(BF16)

    polled(even // 2, inner_grad, (sums, {2: 1, 5: 1}))
    got = dot_nn(cot_ref[...], w2[:, pl.ds((even - 1) * LANES, 2 * LANES)])
    piece = got[:, :LANES]
    cols = pl.ds(2 * (even - 1) * LANES, 2 * LANES)
    ab[:, cols] = (ab[:, cols].astype(F32) * jnp.concatenate([piece, piece], axis=1)).astype(BF16)
    piece = got[:, LANES:]
    piece = jnp.where(lanes < HALF, piece, pltpu.roll(piece, HALF, 1))
    ab[:, tail] = (ab[:, tail].astype(F32) * piece).astype(BF16)

    def normed_grad(index):
        rows = pl.ds(pl.multiple_of(index * tile, tile), tile)
        dn2_part[rows, :] = dot_nt(ab[rows, :], w1[...]).astype(BF16)
        for at in range(4):

            @pl.when(index == at)
            def _(at=at):
                summed.send_core(at)
                if at:
                    ahead(sums, 1)
                    ahead(tensor, 1)

    lax.fori_loop(0, 4, lambda index, carry: (normed_grad(index), carry)[1], 0)

    def output_part(index):
        rows = pl.ds(pl.multiple_of(index * 256, 256), 256)
        cot_ref[:, rows] = dot_nt(hid[...], w2[rows, :]).astype(BF16)

    polled(width // 256, output_part, (sums, {2: 1, 5: 1}), (tensor, {5: 1}))
    saves = [begin(cot_ref, part_out, copy_sems.at[4])]

    def gates_grad(index):
        rows = pl.ds(pl.multiple_of(index * 384, 384), 384)
        for low, high in ((0, split), (split, both)):
            w1[rows, pl.ds(low, high - low)] = dot_tn(n2_ref[:, rows], ab[:, pl.ds(low, high - low)]).astype(BF16)

    polled(width // 384, gates_grad, (sums, every(4)), (tensor, {1: 1, 3: 1}))
    saves.append(begin(w1.at[:, pl.ds(0, split)], first_out, copy_sems.at[5]))
    saves.append(begin(w1.at[:, pl.ds(split, both - split)], second_out, copy_sems.at[6]))
    drain(tensor, sums)
    for index in range(4):
        summed.finish(index)
    saves.append(begin(dn2_ref, dn2_out, copy_sems.at[3]))
    for save in saves:
        save.wait()
    gather.settle()
    scatter.settle()
    summed.settle()


def mlp_call(count, n2, cot, full_gates, pack_down, share=1 / 6):
    seq, width = n2.shape
    rows, down = pack_down.shape
    both = full_gates.shape[1]
    split = 14 * LANES
    shape = jax.ShapeDtypeStruct
    dma = pltpu.SemaphoreType.DMA
    return pl.pallas_call(
        functools.partial(mlp_kernel, count, share),
        out_shape=[
            shape((width, split), BF16),
            shape((width, both - split), BF16),
            shape((seq, width), BF16),
            shape((seq, width), BF16),
            shape((rows, down), F32),
        ],
        in_specs=[in_place()] * 4,
        out_specs=[in_place()] * 4 + [whole_block()],
        scratch_shapes=[
            *[pltpu.VMEM((seq, width), BF16)] * 4,
            pltpu.VMEM((width, both), BF16),
            pltpu.VMEM((width, down), BF16),
            pltpu.VMEM((seq, both), BF16),
            pltpu.VMEM((seq, down), BF16),
            pltpu.VMEM((width, down), BF16),
            *TensorSum.scratch(seq, width, 4, BF16),
            dma((7,)),
            *Gather.sems(count),
            *Scatter.scratch(count, rows, down, late_share(rows, share)),
        ],
        compiler_params=pltpu.CompilerParams(
            collective_id=2, has_side_effects=True, vmem_limit_bytes=61 << 20
        ),
    )(n2, cot, full_gates, pack_down)


def middle_kernel(count, *refs):
    (
        part_in, dn2_hbm, h_hbm, cot_hbm, w0_hbm, ctx_hbm, gain_ref,
        dh_out, dm_out, dwo_out, gates_ref, small_ref,
        partial, dn2_ref, h_ref, cot_ref, wo, ctx_ref, dh_ref, dm_ref, dwo_ref, dhb, copy_sems, *rest,
    ) = refs
    place = Place(count)
    seq, width = dn2_ref.shape
    q_cols = ctx_ref.shape[1]
    heads = q_cols // HALF
    group = heads // 2
    tile = seq // 4
    lanes = lane_ids()
    loads = [
        begin(src, dst, copy_sems.at[index])
        for index, (src, dst) in enumerate(
            (
                (part_in, partial), (dn2_hbm, dn2_ref), (h_hbm, h_ref), (cot_hbm, cot_ref),
                (w0_hbm.at[:, pl.ds(w0_hbm.shape[1] - q_cols, q_cols)], wo), (ctx_hbm, ctx_ref),
            )
        )
    ]
    place.greet(False, False)
    scatter = Scatter(place, partial, gates_ref, late_share(gates_ref.shape[0], 1 / 6), rest)
    loads[0].wait()
    scatter.start()
    sums = scatter.steps()
    g2 = gain_ref[pl.ds(1, 1), :]
    for load in loads[1:]:
        load.wait()
    small_ref[...] = jnp.zeros_like(small_ref)

    def residual_grad(index, carry):
        rows = pl.ds(pl.multiple_of(index * 64, 64), 64)
        grad = dn2_ref[rows, :].astype(F32)
        h = h_ref[rows, :]
        inverse = lax.rsqrt(jnp.mean(h * h, axis=1, keepdims=True) + EPSILON)
        scaled = grad * g2
        inner = jnp.mean(scaled * h, axis=1, keepdims=True)
        dh = cot_ref[rows, :].astype(F32) + inverse * scaled - h * (inverse * inverse * inverse * inner)
        dh_ref[rows, :] = dh
        dhb[rows, :] = dh.astype(BF16)
        return carry + jnp.sum((grad * h * inverse).reshape(8, 8, width), axis=0)

    def back(index):
        small_ref[...] += lax.fori_loop(
            index * (tile // 64), (index + 1) * (tile // 64), residual_grad, jnp.zeros((8, width), F32)
        )
        rows = pl.ds(pl.multiple_of(index * tile, tile), tile)
        dctx = dot_nn(dhb[rows, :], wo[...])
        for pair in range(heads // 2):
            value = dctx[:, pair * LANES : (pair + 1) * LANES]
            swapped = pltpu.roll(value, HALF, 1)
            for side in range(2):
                head = 2 * pair + side
                keep = value if side == head // group else swapped
                dm_ref[head, rows, :] = jnp.where(lanes // HALF == head // group, keep, 0.0).astype(BF16)

    polled(4, back, (sums, {1: 1, 2: 1, 3: 1}))
    saves = [begin(dh_ref, dh_out, copy_sems.at[6]), begin(dm_ref, dm_out, copy_sems.at[7])]

    def out_grad(index):
        rows = pl.ds(pl.multiple_of(index * 384, 384), 384)
        dwo_ref[rows, :] = dot_tn(dhb[:, rows], ctx_ref[...]).astype(BF16)

    polled(width // 384, out_grad, (sums, {1: 1, 3: 1}))
    saves.append(begin(dwo_ref, dwo_out, copy_sems.at[8]))
    drain(sums)
    for save in saves:
        save.wait()
    scatter.settle()


def middle_call(count, part, dn2, h, cot, w0, ctx, gains):
    seq, width = dn2.shape
    q_cols = ctx.shape[1]
    rows = width // count
    shape = jax.ShapeDtypeStruct
    dma = pltpu.SemaphoreType.DMA
    return pl.pallas_call(
        functools.partial(middle_kernel, count),
        out_shape=[
            shape((seq, width), F32),
            shape((q_cols // HALF, seq, LANES), BF16),
            shape((width, q_cols), BF16),
            shape((rows, part.shape[1]), F32),
            shape((8, width), F32),
        ],
        in_specs=[in_place()] * 6 + [whole_block()],
        out_specs=[in_place()] * 3 + [whole_block()] * 2,
        scratch_shapes=[
            pltpu.VMEM(part.shape, BF16),
            pltpu.VMEM((seq, width), BF16),
            pltpu.VMEM((seq, width), F32),
            pltpu.VMEM((seq, width), BF16),
            pltpu.VMEM((width, q_cols), BF16),
            pltpu.VMEM((seq, q_cols), BF16),
            pltpu.VMEM((seq, width), F32),
            pltpu.VMEM((q_cols // HALF, seq, LANES), BF16),
            pltpu.VMEM((width, q_cols), BF16),
            pltpu.VMEM((seq, width), BF16),
            dma((9,)),
            *Scatter.scratch(count, rows, part.shape[1], late_share(rows, 1 / 6)),
        ],
        compiler_params=pltpu.CompilerParams(
            collective_id=3, has_side_effects=True, vmem_limit_bytes=61 << 20
        ),
    )(part, dn2, h, cot, w0, ctx, gains)


def last_kernel(count, *refs):
    (
        part_in, dwo_in, dm_hbm, qm_hbm, kb_hbm, vb_hbm, lse_hbm, qk_hbm, n1_hbm, w0_hbm, x_hbm, dh_hbm,
        cos_ref, sin_ref, seg_col, seg_row, gain_ref, two_ref,
        grad_out, gates_ref, out_ref, qkv_ref, small_ref,
        partial, partial_o, dm_ref, qm_ref, kb_ref, vb_ref, lse_ref, qk_ref, n1_ref, wqkv, x_ref, dh_ref,
        partial_qkv, bias, dk, dv, dlow, part, dn1_ref, small, slots, head_slots,
        near, chip, far, sum_sems, small_send, small_recv, copy_sems, *rest,
    ) = refs
    place = Place(count)
    seq, width = n1_ref.shape
    kv_cols = kb_ref.shape[1]
    q_cols = qk_ref.shape[1] - kv_cols
    pairs = q_cols // LANES
    group = (q_cols // HALF) // (kv_cols // HALF)
    tile = seq // 4
    quarter = width // 4
    lanes = lane_ids()
    sources = (
        (part_in, partial), (dwo_in, partial_o), (qm_hbm, qm_ref), (kb_hbm, kb_ref), (lse_hbm, lse_ref),
        (dm_hbm, dm_ref), (vb_hbm, vb_ref), (qk_hbm, qk_ref),
        (w0_hbm.at[:, pl.ds(0, wqkv.shape[1])], wqkv), (n1_hbm, n1_ref), (x_hbm, x_ref), (dh_hbm, dh_ref),
    )
    loads = [begin(src, dst, copy_sems.at[index]) for index, (src, dst) in enumerate(sources)]
    place.greet(True, True)
    third = len(rest) // 3
    late = late_share(gates_ref.shape[0], 1 / 6)
    scatter = Scatter(place, partial, gates_ref, late, rest[:third])
    scatter_o = Scatter(place, partial_o, out_ref, late, rest[third : 2 * third])
    scatter_qkv = Scatter(place, partial_qkv, qkv_ref, late, rest[2 * third :])
    final = TensorSum(place, part, dn1_ref, 4, (near, chip, far, sum_sems))
    for load in loads[:2]:
        load.wait()
    scatter.start()
    sums, sums_o = scatter.steps(), scatter_o.steps()
    dk[...] = jnp.zeros_like(dk)
    dv[...] = jnp.zeros_like(dv)
    gq = gain_ref[pl.ds(2, 1), pl.ds(0, LANES)]
    gk = gain_ref[pl.ds(3, 1), pl.ds(0, LANES)]
    for load in loads[2:9]:
        load.wait()

    def head_back(grad, raw, cosine, sine, gain):
        back = turn(grad, cosine, -sine)
        inverse = lax.rsqrt(head_mean(raw * raw) + EPSILON)
        scaled = back * gain
        inner = head_mean(scaled * raw)
        low = inverse * scaled - raw * (inverse * inverse * inverse * inner)
        return low.astype(BF16), jnp.sum((back * raw * inverse).reshape(-1, 8, LANES), axis=0)

    gain_q = jnp.zeros((8, LANES), F32)
    gain_k = jnp.zeros((8, LANES), F32)
    for qb in reversed(range(4)):
        last = (qb + 1) * tile
        rows = pl.ds(qb * tile, tile)
        bias_block(seg_col, seg_row, bias, qb * tile, tile)

        def attend_back(pair, carry, last=last, rows=rows):
            keys = pl.ds(0, last)
            sides = []
            for side in range(2):
                head = 2 * pair + side
                kv = head // group
                query, grad = qm_ref[head, rows, :], dm_ref[head, rows, :]
                logsum = jnp.sum(jnp.where(lanes == head, lse_ref[rows, :], 0.0), axis=1, keepdims=True)
                logits = dot_nt(query, kb_ref[keys, :]) + bias[:, keys]
                probs = jnp.exp(logits - logsum)
                dprob = dot_nt(grad, vb_ref[keys, :])
                inner = jnp.sum(probs * dprob, axis=1, keepdims=True)
                ds = (probs * (dprob - inner)).astype(BF16)
                got = dot_nn(ds, kb_ref[keys, :]) * 0.125
                sides.append(jnp.where(kv == side, got, pltpu.roll(got, HALF, 1)))
                dk[keys, :] += dot_tn(ds, query)
                dv[keys, :] += dot_tn(probs.astype(BF16), grad)
            cols = pl.ds(pl.multiple_of(pair * LANES, LANES), LANES)
            low, terms = head_back(
                jnp.where(lanes < HALF, sides[0], sides[1]), qk_ref[rows, cols], cos_ref[rows, :], sin_ref[rows, :], gq
            )
            dlow[rows, cols] = low
            return carry + terms

        gain_q = lax.fori_loop(0, pairs, attend_back, gain_q)
        low, terms = head_back(
            dk[rows, :], qk_ref[rows, pl.ds(q_cols, LANES)], cos_ref[rows, :], sin_ref[rows, :], gk
        )
        dlow[rows, pl.ds(q_cols, LANES)] = low
        dlow[rows, pl.ds(q_cols + LANES, LANES)] = dv[rows, :].astype(BF16)
        gain_k = gain_k + terms
        part[rows, :] = dot_nt(dlow[rows, :], wqkv[...]).astype(BF16)
        final.send_core(qb)
        ahead(sums, 3)
        final.send_across(qb)
        if qb < 3:
            final.send_back(qb + 1)
        if qb == 1:
            scatter_o.start()
    mine = head_slots.at[place.tensor]
    mine[...] = jnp.concatenate([gain_q, gain_k], axis=0)
    head_copies = []
    for step in range(1, 4):
        copy = remote(
            mine, mine, small_send.at[step - 1], small_recv.at[step - 1], place.me, lax.rem(place.tensor + step, 4)
        )
        copy.start()
        head_copies.append(copy)
    for load in loads[9:]:
        load.wait()

    def qkv_grad(start):
        partial_qkv[pl.ds(start, 384), :] = dot_tn(n1_ref[:, pl.ds(start, 384)], dlow[...]).astype(BF16)

    blocks(width, 384, qkv_grad)
    scatter_qkv.start()
    sums_qkv = scatter_qkv.steps()
    for step, copy in enumerate(head_copies):
        whose = head_slots.at[lax.rem(place.tensor + 3 - step, 4)]
        remote(whose, whose, small_send.at[step], small_recv.at[step], place.me, place.tensor).wait_recv()
    heads = head_slots[0] + head_slots[1] + head_slots[2] + head_slots[3]
    ahead(sums_o, 2)
    g1 = gain_ref[pl.ds(0, 1), :]
    gain_one = jnp.zeros((8, width), F32)
    saves = []
    for index in reversed(range(4)):
        if index == 0:
            final.send_back(0)
        ahead(sums, 1)
        ahead(sums_o, 1)
        ahead(sums_qkv, 1)
        final.finish(index)

        def input_grad(sub, carry, index=index):
            rows = pl.ds(pl.multiple_of(index * tile + sub * 64, 64), 64)
            grad = dn1_ref[rows, :].astype(F32)
            x = x_ref[rows, :].astype(F32)
            inverse = lax.rsqrt(jnp.mean(x * x, axis=1, keepdims=True) + EPSILON)
            scaled = grad * g1
            inner = jnp.mean(scaled * x, axis=1, keepdims=True)
            dh_ref[rows, :] = dh_ref[rows, :] + inverse * scaled - x * (inverse * inverse * inverse * inner)
            return carry + jnp.sum((grad * x * inverse).reshape(8, 8, width), axis=0)

        gain_one = lax.fori_loop(0, tile // 64, input_grad, gain_one)
        rows = pl.ds(index * tile, tile)
        saves.append(begin(dh_ref.at[rows, :], grad_out.at[rows, :], copy_sems.at[index]))
    one = jnp.sum(gain_one, axis=0, keepdims=True)
    two = jnp.sum(two_ref[...], axis=0, keepdims=True)
    small[...] = jnp.zeros_like(small)
    for index in range(4):
        cols = slice(index * quarter, (index + 1) * quarter)
        small[pl.ds(index, 1), pl.ds(0, quarter)] = one[:, cols]
        small[pl.ds(4 + index, 1), pl.ds(0, quarter)] = two[:, cols]
    small[pl.ds(0, 1), pl.ds(quarter, LANES)] = jnp.sum(heads[:8], axis=0, keepdims=True)
    small[pl.ds(1, 1), pl.ds(quarter, LANES)] = jnp.sum(heads[8:], axis=0, keepdims=True)
    small_copies = []
    for step in range(1, count):
        copy = remote(
            small, slots.at[step], small_send.at[2 + step], small_recv.at[2 + step],
            lax.rem(place.me + step, count), place.tensor,
        )
        copy.start()
        small_copies.append(copy)
    drain(sums, sums_o, sums_qkv)
    total = small[...]
    for copy in small_copies:
        copy.wait_recv()
    for step in range(1, count):
        total = total + slots[step]
    small_ref[...] = total
    for save in saves:
        save.wait()
    for copy in head_copies + small_copies:
        copy.wait_send()
    for each in (scatter, scatter_o, scatter_qkv, final):
        each.settle()


def last_call(count, part, dwo, dm, qm, kb, vb, lse, qk, n1, w0, x, dh, cosine, sine, seg_col, seg_row, gains, two):
    seq, width = n1.shape
    rows = width // count
    q_cols = dwo.shape[1]
    low = qk.shape[1] + LANES
    shape = jax.ShapeDtypeStruct
    dma = pltpu.SemaphoreType.DMA
    loaded = [part, dwo, dm, qm, kb, vb, lse, qk, n1, jax.ShapeDtypeStruct((width, low), BF16), x, dh]
    small = (8, width // 4 + LANES)
    return pl.pallas_call(
        functools.partial(last_kernel, count),
        out_shape=[
            shape((seq, width), F32),
            shape((rows, part.shape[1]), F32),
            shape((rows, q_cols), F32),
            shape((rows, low), F32),
            shape(small, F32),
        ],
        in_specs=[in_place()] * 12 + [whole_block()] * 6,
        out_specs=[in_place()] + [whole_block()] * 4,
        scratch_shapes=[
            *[pltpu.VMEM(one.shape, one.dtype) for one in loaded],
            pltpu.VMEM((width, low), BF16),
            pltpu.VMEM((seq // 4, seq), F32),
            pltpu.VMEM((seq, LANES), F32),
            pltpu.VMEM((seq, LANES), F32),
            pltpu.VMEM((seq, low), BF16),
            pltpu.VMEM((seq, width), BF16),
            pltpu.VMEM((seq, width), BF16),
            pltpu.VMEM(small, F32),
            pltpu.VMEM((count,) + small, F32),
            pltpu.VMEM((4, 16, LANES), F32),
            *TensorSum.scratch(seq, width, 4, BF16),
            dma((count + 2,)),
            dma((count + 2,)),
            dma((12,)),
            *Scatter.scratch(count, rows, part.shape[1], late_share(rows, 1 / 6)),
            *Scatter.scratch(count, rows, q_cols, late_share(rows, 1 / 6)),
            *Scatter.scratch(count, rows, low, late_share(rows, 1 / 6)),
        ],
        compiler_params=pltpu.CompilerParams(
            collective_id=4, has_side_effects=True, vmem_limit_bytes=61 << 20
        ),
    )(part, dwo, dm, qm, kb, vb, lse, qk, n1, w0, x, dh, cosine, sine, seg_col, seg_row, gains, two)


def rotation_tables(positions, head_dim):
    half_dim = head_dim // 2
    frequency = ROPE_BASE ** (-jnp.arange(half_dim, dtype=jnp.float32) * 2.0 / head_dim)
    angles = positions.astype(jnp.float32)[:, None] * frequency[None, :]
    return (jnp.cos(angles)[:, None, :], jnp.sin(angles)[:, None, :])


def lay(gate, up):
    rows, cols = gate.shape
    even = cols // LANES * LANES
    pairs = jnp.stack(
        [gate[:, :even].reshape(rows, -1, LANES), up[:, :even].reshape(rows, -1, LANES)], axis=2
    ).reshape(rows, 2 * even)
    return jnp.concatenate([pairs, gate[:, even:], up[:, even:]], axis=1)


def unlay(both):
    rows, cols = both.shape
    even = cols // 2 // LANES * LANES
    pairs = both[:, : 2 * even].reshape(rows, -1, 2, LANES)
    rest = both[:, 2 * even :]
    size = rest.shape[1] // 2
    return (
        jnp.concatenate([pairs[:, :, 0].reshape(rows, even), rest[:, :size]], axis=1),
        jnp.concatenate([pairs[:, :, 1].reshape(rows, even), rest[:, size:]], axis=1),
    )


def spread(gain, me, width):
    full = jnp.zeros((width,), F32)
    return lax.dynamic_update_slice(full, lax.reduce_precision(gain, 8, 7), (me * gain.shape[0],))


def gain_rows(norm1_gain, norm2_gain, q_gain, k_gain, count):
    me = lax.axis_index("dp")
    width = norm1_gain.shape[0] * count
    head = q_gain.shape[0] * count
    rows = [spread(norm1_gain, me, width), spread(norm2_gain, me, width)]
    for gain in (q_gain, k_gain):
        one = spread(gain, me, head)
        rows.append(jnp.pad(jnp.concatenate([one, one]), (0, width - 2 * head)))
    return jnp.pad(jnp.stack(rows), ((0, 4), (0, 0)))


def rotation_lanes(positions):
    cosine, sine = rotation_tables(positions, HALF)
    cosine, sine = cosine[:, 0], sine[:, 0]
    return (
        jnp.concatenate([cosine] * 4, axis=1),
        jnp.concatenate([-sine, sine, -sine, sine], axis=1),
    )


def shards(
    block_input,
    segments,
    positions,
    norm1_gain,
    q_norm_gain,
    k_norm_gain,
    w_q,
    w_k,
    w_v,
    w_o,
    norm2_gain,
    w_gate,
    w_up,
    w_down,
    cotangent,
    *,
    n_dp,
    n_tensor,
):
    rows = w_q.shape[0]
    q_cols, kv_cols, ff_cols = w_q.shape[1], w_k.shape[1], w_gate.shape[1]
    small_gain = q_norm_gain.shape[0]
    head_dim = small_gain * n_dp
    seg_col, seg_row = segments[:, None], segments[None, :]
    gains = gain_rows(norm1_gain, norm2_gain, q_norm_gain, k_norm_gain, n_dp)
    pack_attn = jnp.concatenate(
        [w_q.astype(BF16), w_k.astype(BF16), w_v.astype(BF16), w_o.T.astype(BF16)], axis=1
    )
    pack_gates = lay(w_gate.astype(BF16), w_up.astype(BF16))
    pack_down = jnp.pad(w_down.T.astype(BF16), ((0, 0), (0, -ff_cols % LANES)))
    cosine, sine = rotation_lanes(positions)
    w0, w1, n1, qk, qm, kb, vb, lse, ctx, h, n2, gains = forward_call(
        n_dp, block_input, seg_col, seg_row, cosine, sine, gains, pack_attn, pack_gates
    )
    first, second, dn2, mlp, down = mlp_call(n_dp, n2, cotangent, w1, pack_down)
    mlp_total = lax.psum(mlp, "tensor")
    dh, dm, dwo, gates_one, small_two = middle_call(n_dp, first, dn2, h, cotangent, w0, ctx, gains)
    grad_input, gates_two, grad_o, grad_qkv, small = last_call(
        n_dp, second, dwo, dm, qm, kb, vb, lse, qk, n1, w0, block_input, dh,
        cosine, sine, seg_col, seg_row, gains, small_two,
    )
    output_rows = (h + mlp_total.astype(F32)).astype(BF16)
    me = lax.axis_index("dp")
    quarter = block_input.shape[1] // 4
    one, two = small[:4, :quarter].reshape(-1), small[4:, :quarter].reshape(-1)
    heads = small[:2, quarter:].reshape(2, 2, head_dim).sum(axis=1)

    def own(values, size):
        return lax.dynamic_slice_in_dim(values, me * size, size, 0)

    grad_gate, grad_up = unlay(jnp.concatenate([gates_one, gates_two], axis=1))
    return (
        output_rows,
        grad_input,
        own(one, rows),
        own(heads[0], small_gain),
        own(heads[1], small_gain),
        grad_qkv[:, :q_cols],
        grad_qkv[:, q_cols : q_cols + kv_cols],
        grad_qkv[:, q_cols + kv_cols :],
        grad_o.T,
        own(two, rows),
        grad_gate,
        grad_up,
        down[:, :ff_cols].T,
    )


def solution(mesh):
    placed = (
        P("dp", None),
        P("dp"),
        P("dp"),
        P("dp"),
        P("dp"),
        P("dp"),
        P("dp", "tensor"),
        P("dp", "tensor"),
        P("dp", "tensor"),
        P("tensor", "dp"),
        P("dp"),
        P("dp", "tensor"),
        P("dp", "tensor"),
        P("tensor", "dp"),
        P("dp", None),
    )
    return jax.shard_map(
        functools.partial(shards, n_dp=mesh.shape["dp"], n_tensor=mesh.shape["tensor"]),
        mesh=mesh,
        in_specs=placed,
        out_specs=(
            P("dp", None),
            P("dp", None),
            P("dp"),
            P("dp"),
            P("dp"),
            P("dp", "tensor"),
            P("dp", "tensor"),
            P("dp", "tensor"),
            P("tensor", "dp"),
            P("dp"),
            P("dp", "tensor"),
            P("dp", "tensor"),
            P("tensor", "dp"),
        ),
        check_vma=False,
    )
```

time: 670 us -> 554 us (0.83)
  Pallas kernels: 560 us -> 471 us
  blocking collectives: 39.4 us -> 0 us
  between operations: 1.49 us -> 14.5 us
  local copies, waits for them, and re-layouts: 28.8 us -> 40 us
    pallas_call x3, Pallas kernels: 477 us -> 405 us  [the longest x1 161 us: forward_call(): pl.pallas_call(functools.partial(forward_kernel, count), out_shape=[jax.S...]
    psum x1 -> x0, blocking collectives: 39.4 us -> none  [shards(): lax.psum(jnp.concatenate([grad_gain_one * share, small_two.sum(axis=0) *...]
    pallas_call x1, Pallas kernels: 83.7 us -> 65.4 us  [middle_call(): pl.pallas_call(functools.partial(middle_kernel, count), out_shape=[shape(...]
    unnamed x35 -> x42, local copies, waits for them, and re-layouts: 2.62 us -> 11.5 us
  transfers between devices with their start and end apart: 0 -> 1, of which waited for: 0 -> 0; matrix products, arithmetic and copies ran while one was open for 0% -> 5% of each run, Pallas kernels for 0% -> 33%
where the time goes in v3:
time: 554 us; the launch traced here: 550 us
  Pallas kernels  471 us (85%)
  local copies, waits for them, and re-layouts  40 us (7%)
  other arithmetic  24.6 us (4%)
  between operations  14.5 us (3%)
    pallas_call x1, Pallas kernels, forward_call(): pl.pallas_call(functools.partial(forward_kernel, count), out_shape=[jax.S...  161 us
    pallas_call x1, Pallas kernels, mlp_call(): pl.pallas_call(functools.partial(mlp_kernel, count, share), out_shape=[sh...  128 us
    pallas_call x1, Pallas kernels, last_call(): pl.pallas_call(functools.partial(last_kernel, count), out_shape=[shape((s...  116 us
    pallas_call x1, Pallas kernels, middle_call(): pl.pallas_call(functools.partial(middle_kernel, count), out_shape=[shape(...  65.4 us
    unnamed x42, local copies, waits for them, and re-layouts  11.5 us
  transfers between devices with their start and end apart: 1, of which 0 were waited for; matrix products, arithmetic and copies ran while one was open for 5% of the time, Pallas kernels for 33%

profile of v3, /device:TPU:0, one launch (start us, length us, event | category | flops | bytes accessed | tf_op | source)
XLA Modules:
  0.0 549.8 jit_solution(15268038115869536513)
XLA Ops:
  7.8 1.5 convert_element_type.49
  10.2 0.8 copy-done.2
  14.3 2.0 copy.33
  16.3 0.7 reshape.54
  17.1 1.0 copy.34.refs_1_.refs_14_
  18.1 1.0 convert_bitcast_fusion.1
  19.1 1.6 convert_element_type.44
  20.8 0.9 convert_element_type.45
  22.4 0.8 dynamic_update_slice.14
  23.4 2.6 fusion
  25.9 0.9 pad.18.refs_3_
  26.9 1.8 pad_maximum_fusion.4
  28.7 1.8 concatenate.32.refs_7_
  31.1 0.8 pad_maximum_fusion.6.refs_6_
  31.9 161.3 %shard_map.246 = (bf16[1536,1024]{1,0:T(8,128)(2,1)}, bf16[1536,3456]{1,0:T(8,128)(2,1)}, bf16[1024,1536]{1,0:T(8,128)(2,1)}, f32[1024,512]{1,0:T(8,128)}, bf16[...) custom-call(bf16[1024,1536]{1,0:T(8,128)(2,1)} %refs_10_.1, ...), custom_call_target="tpu_custom_call" | custom-call | tf_op jit(solution)/shard_map/pallas_call | solution.py:541
  193.2 128.2 %shard_map.247 = (bf16[1536,1792]{1,0:T(8,128)(2,1)}, bf16[1536,1664]{1,0:T(8,128)(2,1)}, bf16[1024,1536]{1,0:T(8,128)(2,1)}, bf16[1024,1536]{1,0:T(8,128)(2,1)}, f32[192,1792]{1,0:T(8,128)}) custom-call(bf16[1024,1536]{1,0:T(8,128)(2,1)} %get-tuple-element.41.refs_0_, bf16[1024,1536]{1,0:T(8,128)(2,1)} %refs_3_.1, ...), custom_call_target="tpu_custom_call" | custom-call | tf_op jit(solution)/shard_map/pallas_call | solution.py:872
  321.5 65.4 %shard_map.248 = (f32[1024,1536]{1,0:T(8,128)}, bf16[6,1024,128]{2,1,0:T(8,128)(2,1)}, bf16[1536,384]{1,0:T(8,128)(2,1)}, f32[192,1792]{1,0:T(8,128)}, f32[8,1536]{1,0:T(8,128)}) custom-call(bf16[1536,1792]{1,0:T(8,128)(2,1)} %get-tuple-element.45.refs_0_, bf16[1024,1536]{1,0:T(8,128)(2,1)} %get-tuple-element.46.refs_1_, ...), custom_call_target="tpu_custom_call" | custom-call | tf_op jit(solution)/shard_map/pallas_call | solution.py:980
  386.9 115.7 %shard_map.249 = (f32[1024,1536]{1,0:T(8,128)}, f32[192,1664]{1,0:T(8,128)}, f32[192,384]{1,0:T(8,128)}, f32[192,640]{1,0:T(8,128)}, f32[8,512]{1,0:T(8,128)}) custom-call(bf16[1536,1664]{1,0:T(8,128)(2,1)} %get-tuple-element.44.refs_0_, bf16[1536,384]{1,0:T(8,128)(2,1)} %get-tuple-element.50.refs_1_, bf16[6,1024,128]{2,1,0:T(8,128)(2,1)} %get-tuple-element.51.refs_2_, ...), custom_call_target="tpu_custom_call" | custom-call | tf_op jit(solution)/shard_map/pallas_call | solution.py:1195
  502.6 0.8 fusion.3
  504.0 1.9 pad_maximum_fusion
  505.9 2.4 reshape.58
  508.3 9.5 %slice_reduce_fusion = (f32[192,13,128]{2,1,0:T(8,128)S(1)}, f32[192,13,128]{2,1,0:T(8,128)S(1)}) fusion(f32[192,13,2,128]{3,2,1,0:T(2,128)} %reshape.58), kind=kLoop, calls=%fused_computation.8 | loop fusion | bytes 5111808 | tf_op jit(solution)/shard_map/slice | solution.py:1256
  519.1 1.5 copy.40
  521.7 0.7 slice.65
  523.7 1.1 fusion.1
  524.7 0.7 fusion.2
  525.4 1.2 pad_maximum_fusion.3
  526.6 1.2 pad_maximum_fusion.2
  528.4 1.2 slice_bitcast_fusion
  529.6 6.4 %add_convert_fusion = bf16[1024,1536]{1,0:T(8,128)(2,1)} fusion(f32[1024,1536]{1,0:T(8,128)} %get-tuple-element.40.refs_2_, bf16[1024,1536]{1,0:T(8,128)(2,1)} %all-reduce.6.cloned.1.call-done), kind=kLoop, calls=%fused_computation | loop fusion | flops 4718592 | bytes 12582912 | tf_op jit(solution)/shard_map/convert_element_type | solution.py:1327
  536.0 6.0 %copy.50 = f32[1024,1536]{1,0:T(8,128)} copy(f32[1024,1536]{1,0:T(8,128)} %get-tuple-element.96) | data formatting | bytes 12582912
  542.0 0.7 copy.51
  (79 shorter events, 11.3 us)
Async XLA Ops:
  7.2 522.4 %all-reduce.6.cloned.1.call-start = ((), (), s32[]{:S(2)}) async-start(), calls=%async_computation | async-start | bytes 6291456 | tf_op jit(solution)/shard_map/psum | solution.py:1321
  7.8 1.8 copy-start.4
  9.3 0.8 copy-start.1
  9.5 1.5 copy-start.17
  9.5 1.6 copy-start.18
  9.5 2.4 copy-start.15
  9.5 3.0 copy-start.16
  9.5 3.6 copy-start.14
  10.1 0.8 copy-start.2
  16.3 0.8 copy-start.11
  17.1 4.6 copy-start.10
  17.1 5.2 copy-start.5
  18.1 5.1 copy-start.13
  26.8 1.8 slice-start
  26.9 1.8 slice-start.1
  28.7 1.8 copy-start.12
  28.7 2.5 copy-start.6
  28.7 2.4 copy-start.9
  520.6 1.0 copy-start.7
  521.1 4.3 copy-start
  526.6 1.8 copy-start.3
  536.0 6.0 %copy-start.8 = (f32[192,384]{1,0:T(8,128)S(1)}, f32[192,384]{1,0:T(8,128)}, u32[]{:S(2)}) copy-start(f32[192,384]{1,0:T(8,128)} %get-tuple-element.63) | copy-start | bytes 884740
Sparse Core Ops, SparseCore 0:
  321.6 72.7 all-reduce.5

commit v4 on v3

--- a/solution.py
+++ b/solution.py
@@ -2,6 +2,7 @@
 
 import jax
 import jax.numpy as jnp
+import numpy as np
 from jax import lax
 from jax.experimental import pallas as pl
 from jax.experimental.pallas import tpu as pltpu
@@ -370,10 +371,10 @@
 
 def forward_kernel(count, *refs):
     (
-        x_hbm, seg_col, seg_row, cos_ref, sin_ref, gain_ref, pack_attn, pack_gates,
+        x_hbm, gate_hbm, up_hbm, seg_col, seg_row, cos_ref, sin_ref, gain_ref, wq_ref, wk_ref, wv_ref, wot_ref,
         full_attn, full_gates, n1_out, qk_out, qm_out, kb_out, vb_out, lse_out, ctx_out, h_out, n2_out, gains_out,
         x_ref, w0, n1_ref, qk_ref, qm_ref, kb_ref, vb_ref, lse_ref, ctx_ref, h_ref, n2_ref,
-        bias, gain_slots, part, total, tmp_near, tmp_chip, tmp_far, sum_sems, gain_send, gain_recv, copy_sems,
+        pack_attn, pack_gates, gate_ref, up_ref, bias, gain_slots, part, total, tmp_near, tmp_chip, tmp_far, sum_sems, gain_send, gain_recv, copy_sems,
         *gather_sems,
     ) = refs
     place = Place(count)
@@ -384,26 +385,55 @@
     group = (q_cols // HALF) // (kv_cols // HALF)
     tile = seq // 4
     load = begin(x_hbm, x_ref, copy_sems.at[0])
+    weights = [begin(gate_hbm, gate_ref, copy_sems.at[11]), begin(up_hbm, up_ref, copy_sems.at[12])]
+    spot = 0
+    for ref in (wq_ref, wk_ref, wv_ref, wot_ref):
+        pack_attn[:, pl.ds(spot, ref.shape[1])] = ref[...].astype(BF16)
+        spot += ref.shape[1]
+    gain_slots[place.me] = gain_ref[...].astype(BF16).astype(F32)
     place.greet(True, True)
     first = Gather(place, pack_attn, w0, late_share(pack_attn.shape[0], 1 / 6), gather_sems[:5])
     second = Gather(place, pack_gates, full_gates, late_share(pack_gates.shape[0], 1 / 6), gather_sems[5:])
+    first.start()
     gain_copies = []
     for step in range(1, count):
         copy = remote(
-            gain_ref, gain_slots.at[step], gain_send.at[step], gain_recv.at[step],
+            gain_slots.at[place.me], gain_slots.at[place.me], gain_send.at[step], gain_recv.at[step],
             lax.rem(place.me + step, count), place.tensor,
         )
         copy.start()
         gain_copies.append(copy)
-    first.start()
+    for weight in weights:
+        weight.wait()
+    even = gate_ref.shape[1] // LANES
+
+    def lay(index, carry):
+        cols = pl.ds(pl.multiple_of(index * LANES, LANES), LANES)
+        for side, ref in enumerate((gate_ref, up_ref)):
+            spot = pl.multiple_of((2 * index + side) * LANES, LANES)
+            pack_gates[:, pl.ds(spot, LANES)] = ref[:, cols].astype(BF16)
+        return carry
+
+    lax.fori_loop(0, even, lay, 0)
+    rest = pl.ds(even * LANES, HALF)
+    pack_gates[:, pl.ds(2 * even * LANES, LANES)] = jnp.concatenate(
+        [gate_ref[:, rest], up_ref[:, rest]], axis=1
+    ).astype(BF16)
     for qb in range(4):
         bias_block(seg_col, seg_row, bias.at[qb], qb * tile, tile)
-    gains = gain_ref[...]
-    for copy in gain_copies:
-        copy.wait_recv()
     for step in range(1, count):
-        gains = gains + gain_slots[step]
-    gains_out[...] = gains
+        whose = gain_slots.at[lax.rem(place.me + count - step, count)]
+        remote(whose, whose, gain_send.at[step], gain_recv.at[step], place.me, place.tensor).wait_recv()
+    gains_out[...] = jnp.zeros_like(gains_out)
+    own = width // count
+    for row in range(2):
+        gains_out[pl.ds(row, 1), :] = jnp.concatenate(
+            [gain_slots[d, pl.ds(row, 1), pl.ds(0, own)] for d in range(count)], axis=1
+        )
+    for row in range(2, 4):
+        gains_out[pl.ds(row, 1), pl.ds(0, LANES)] = jnp.concatenate(
+            [gain_slots[d, pl.ds(row, 1), pl.ds(0, HALF // count)] for d in range(count)] * 2, axis=1
+        )
     moves_first = first.steps()
     ahead(moves_first, 2)
     g1 = gains_out[pl.ds(0, 1), :]
@@ -520,10 +550,11 @@
     summed.settle()
 
 
-def forward_call(count, x, seg_col, seg_row, cosine, sine, gains, pack_attn, pack_gates):
+def forward_call(count, x, gate, up, seg_col, seg_row, cosine, sine, gains, wq, wk, wv, wot):
     seq, width = x.shape
-    rows = pack_attn.shape[0]
-    q_cols, kv_cols = 384, LANES
+    rows = wq.shape[0]
+    q_cols, kv_cols = wq.shape[1], LANES
+    attn_cols = wq.shape[1] + wk.shape[1] + wv.shape[1] + wot.shape[1]
     kept = [
         ((seq, width), BF16),
         ((seq, q_cols + kv_cols), F32),
@@ -535,18 +566,22 @@
         ((seq, width), F32),
         ((seq, width), BF16),
     ]
-    attn = ((count * rows, pack_attn.shape[1]), BF16)
-    outs = [attn, ((count * rows, pack_gates.shape[1]), BF16), *kept, (gains.shape, F32)]
+    attn = ((count * rows, attn_cols), BF16)
+    outs = [attn, ((count * rows, 2 * gate.shape[1]), BF16), *kept, ((8, width), F32)]
     dma = pltpu.SemaphoreType.DMA
     return pl.pallas_call(
         functools.partial(forward_kernel, count),
         out_shape=[jax.ShapeDtypeStruct(*out) for out in outs],
-        in_specs=[in_place()] + [whole_block()] * 5 + [in_place()] * 2,
+        in_specs=[in_place()] * 3 + [whole_block()] * 9,
         out_specs=[in_place()] * 11 + [whole_block()],
         scratch_shapes=[
             pltpu.VMEM((seq, width), BF16),
             pltpu.VMEM(*attn),
             *[pltpu.VMEM(*one) for one in kept],
+            pltpu.VMEM((rows, attn_cols), BF16),
+            pltpu.VMEM((rows, 2 * gate.shape[1]), BF16),
+            pltpu.VMEM(gate.shape, F32),
+            pltpu.VMEM(up.shape, F32),
             pltpu.VMEM((4, seq // 4, seq), F32),
             pltpu.VMEM((count,) + gains.shape, F32),
             pltpu.VMEM((seq, width), F32),
@@ -554,19 +589,37 @@
             *TensorSum.scratch(seq, width, 4, F32),
             dma((count,)),
             dma((count,)),
-            dma((11,)),
+            dma((13,)),
             *Gather.sems(count),
             *Gather.sems(count),
         ],
         compiler_params=pltpu.CompilerParams(
             collective_id=1, has_side_effects=True, vmem_limit_bytes=61 << 20
         ),
-    )(x, seg_col, seg_row, cosine, sine, gains, pack_attn, pack_gates)
+    )(x, gate, up, seg_col, seg_row, cosine, sine, gains, wq, wk, wv, wot)
+
+
+def store(ref, rows, value):
+    ref[rows, :] = value
+
+
+def store_apart(gate, up, rows, value):
+    even = gate.shape[1] // LANES
+    for index in range(even):
+        cols = pl.ds(index * LANES, LANES)
+        gate[rows, cols] = value[:, 2 * index * LANES : (2 * index + 1) * LANES]
+        up[rows, cols] = value[:, (2 * index + 1) * LANES : (2 * index + 2) * LANES]
+    if gate.shape[1] % LANES:
+        rest = value[:, 2 * even * LANES :]
+        cols = pl.ds(even * LANES, HALF)
+        gate[rows, cols] = rest[:, :HALF]
+        up[rows, cols] = pltpu.roll(rest, HALF, 1)[:, :HALF]
 
 
 class Scatter:
     def __init__(self, place, partial, result, late, scratch):
-        self.place, self.partial, self.result = place, partial, result
+        self.place, self.partial = place, partial
+        self.put = result if callable(result) else functools.partial(store, result)
         self.rows = partial.shape[0] // place.count
         self.late = late
         early = self.rows - late
@@ -625,8 +678,18 @@
             self.sent.append(lambda: self.over(number))
 
     def start(self):
+        self.start_far()
+        self.start_near()
+
+    def start_near(self):
         for number in range(len(self.cuts)):
             self.cross(number)
+
+    def start_far(self):
+        if self.late:
+            for index in range(self.place.depth - 1):
+                for item in (2, 3):
+                    pl.when(jnp.logical_not(self.fed(index)))(lambda index=index, item=item: self.hop(index, item).start())
 
     def add(self, spot, sources):
         size = sources[0].shape[0]
@@ -676,25 +739,26 @@
         start, size = self.cuts[cut]
         return self.over_in.at[index, pl.ds(start, size), :]
 
-    def pass_on(self, index, item):
-        place = self.place
-        goal = self.goals[index]
-        up = goal > place.far
-        fed = (up & (place.far > 0)) | (jnp.logical_not(up) & (place.far < place.depth - 1))
-        spot = self.spot(goal, *self.item(item))
-        base = [self.arrived(index, item)] if item < 2 else []
-
-        @pl.when(fed)
-        def _():
-            self.add(spot, base + [self.wait_far(goal, item)])
-
-        if base:
-
-            @pl.when(jnp.logical_not(fed))
-            def _():
-                self.add(spot, base)
-
+    def fed(self, index):
+        place = self.place
+        up = self.goals[index] > place.far
+        return (up & (place.far > 0)) | (jnp.logical_not(up) & (place.far < place.depth - 1))
+
+    def pass_on(self, index, item, base):
+        self.add(self.spot(self.goals[index], *self.item(item)), base)
         self.hop(index, item).start()
+
+    def first(self, number):
+        index, cut = self.pieces[number]
+        came = self.arrived(index, cut)
+        if index < self.place.depth - 1:
+            pl.when(jnp.logical_not(self.fed(index)))(lambda: self.pass_on(index, cut, [came]))
+
+    def then(self, index, item):
+        base = [self.over_in.at[index, pl.ds(*self.cuts[item]), :]] if item < 2 else []
+        pl.when(self.fed(index))(
+            lambda: self.pass_on(index, item, base + [self.wait_far(self.goals[index], item)])
+        )
         self.sent.append(lambda: self.hop(index, item))
 
     def close(self, item):
@@ -713,33 +777,44 @@
             self.lsend, self.lrecv, place.beside, place.tensor,
         )
 
-    def steps(self):
-        place = self.place
-        for index in range(place.depth - 1):
-            if self.late:
-                self.pass_on(index, 2)
-                self.pass_on(index, 3)
-                yield
-            for cut in range(len(self.cuts)):
-                self.pass_on(index, cut)
-                yield
-        if self.late:
-            self.close(3)
-            self.last().start()
-            self.sent.append(self.last)
-            self.close(2)
+    def far_steps(self):
+        for index in range(self.place.depth - 1 if self.late else 0):
+            for item in (2, 3):
+                self.then(index, item)
             yield
-        for cut, (start, size) in enumerate(self.cuts):
-            own = self.spot(place.far, 0, start, size)
-            self.add(own, [self.arrived(place.depth - 1, cut)])
-            self.close(cut)
-            self.result[pl.ds(start, size), :] = self.partial[own, :].astype(F32)
+
+    def steps(self, far=True):
+        place = self.place
+        cuts = len(self.cuts)
+        passing = cuts * (place.depth - 1)
+        for number in range(len(self.pieces) + cuts):
+            if number < len(self.pieces):
+                self.first(number)
+            index = (number - 1) // cuts
+            if far and self.late and number and (number - 1) % cuts == 0 and index < place.depth - 1:
+                self.then(index, 2)
+                self.then(index, 3)
+            if cuts <= number < passing + cuts:
+                self.then(*self.pieces[number - cuts])
+            if number == len(self.pieces) - 1 and self.late:
+                self.close(3)
+                self.last().start()
+                self.sent.append(self.last)
+                self.close(2)
+            if number >= passing + cuts:
+                cut = number - passing - cuts
+                start, size = self.cuts[cut]
+                own = self.spot(place.far, 0, start, size)
+                self.add(own, [self.over_in.at[place.depth - 1, pl.ds(start, size), :]])
+                self.close(cut)
+                self.put(pl.ds(start, size), self.partial[own, :].astype(F32))
             yield
         if self.late:
             start, size = self.tail
             self.last().wait_recv()
-            self.result[pl.ds(start, size), :] = (
-                self.partial[self.spot(place.far, 0, start, size), :].astype(F32) + self.late_in[...].astype(F32)
+            self.put(
+                pl.ds(start, size),
+                self.partial[self.spot(place.far, 0, start, size), :].astype(F32) + self.late_in[...].astype(F32),
             )
             yield
 
@@ -748,7 +823,7 @@
             make().wait_send()
 
 
-def mlp_kernel(count, share, *refs):
+def mlp_kernel(count, shares, *refs):
     (
         n2_hbm, cot_hbm, gates_hbm, pack_down,
         first_out, second_out, dn2_out, part_out, down_ref,
@@ -766,12 +841,11 @@
         for index, (src, dst) in enumerate(((n2_hbm, n2_ref), (gates_hbm, w1), (cot_hbm, cot_ref)))
     ]
     place.greet(False, True)
-    late = late_share(pack_down.shape[0], share)
-    gather = Gather(place, pack_down, w2, late, rest[:5])
-    scatter = Scatter(place, partial, down_ref, late, rest[5:])
+    gather = Gather(place, pack_down, w2, shares[0], rest[:5])
+    scatter = Scatter(place, partial, down_ref, shares[1], rest[5:])
     summed = TensorSum(place, dn2_part, dn2_ref, 4, (near, chip, far, sum_sems))
     gather.start()
-    moves, sums, tensor = gather.steps(), scatter.steps(), summed.steps()
+    moves, sums, tensor = gather.steps(), scatter.steps(False), summed.steps()
     loads[0].wait()
     loads[1].wait()
 
@@ -801,10 +875,11 @@
         partial[rows, :] = dot_tn(cot_ref[:, rows], hid[...]).astype(BF16)
 
     polled(width // 384, down_grad, (moves, {1: 1, 3: 1}))
-    scatter.start()
+    scatter.start_far()
     drain(moves)
-    ahead(sums, 3)
+    drain(scatter.far_steps())
     gather.finish()
+    scatter.start_near()
 
     def inner_grad(index):
         got = dot_nn(cot_ref[...], w2[:, pl.ds(pl.multiple_of(index * 2 * LANES, 2 * LANES), 2 * LANES)])
@@ -813,7 +888,7 @@
             cols = pl.ds(pl.multiple_of(index * 4 * LANES + side * 2 * LANES, 2 * LANES), 2 * LANES)
             ab[:, cols] = (ab[:, cols].astype(F32) * jnp.concatenate([piece, piece], axis=1)).astype(BF16)
 
-    polled(even // 2, inner_grad, (sums, {2: 1, 5: 1}))
+    polled(even // 2, inner_grad, (sums, {5: 1}))
     got = dot_nn(cot_ref[...], w2[:, pl.ds((even - 1) * LANES, 2 * LANES)])
     piece = got[:, :LANES]
     cols = pl.ds(2 * (even - 1) * LANES, 2 * LANES)
@@ -830,8 +905,8 @@
             @pl.when(index == at)
             def _(at=at):
                 summed.send_core(at)
+                ahead(sums, 1)
                 if at:
-                    ahead(sums, 1)
                     ahead(tensor, 1)
 
     lax.fori_loop(0, 4, lambda index, carry: (normed_grad(index), carry)[1], 0)
@@ -862,15 +937,16 @@
     summed.settle()
 
 
-def mlp_call(count, n2, cot, full_gates, pack_down, share=1 / 6):
+def mlp_call(count, n2, cot, full_gates, pack_down):
     seq, width = n2.shape
     rows, down = pack_down.shape
+    shares = late_share(rows, 1 / 6), late_share(rows, 1 / 4)
     both = full_gates.shape[1]
     split = 14 * LANES
     shape = jax.ShapeDtypeStruct
     dma = pltpu.SemaphoreType.DMA
     return pl.pallas_call(
-        functools.partial(mlp_kernel, count, share),
+        functools.partial(mlp_kernel, count, shares),
         out_shape=[
             shape((width, split), BF16),
             shape((width, both - split), BF16),
@@ -890,7 +966,7 @@
             *TensorSum.scratch(seq, width, 4, BF16),
             dma((7,)),
             *Gather.sems(count),
-            *Scatter.scratch(count, rows, down, late_share(rows, share)),
+            *Scatter.scratch(count, rows, down, shares[1]),
         ],
         compiler_params=pltpu.CompilerParams(
             collective_id=2, has_side_effects=True, vmem_limit_bytes=61 << 20
@@ -901,7 +977,7 @@
 def middle_kernel(count, *refs):
     (
         part_in, dn2_hbm, h_hbm, cot_hbm, w0_hbm, ctx_hbm, gain_ref,
-        dh_out, dm_out, dwo_out, gates_ref, small_ref,
+        dh_out, dm_out, dwo_out, gate_ref, up_ref, small_ref,
         partial, dn2_ref, h_ref, cot_ref, wo, ctx_ref, dh_ref, dm_ref, dwo_ref, dhb, copy_sems, *rest,
     ) = refs
     place = Place(count)
@@ -921,7 +997,8 @@
         )
     ]
     place.greet(False, False)
-    scatter = Scatter(place, partial, gates_ref, late_share(gates_ref.shape[0], 1 / 6), rest)
+    put = functools.partial(store_apart, gate_ref, up_ref)
+    scatter = Scatter(place, partial, put, late_share(gate_ref.shape[0], 1 / 6), rest)
     loads[0].wait()
     scatter.start()
     sums = scatter.steps()
@@ -983,11 +1060,12 @@
             shape((seq, width), F32),
             shape((q_cols // HALF, seq, LANES), BF16),
             shape((width, q_cols), BF16),
-            shape((rows, part.shape[1]), F32),
+            shape((rows, part.shape[1] // 2), F32),
+            shape((rows, part.shape[1] // 2), F32),
             shape((8, width), F32),
         ],
         in_specs=[in_place()] * 6 + [whole_block()],
-        out_specs=[in_place()] * 3 + [whole_block()] * 2,
+        out_specs=[in_place()] * 3 + [whole_block()] * 3,
         scratch_shapes=[
             pltpu.VMEM(part.shape, BF16),
             pltpu.VMEM((seq, width), BF16),
@@ -1012,9 +1090,9 @@
     (
         part_in, dwo_in, dm_hbm, qm_hbm, kb_hbm, vb_hbm, lse_hbm, qk_hbm, n1_hbm, w0_hbm, x_hbm, dh_hbm,
         cos_ref, sin_ref, seg_col, seg_row, gain_ref, two_ref,
-        grad_out, gates_ref, out_ref, qkv_ref, small_ref,
+        grad_out, gate_ref, up_ref, out_ref, qkv_ref, small_ref,
         partial, partial_o, dm_ref, qm_ref, kb_ref, vb_ref, lse_ref, qk_ref, n1_ref, wqkv, x_ref, dh_ref,
-        partial_qkv, bias, dk, dv, dlow, part, dn1_ref, small, slots, head_slots,
+        partial_qkv, bias, dk, dv, head_sums, dlow, part, dn1_ref, small, slots, head_slots,
         near, chip, far, sum_sems, small_send, small_recv, copy_sems, *rest,
     ) = refs
     place = Place(count)
@@ -1024,7 +1102,8 @@
     pairs = q_cols // LANES
     group = (q_cols // HALF) // (kv_cols // HALF)
     tile = seq // 4
-    quarter = width // 4
+    own = width // count
+    few = HALF // count
     lanes = lane_ids()
     sources = (
         (part_in, partial), (dwo_in, partial_o), (qm_hbm, qm_ref), (kb_hbm, kb_ref), (lse_hbm, lse_ref),
@@ -1034,8 +1113,8 @@
     loads = [begin(src, dst, copy_sems.at[index]) for index, (src, dst) in enumerate(sources)]
     place.greet(True, True)
     third = len(rest) // 3
-    late = late_share(gates_ref.shape[0], 1 / 6)
-    scatter = Scatter(place, partial, gates_ref, late, rest[:third])
+    late = late_share(gate_ref.shape[0], 1 / 6)
+    scatter = Scatter(place, partial, functools.partial(store_apart, gate_ref, up_ref), late, rest[:third])
     scatter_o = Scatter(place, partial_o, out_ref, late, rest[third : 2 * third])
     scatter_qkv = Scatter(place, partial_qkv, qkv_ref, late, rest[2 * third :])
     final = TensorSum(place, part, dn1_ref, 4, (near, chip, far, sum_sems))
@@ -1058,14 +1137,14 @@
         low = inverse * scaled - raw * (inverse * inverse * inverse * inner)
         return low.astype(BF16), jnp.sum((back * raw * inverse).reshape(-1, 8, LANES), axis=0)
 
-    gain_q = jnp.zeros((8, LANES), F32)
-    gain_k = jnp.zeros((8, LANES), F32)
+    head_sums[...] = jnp.zeros_like(head_sums)
+    turns = {3: every(3), 2: every(3), 1: {0: 1, 2: 1}, 0: {2: 1}}
     for qb in reversed(range(4)):
         last = (qb + 1) * tile
         rows = pl.ds(qb * tile, tile)
         bias_block(seg_col, seg_row, bias, qb * tile, tile)
 
-        def attend_back(pair, carry, last=last, rows=rows):
+        def attend_back(pair, last=last, rows=rows):
             keys = pl.ds(0, last)
             sides = []
             for side in range(2):
@@ -1087,25 +1166,26 @@
                 jnp.where(lanes < HALF, sides[0], sides[1]), qk_ref[rows, cols], cos_ref[rows, :], sin_ref[rows, :], gq
             )
             dlow[rows, cols] = low
-            return carry + terms
-
-        gain_q = lax.fori_loop(0, pairs, attend_back, gain_q)
+            head_sums[pl.ds(0, 8), :] += terms
+
+        polled(pairs, attend_back, (sums, turns[qb]))
         low, terms = head_back(
             dk[rows, :], qk_ref[rows, pl.ds(q_cols, LANES)], cos_ref[rows, :], sin_ref[rows, :], gk
         )
         dlow[rows, pl.ds(q_cols, LANES)] = low
         dlow[rows, pl.ds(q_cols + LANES, LANES)] = dv[rows, :].astype(BF16)
-        gain_k = gain_k + terms
+        head_sums[pl.ds(8, 8), :] += terms
         part[rows, :] = dot_nt(dlow[rows, :], wqkv[...]).astype(BF16)
         final.send_core(qb)
-        ahead(sums, 3)
-        final.send_across(qb)
         if qb < 3:
             final.send_back(qb + 1)
-        if qb == 1:
+        final.send_across(qb)
+        if qb == 2:
             scatter_o.start()
+        if qb < 2:
+            ahead(sums_o, 2)
     mine = head_slots.at[place.tensor]
-    mine[...] = jnp.concatenate([gain_q, gain_k], axis=0)
+    mine[...] = head_sums[...]
     head_copies = []
     for step in range(1, 4):
         copy = remote(
@@ -1154,30 +1234,39 @@
     one = jnp.sum(gain_one, axis=0, keepdims=True)
     two = jnp.sum(two_ref[...], axis=0, keepdims=True)
     small[...] = jnp.zeros_like(small)
-    for index in range(4):
-        cols = slice(index * quarter, (index + 1) * quarter)
-        small[pl.ds(index, 1), pl.ds(0, quarter)] = one[:, cols]
-        small[pl.ds(4 + index, 1), pl.ds(0, quarter)] = two[:, cols]
-    small[pl.ds(0, 1), pl.ds(quarter, LANES)] = jnp.sum(heads[:8], axis=0, keepdims=True)
-    small[pl.ds(1, 1), pl.ds(quarter, LANES)] = jnp.sum(heads[8:], axis=0, keepdims=True)
-    small_copies = []
-    for step in range(1, count):
-        copy = remote(
-            small, slots.at[step], small_send.at[2 + step], small_recv.at[2 + step],
-            lax.rem(place.me + step, count), place.tensor,
-        )
-        copy.start()
-        small_copies.append(copy)
+    q_sum = jnp.sum(heads[:8], axis=0, keepdims=True)
+    k_sum = jnp.sum(heads[8:], axis=0, keepdims=True)
+    q_sum = q_sum + pltpu.roll(q_sum, HALF, 1)
+    k_sum = k_sum + pltpu.roll(k_sum, HALF, 1)
+
+    def small_copy(d):
+        return remote(
+            small.at[d], slots.at[place.me], small_send.at[3 + d], small_recv.at[3 + place.me], d, place.tensor
+        )
+
+    for d in range(count):
+        for row, (values, size) in enumerate(((one, own), (two, own), (q_sum, few), (k_sum, few))):
+            small[d, pl.ds(row, 1), pl.ds(0, size)] = values[:, d * size : (d + 1) * size]
+        pl.when(place.me != d)(lambda d=d: small_copy(d).start())
+    slots[place.me] = small[place.me]
     drain(sums, sums_o, sums_qkv)
-    total = small[...]
-    for copy in small_copies:
-        copy.wait_recv()
-    for step in range(1, count):
-        total = total + slots[step]
+    for d in range(count):
+
+        @pl.when(place.me != d)
+        def _(d=d):
+            remote(
+                slots.at[d], slots.at[d], small_send.at[3 + d], small_recv.at[3 + d], d, place.tensor
+            ).wait_recv()
+
+    total = slots[0]
+    for d in range(1, count):
+        total = total + slots[d]
     small_ref[...] = total
+    for d in range(count):
+        pl.when(place.me != d)(lambda d=d: small_copy(d).wait_send())
     for save in saves:
         save.wait()
-    for copy in head_copies + small_copies:
+    for copy in head_copies:
         copy.wait_send()
     for each in (scatter, scatter_o, scatter_qkv, final):
         each.settle()
@@ -1191,33 +1280,35 @@
     shape = jax.ShapeDtypeStruct
     dma = pltpu.SemaphoreType.DMA
     loaded = [part, dwo, dm, qm, kb, vb, lse, qk, n1, jax.ShapeDtypeStruct((width, low), BF16), x, dh]
-    small = (8, width // 4 + LANES)
+    small = (8, 2 * LANES)
     return pl.pallas_call(
         functools.partial(last_kernel, count),
         out_shape=[
             shape((seq, width), F32),
-            shape((rows, part.shape[1]), F32),
+            shape((rows, part.shape[1] // 2), F32),
+            shape((rows, part.shape[1] // 2), F32),
             shape((rows, q_cols), F32),
             shape((rows, low), F32),
             shape(small, F32),
         ],
         in_specs=[in_place()] * 12 + [whole_block()] * 6,
-        out_specs=[in_place()] + [whole_block()] * 4,
+        out_specs=[in_place()] + [whole_block()] * 5,
         scratch_shapes=[
             *[pltpu.VMEM(one.shape, one.dtype) for one in loaded],
             pltpu.VMEM((width, low), BF16),
             pltpu.VMEM((seq // 4, seq), F32),
             pltpu.VMEM((seq, LANES), F32),
             pltpu.VMEM((seq, LANES), F32),
+            pltpu.VMEM((16, LANES), F32),
             pltpu.VMEM((seq, low), BF16),
             pltpu.VMEM((seq, width), BF16),
             pltpu.VMEM((seq, width), BF16),
-            pltpu.VMEM(small, F32),
+            pltpu.VMEM((count,) + small, F32),
             pltpu.VMEM((count,) + small, F32),
             pltpu.VMEM((4, 16, LANES), F32),
             *TensorSum.scratch(seq, width, 4, BF16),
-            dma((count + 2,)),
-            dma((count + 2,)),
+            dma((count + 3,)),
+            dma((count + 3,)),
             dma((12,)),
             *Scatter.scratch(count, rows, part.shape[1], late_share(rows, 1 / 6)),
             *Scatter.scratch(count, rows, q_cols, late_share(rows, 1 / 6)),
@@ -1229,57 +1320,12 @@
     )(part, dwo, dm, qm, kb, vb, lse, qk, n1, w0, x, dh, cosine, sine, seg_col, seg_row, gains, two)
 
 
-def rotation_tables(positions, head_dim):
-    half_dim = head_dim // 2
-    frequency = ROPE_BASE ** (-jnp.arange(half_dim, dtype=jnp.float32) * 2.0 / head_dim)
-    angles = positions.astype(jnp.float32)[:, None] * frequency[None, :]
-    return (jnp.cos(angles)[:, None, :], jnp.sin(angles)[:, None, :])
-
-
-def lay(gate, up):
-    rows, cols = gate.shape
-    even = cols // LANES * LANES
-    pairs = jnp.stack(
-        [gate[:, :even].reshape(rows, -1, LANES), up[:, :even].reshape(rows, -1, LANES)], axis=2
-    ).reshape(rows, 2 * even)
-    return jnp.concatenate([pairs, gate[:, even:], up[:, even:]], axis=1)
-
-
-def unlay(both):
-    rows, cols = both.shape
-    even = cols // 2 // LANES * LANES
-    pairs = both[:, : 2 * even].reshape(rows, -1, 2, LANES)
-    rest = both[:, 2 * even :]
-    size = rest.shape[1] // 2
-    return (
-        jnp.concatenate([pairs[:, :, 0].reshape(rows, even), rest[:, :size]], axis=1),
-        jnp.concatenate([pairs[:, :, 1].reshape(rows, even), rest[:, size:]], axis=1),
-    )
-
-
-def spread(gain, me, width):
-    full = jnp.zeros((width,), F32)
-    return lax.dynamic_update_slice(full, lax.reduce_precision(gain, 8, 7), (me * gain.shape[0],))
-
-
-def gain_rows(norm1_gain, norm2_gain, q_gain, k_gain, count):
-    me = lax.axis_index("dp")
-    width = norm1_gain.shape[0] * count
-    head = q_gain.shape[0] * count
-    rows = [spread(norm1_gain, me, width), spread(norm2_gain, me, width)]
-    for gain in (q_gain, k_gain):
-        one = spread(gain, me, head)
-        rows.append(jnp.pad(jnp.concatenate([one, one]), (0, width - 2 * head)))
-    return jnp.pad(jnp.stack(rows), ((0, 4), (0, 0)))
-
-
 def rotation_lanes(positions):
-    cosine, sine = rotation_tables(positions, HALF)
-    cosine, sine = cosine[:, 0], sine[:, 0]
-    return (
-        jnp.concatenate([cosine] * 4, axis=1),
-        jnp.concatenate([-sine, sine, -sine, sine], axis=1),
-    )
+    lane = np.arange(LANES)
+    frequency = ROPE_BASE ** (-(lane % (HALF // 2)) * 2.0 / HALF)
+    sign = np.where(lane % HALF < HALF // 2, -1.0, 1.0)
+    angles = positions.astype(F32)[:, None] * frequency.astype(np.float32)[None, :]
+    return jnp.cos(angles), jnp.sin(angles) * sign.astype(np.float32)[None, :]
 
 
 def shards(
@@ -1305,48 +1351,37 @@
     rows = w_q.shape[0]
     q_cols, kv_cols, ff_cols = w_q.shape[1], w_k.shape[1], w_gate.shape[1]
     small_gain = q_norm_gain.shape[0]
-    head_dim = small_gain * n_dp
     seg_col, seg_row = segments[:, None], segments[None, :]
-    gains = gain_rows(norm1_gain, norm2_gain, q_norm_gain, k_norm_gain, n_dp)
-    pack_attn = jnp.concatenate(
-        [w_q.astype(BF16), w_k.astype(BF16), w_v.astype(BF16), w_o.T.astype(BF16)], axis=1
-    )
-    pack_gates = lay(w_gate.astype(BF16), w_up.astype(BF16))
+    gains = jnp.concatenate(
+        [jnp.pad(gain, (0, 2 * LANES - gain.shape[0])) for gain in (norm1_gain, norm2_gain, q_norm_gain, k_norm_gain)]
+        + [jnp.zeros((8 * LANES,), F32)]
+    ).reshape(8, 2 * LANES)
     pack_down = jnp.pad(w_down.T.astype(BF16), ((0, 0), (0, -ff_cols % LANES)))
     cosine, sine = rotation_lanes(positions)
     w0, w1, n1, qk, qm, kb, vb, lse, ctx, h, n2, gains = forward_call(
-        n_dp, block_input, seg_col, seg_row, cosine, sine, gains, pack_attn, pack_gates
+        n_dp, block_input, w_gate, w_up, seg_col, seg_row, cosine, sine, gains, w_q, w_k, w_v, w_o.T.astype(BF16)
     )
     first, second, dn2, mlp, down = mlp_call(n_dp, n2, cotangent, w1, pack_down)
     mlp_total = lax.psum(mlp, "tensor")
-    dh, dm, dwo, gates_one, small_two = middle_call(n_dp, first, dn2, h, cotangent, w0, ctx, gains)
-    grad_input, gates_two, grad_o, grad_qkv, small = last_call(
+    dh, dm, dwo, gate_one, up_one, small_two = middle_call(n_dp, first, dn2, h, cotangent, w0, ctx, gains)
+    grad_input, gate_two, up_two, grad_o, grad_qkv, small = last_call(
         n_dp, second, dwo, dm, qm, kb, vb, lse, qk, n1, w0, block_input, dh,
         cosine, sine, seg_col, seg_row, gains, small_two,
     )
     output_rows = (h + mlp_total.astype(F32)).astype(BF16)
-    me = lax.axis_index("dp")
-    quarter = block_input.shape[1] // 4
-    one, two = small[:4, :quarter].reshape(-1), small[4:, :quarter].reshape(-1)
-    heads = small[:2, quarter:].reshape(2, 2, head_dim).sum(axis=1)
-
-    def own(values, size):
-        return lax.dynamic_slice_in_dim(values, me * size, size, 0)
-
-    grad_gate, grad_up = unlay(jnp.concatenate([gates_one, gates_two], axis=1))
     return (
         output_rows,
         grad_input,
-        own(one, rows),
-        own(heads[0], small_gain),
-        own(heads[1], small_gain),
+        small[0, :rows],
+        small[2, :small_gain],
+        small[3, :small_gain],
         grad_qkv[:, :q_cols],
         grad_qkv[:, q_cols : q_cols + kv_cols],
         grad_qkv[:, q_cols + kv_cols :],
         grad_o.T,
-        own(two, rows),
-        grad_gate,
-        grad_up,
+        small[1, :rows],
+        jnp.concatenate([gate_one, gate_two], axis=1),
+        jnp.concatenate([up_one, up_two], axis=1),
         down[:, :ff_cols].T,
     )
 

time: 554 us -> 507 us (0.915)
  Pallas kernels: 471 us -> 447 us
  local copies, waits for them, and re-layouts: 40 us -> 19.8 us
  other arithmetic: 24.6 us -> 16.2 us
    slice x11 -> x1, local copies, waits for them, and re-layouts: 12.1 us -> 1.34 us  [shards(): small[1, :rows]]
    pallas_call x1, Pallas kernels: 116 us -> 106 us  [last_call(): pl.pallas_call(functools.partial(last_kernel, count), out_shape=[shape((s...]
    pallas_call x1, Pallas kernels: 128 us -> 122 us  [mlp_call(): pl.pallas_call(functools.partial(mlp_kernel, count, shares), out_shape=[s...]
    unnamed x42 -> x18, local copies, waits for them, and re-layouts: 11.5 us -> 9.41 us
  transfers between devices with their start and end apart: 1 -> 1, of which waited for: 0 -> 0; matrix products, arithmetic and copies ran while one was open for 5% -> 2% of each run, Pallas kernels for 33% -> 34%
where the time goes in v4:
time: 507 us; the launch traced here: 498 us
  Pallas kernels  447 us (88%)
  local copies, waits for them, and re-layouts  19.8 us (4%)
  other arithmetic  16.2 us (3%)
  between operations  14.6 us (3%)
    pallas_call x1, Pallas kernels, forward_call(): pl.pallas_call(functools.partial(forward_kernel, count), out_shape=[jax.S...  158 us
    pallas_call x1, Pallas kernels, mlp_call(): pl.pallas_call(functools.partial(mlp_kernel, count, shares), out_shape=[s...  122 us
    pallas_call x1, Pallas kernels, last_call(): pl.pallas_call(functools.partial(last_kernel, count), out_shape=[shape((s...  106 us
    pallas_call x1, Pallas kernels, middle_call(): pl.pallas_call(functools.partial(middle_kernel, count), out_shape=[shape(...  62.1 us
  transfers between devices with their start and end apart: 1, of which 0 were waited for; matrix products, arithmetic and copies ran while one was open for 2% of the time, Pallas kernels for 34%

profile of v4, /device:TPU:0, one launch (start us, length us, event | category | flops | bytes accessed | tf_op | source)
XLA Modules:
  0.0 498.1 jit_solution(9342895853899451768)
XLA Ops:
  7.2 0.0 copy-start.4
  7.2 0.0 copy-start.5
  7.2 0.0 all-reduce.7.cloned.1.call-start
  7.3 0.7 convert_element_type.28
  8.0 0.7 constant_dynamic-update-slice_fusion.4
  8.6 0.7 constant_dynamic-update-slice_fusion.3
  9.3 0.7 constant_dynamic-update-slice_fusion.2
  10.0 0.7 constant_dynamic-update-slice_fusion.1
  10.6 0.6 reshape.30.refs_7_
  11.3 1.6 convert_bitcast_fusion.1.refs_11_
  12.9 1.7 copy.30.refs_3_.refs_14_
  14.6 1.4 convert_bitcast_fusion
  16.0 0.9 pad.22.refs_3_
  16.9 0.0 copy-done.5
  16.9 3.0 fusion
  20.0 157.8 %shard_map.264 = (bf16[1536,1024]{1,0:T(8,128)(2,1)}, bf16[1536,3456]{1,0:T(8,128)(2,1)}, bf16[1024,1536]{1,0:T(8,128)(2,1)}, f32[1024,512]{1,0:T(8,128)}, bf16[...) custom-call(bf16[1024,1536]{1,0:T(8,128)(2,1)} %refs_10_.3, ...), custom_call_target="tpu_custom_call" | custom-call | tf_op jit(solution)/shard_map/pallas_call | solution.py:572
  177.8 121.8 %shard_map.265 = (bf16[1536,1792]{1,0:T(8,128)(2,1)}, bf16[1536,1664]{1,0:T(8,128)(2,1)}, bf16[1024,1536]{1,0:T(8,128)(2,1)}, bf16[1024,1536]{1,0:T(8,128)(2,1)}, f32[192,1792]{1,0:T(8,128)}) custom-call(bf16[1024,1536]{1,0:T(8,128)(2,1)} %get-tuple-element.43.refs_0_, bf16[1024,1536]{1,0:T(8,128)(2,1)} %refs_3_.1, ...), custom_call_target="tpu_custom_call" | custom-call | tf_op jit(solution)/shard_map/pallas_call | solution.py:948
  299.6 0.0 all-reduce.7.cloned.1.call-update
  299.6 62.1 %shard_map.266 = (f32[1024,1536]{1,0:T(8,128)}, bf16[6,1024,128]{2,1,0:T(8,128)(2,1)}, bf16[1536,384]{1,0:T(8,128)(2,1)}, f32[192,896]{1,0:T(8,128)}, f32[192,896]{1,0:T(8,128)}, /*index=5*/f32[8,1536]{1,0:T(8,128)}) custom-call(bf16[1536,1792]{1,0:T(8,128)(2,1)} %get-tuple-element.47.refs_0_, bf16[1024,1536]{1,0:T(8,128)(2,1)} %get-tuple-element.48.refs_1_, ...), custom_call_target="tpu_custom_call" | custom-call | tf_op jit(solution)/shard_map/pallas_call | solution.py:1057
  361.8 0.0 copy-start.1
  361.8 0.0 copy-start.2
  361.8 105.7 %shard_map.267 = (f32[1024,1536]{1,0:T(8,128)}, f32[192,832]{1,0:T(8,128)}, f32[192,832]{1,0:T(8,128)}, f32[192,384]{1,0:T(8,128)}, f32[192,640]{1,0:T(8,128)}, /*index=5*/f32[8,256]{1,0:T(8,128)}) custom-call(bf16[1536,1664]{1,0:T(8,128)(2,1)} %get-tuple-element.46.refs_0_, bf16[1536,384]{1,0:T(8,128)(2,1)} %get-tuple-element.52.refs_1_, ...), custom_call_target="tpu_custom_call" | custom-call | tf_op jit(solution)/shard_map/pallas_call | solution.py:1284
  467.5 1.8 slice.27
  469.3 1.3 slice_bitcast_fusion.1
  470.6 1.3 fusion.2
  471.9 1.6 fusion.1
  473.5 0.0 copy-done.1
  473.5 3.0 pad_maximum_fusion
  476.6 1.2 slice_bitcast_fusion
  477.7 6.4 %add_convert_fusion = bf16[1024,1536]{1,0:T(8,128)(2,1)} fusion(f32[1024,1536]{1,0:T(8,128)} %get-tuple-element.42.refs_2_, bf16[1024,1536]{1,0:T(8,128)(2,1)} %all-reduce.7.cloned.1.call-done), kind=kLoop, calls=%fused_computation | loop fusion | flops 4718592 | bytes 12582912 | tf_op jit(solution)/shard_map/convert_element_type | solution.py:1371
  484.1 6.0 %copy.40 = f32[1024,1536]{1,0:T(8,128)} copy(f32[1024,1536]{1,0:T(8,128)} %get-tuple-element.95) | data formatting | bytes 12582912
  490.1 0.7 copy.41
  (9 shorter events, 0.0 us)
Async XLA Ops:
  7.2 9.7 %copy-start.4 = (f32[128]{0:T(128)S(1)}, f32[128]{0:T(128)}, u32[]{:S(2)}) copy-start(f32[128]{0:T(128)} %constant.23) | copy-start | bytes 1540
  7.2 9.7 %copy-start.5 = (f32[128]{0:T(128)S(1)}, f32[128]{0:T(128)}, u32[]{:S(2)}) copy-start(f32[128]{0:T(128)} %constant.22) | copy-start | bytes 1540
  7.2 470.5 %all-reduce.7.cloned.1.call-start = ((), (), s32[]{:S(2)}) async-start(), calls=%async_computation | async-start | bytes 6291456 | tf_op jit(solution)/shard_map/psum | solution.py:1365
  361.8 111.8 %copy-start.1 = (f32[192,896]{1,0:T(8,128)S(1)}, f32[192,896]{1,0:T(8,128)}, u32[]{:S(2)}) copy-start(f32[192,896]{1,0:T(8,128)} %get-tuple-element.66) | copy-start | bytes 2064388
  361.8 111.8 %copy-start.2 = (f32[192,896]{1,0:T(8,128)S(1)}, f32[192,896]{1,0:T(8,128)}, u32[]{:S(2)}) copy-start(f32[192,896]{1,0:T(8,128)} %get-tuple-element.68) | copy-start | bytes 2064388
  467.5 9.1 %copy-start = (f32[192,1792]{1,0:T(8,128)S(1)}, f32[192,1792]{1,0:T(8,128)}, u32[]{:S(2)}) copy-start(f32[192,1792]{1,0:T(8,128)} %get-tuple-element.70) | copy-start | bytes 4128772
  484.1 6.0 %copy-start.3 = (f32[192,384]{1,0:T(8,128)S(1)}, f32[192,384]{1,0:T(8,128)}, u32[]{:S(2)}) copy-start(f32[192,384]{1,0:T(8,128)} %get-tuple-element.65) | copy-start | bytes 884740
Sparse Core Ops, SparseCore 0:
  299.7 68.8 all-reduce.6

commit v5 on v4

--- a/solution.py
+++ b/solution.py
@@ -321,11 +321,19 @@
     return values * cosine + jnp.where(first, ahead, back) * sine
 
 
+def column_of(row_ref, column):
+    for index in range(row_ref.shape[1] // LANES):
+        spot = pl.ds(index * LANES, LANES)
+        row = row_ref[:, spot].astype(F32)
+        column[spot, :] = jnp.broadcast_to(row, (LANES, LANES)).T
+
+
 def bias_block(seg_col, seg_row, bias, first, tile):
     last = first + tile
     rows = lax.broadcasted_iota(jnp.int32, (tile, last), 0) + first
     cols = lax.broadcasted_iota(jnp.int32, (tile, last), 1)
-    allowed = (seg_col[pl.ds(first, tile), :] == seg_row[:, pl.ds(0, last)]) & (rows >= cols)
+    same = seg_col[pl.ds(first, tile), pl.ds(0, 1)] == seg_row[:, pl.ds(0, last)].astype(F32)
+    allowed = same & (rows >= cols)
     bias[:, pl.ds(0, last)] = jnp.where(allowed, 0.0, MASKED)
 
 
@@ -371,10 +379,12 @@
 
 def forward_kernel(count, *refs):
     (
-        x_hbm, gate_hbm, up_hbm, seg_col, seg_row, cos_ref, sin_ref, gain_ref, wq_ref, wk_ref, wv_ref, wot_ref,
-        full_attn, full_gates, n1_out, qk_out, qm_out, kb_out, vb_out, lse_out, ctx_out, h_out, n2_out, gains_out,
-        x_ref, w0, n1_ref, qk_ref, qm_ref, kb_ref, vb_ref, lse_ref, ctx_ref, h_ref, n2_ref,
-        pack_attn, pack_gates, gate_ref, up_ref, bias, gain_slots, part, total, tmp_near, tmp_chip, tmp_far, sum_sems, gain_send, gain_recv, copy_sems,
+        x_hbm, gate_hbm, up_hbm, seg_row, pos_row, turn_ref, g1_ref, g2_ref, gq_ref, gk_ref,
+        wq_ref, wk_ref, wv_ref, wot_ref,
+        full_attn, full_gates, n1_out, qk_out, qm_out, kb_out, vb_out, lse_out, ctx_out, h_out, n2_out, cos_out, sin_out, hq_out,
+        gains_out,
+        x_ref, w0, n1_ref, qk_ref, qm_ref, kb_ref, vb_ref, lse_ref, ctx_ref, h_ref, n2_ref, cos_ref, sin_ref, hq_ref,
+        column, pack_attn, pack_gates, gate_ref, up_ref, bias, gain_slots, part, total, tmp_near, tmp_chip, tmp_far, sum_sems, gain_send, gain_recv, copy_sems,
         *gather_sems,
     ) = refs
     place = Place(count)
@@ -390,7 +400,9 @@
     for ref in (wq_ref, wk_ref, wv_ref, wot_ref):
         pack_attn[:, pl.ds(spot, ref.shape[1])] = ref[...].astype(BF16)
         spot += ref.shape[1]
-    gain_slots[place.me] = gain_ref[...].astype(BF16).astype(F32)
+    gain_slots[place.me] = jnp.zeros(gain_slots.shape[1:], F32)
+    for row, ref in enumerate((g1_ref, g2_ref, gq_ref, gk_ref)):
+        gain_slots[place.me, pl.ds(row, 1), pl.ds(0, ref.shape[1])] = ref[...].astype(BF16).astype(F32)
     place.greet(True, True)
     first = Gather(place, pack_attn, w0, late_share(pack_attn.shape[0], 1 / 6), gather_sems[:5])
     second = Gather(place, pack_gates, full_gates, late_share(pack_gates.shape[0], 1 / 6), gather_sems[5:])
@@ -419,8 +431,19 @@
     pack_gates[:, pl.ds(2 * even * LANES, LANES)] = jnp.concatenate(
         [gate_ref[:, rest], up_ref[:, rest]], axis=1
     ).astype(BF16)
+    column_of(pos_row, column)
+
+    def angles(index, carry):
+        rows = pl.ds(pl.multiple_of(index * LANES, LANES), LANES)
+        angle = column[rows, pl.ds(0, 1)] * turn_ref[pl.ds(0, 1), :]
+        cos_ref[rows, :] = jnp.cos(angle)
+        sin_ref[rows, :] = jnp.sin(angle) * turn_ref[pl.ds(1, 1), :]
+        return carry
+
+    lax.fori_loop(0, seq // LANES, angles, 0)
+    column_of(seg_row, column)
     for qb in range(4):
-        bias_block(seg_col, seg_row, bias.at[qb], qb * tile, tile)
+        bias_block(column, seg_row, bias.at[qb], qb * tile, tile)
     for step in range(1, count):
         whose = gain_slots.at[lax.rem(place.me + count - step, count)]
         remote(whose, whose, gain_send.at[step], gain_recv.at[step], place.me, place.tensor).wait_recv()
@@ -448,7 +471,11 @@
         return carry
 
     lax.fori_loop(0, seq // LANES, norm_one, 0)
-    saves = [begin(n1_ref, n1_out, copy_sems.at[1])]
+    saves = [
+        begin(n1_ref, n1_out, copy_sems.at[1]),
+        begin(cos_ref, cos_out, copy_sems.at[13]),
+        begin(sin_ref, sin_out, copy_sems.at[14]),
+    ]
     drain(moves_first)
     second.start()
     moves = second.steps()
@@ -531,6 +558,7 @@
             rows = pl.ds(pl.multiple_of(index * tile + sub * LANES, LANES), LANES)
             h = x_ref[rows, :].astype(F32) + total[rows, :]
             h_ref[rows, :] = h
+            hq_ref[rows, :] = (h * 0.25).astype(BF16)
             inverse = lax.rsqrt(jnp.mean(h * h, axis=1, keepdims=True) + EPSILON)
             n2_ref[rows, :] = (h * inverse * g2).astype(BF16)
             return carry
@@ -539,6 +567,7 @@
         next(moves, None)
     saves.append(begin(h_ref, h_out, copy_sems.at[9]))
     saves.append(begin(n2_ref, n2_out, copy_sems.at[10]))
+    saves.append(begin(hq_ref, hq_out, copy_sems.at[15]))
     drain(moves)
     second.finish()
     for save in saves:
@@ -550,7 +579,7 @@
     summed.settle()
 
 
-def forward_call(count, x, gate, up, seg_col, seg_row, cosine, sine, gains, wq, wk, wv, wot):
+def forward_call(count, x, gate, up, seg_row, pos_row, turns, g1, g2, gq, gk, wq, wk, wv, wot):
     seq, width = x.shape
     rows = wq.shape[0]
     q_cols, kv_cols = wq.shape[1], LANES
@@ -565,6 +594,9 @@
         ((seq, q_cols), BF16),
         ((seq, width), F32),
         ((seq, width), BF16),
+        ((seq, LANES), F32),
+        ((seq, LANES), F32),
+        ((seq, width), BF16),
     ]
     attn = ((count * rows, attn_cols), BF16)
     outs = [attn, ((count * rows, 2 * gate.shape[1]), BF16), *kept, ((8, width), F32)]
@@ -572,31 +604,32 @@
     return pl.pallas_call(
         functools.partial(forward_kernel, count),
         out_shape=[jax.ShapeDtypeStruct(*out) for out in outs],
-        in_specs=[in_place()] * 3 + [whole_block()] * 9,
-        out_specs=[in_place()] * 11 + [whole_block()],
+        in_specs=[in_place()] * 3 + [whole_block()] * 11,
+        out_specs=[in_place()] * 14 + [whole_block()],
         scratch_shapes=[
             pltpu.VMEM((seq, width), BF16),
             pltpu.VMEM(*attn),
             *[pltpu.VMEM(*one) for one in kept],
+            pltpu.VMEM((seq, LANES), F32),
             pltpu.VMEM((rows, attn_cols), BF16),
             pltpu.VMEM((rows, 2 * gate.shape[1]), BF16),
             pltpu.VMEM(gate.shape, F32),
             pltpu.VMEM(up.shape, F32),
             pltpu.VMEM((4, seq // 4, seq), F32),
-            pltpu.VMEM((count,) + gains.shape, F32),
+            pltpu.VMEM((count, 8, 2 * LANES), F32),
             pltpu.VMEM((seq, width), F32),
             pltpu.VMEM((seq, width), F32),
             *TensorSum.scratch(seq, width, 4, F32),
             dma((count,)),
             dma((count,)),
-            dma((13,)),
+            dma((16,)),
             *Gather.sems(count),
             *Gather.sems(count),
         ],
         compiler_params=pltpu.CompilerParams(
             collective_id=1, has_side_effects=True, vmem_limit_bytes=61 << 20
         ),
-    )(x, gate, up, seg_col, seg_row, cosine, sine, gains, wq, wk, wv, wot)
+    )(x, gate, up, seg_row, pos_row, turns, g1, g2, gq, gk, wq, wk, wv, wot)
 
 
 def store(ref, rows, value):
@@ -617,8 +650,10 @@
 
 
 class Scatter:
-    def __init__(self, place, partial, result, late, scratch):
+    def __init__(self, place, partial, result, late, scratch, flight=2, source=None):
         self.place, self.partial = place, partial
+        self.flight = flight
+        self.source = partial if source is None else source
         self.put = result if callable(result) else functools.partial(store, result)
         self.rows = partial.shape[0] // place.count
         self.late = late
@@ -667,7 +702,7 @@
         index, cut = self.pieces[number]
         start, size = self.cuts[cut]
         return remote(
-            self.partial.at[self.spot(self.goals[index], True, start, size), :],
+            self.source.at[self.spot(self.goals[index], True, start, size), :],
             self.over_in.at[index, pl.ds(start, size), :],
             self.ysend.at[index, cut], self.yrecv.at[index, cut], place.beside, place.tensor,
         )
@@ -682,7 +717,7 @@
         self.start_near()
 
     def start_near(self):
-        for number in range(len(self.cuts)):
+        for number in range(self.flight):
             self.cross(number)
 
     def start_far(self):
@@ -735,7 +770,7 @@
     def arrived(self, index, cut):
         number = index * len(self.cuts) + cut
         self.over(number).wait_recv()
-        self.cross(number + len(self.cuts))
+        self.cross(number + self.flight)
         start, size = self.cuts[cut]
         return self.over_in.at[index, pl.ds(start, size), :]
 
@@ -825,7 +860,7 @@
 
 def mlp_kernel(count, shares, *refs):
     (
-        n2_hbm, cot_hbm, gates_hbm, pack_down,
+        n2_hbm, cot_hbm, gates_hbm, hq_hbm, pack_down,
         first_out, second_out, dn2_out, part_out, down_ref,
         n2_ref, cot_ref, dn2_part, dn2_ref, w1, w2, ab, hid, partial, near, chip, far, sum_sems, copy_sems, *rest,
     ) = refs
@@ -897,6 +932,8 @@
     piece = jnp.where(lanes < HALF, piece, pltpu.roll(piece, HALF, 1))
     ab[:, tail] = (ab[:, tail].astype(F32) * piece).astype(BF16)
 
+    base = begin(hq_hbm, cot_ref, copy_sems.at[2])
+
     def normed_grad(index):
         rows = pl.ds(pl.multiple_of(index * tile, tile), tile)
         dn2_part[rows, :] = dot_nt(ab[rows, :], w1[...]).astype(BF16)
@@ -913,8 +950,9 @@
 
     def output_part(index):
         rows = pl.ds(pl.multiple_of(index * 256, 256), 256)
-        cot_ref[:, rows] = dot_nt(hid[...], w2[rows, :]).astype(BF16)
-
+        cot_ref[:, rows] = (dot_nt(hid[...], w2[rows, :]) + cot_ref[:, rows].astype(F32)).astype(BF16)
+
+    base.wait()
     polled(width // 256, output_part, (sums, {2: 1, 5: 1}), (tensor, {5: 1}))
     saves = [begin(cot_ref, part_out, copy_sems.at[4])]
 
@@ -937,7 +975,7 @@
     summed.settle()
 
 
-def mlp_call(count, n2, cot, full_gates, pack_down):
+def mlp_call(count, n2, cot, full_gates, hq, pack_down):
     seq, width = n2.shape
     rows, down = pack_down.shape
     shares = late_share(rows, 1 / 6), late_share(rows, 1 / 4)
@@ -954,7 +992,7 @@
             shape((seq, width), BF16),
             shape((rows, down), F32),
         ],
-        in_specs=[in_place()] * 4,
+        in_specs=[in_place()] * 5,
         out_specs=[in_place()] * 4 + [whole_block()],
         scratch_shapes=[
             *[pltpu.VMEM((seq, width), BF16)] * 4,
@@ -971,7 +1009,7 @@
         compiler_params=pltpu.CompilerParams(
             collective_id=2, has_side_effects=True, vmem_limit_bytes=61 << 20
         ),
-    )(n2, cot, full_gates, pack_down)
+    )(n2, cot, full_gates, hq, pack_down)
 
 
 def middle_kernel(count, *refs):
@@ -987,23 +1025,25 @@
     group = heads // 2
     tile = seq // 4
     lanes = lane_ids()
+    load = begin(part_in, partial, copy_sems.at[0])
+    place.greet(False, False)
+    put = functools.partial(store_apart, gate_ref, up_ref)
+    scatter = Scatter(place, partial, put, late_share(gate_ref.shape[0], 1 / 6), rest, 3, part_in)
+    scatter.start_near()
+    load.wait()
+    scatter.start_far()
     loads = [
-        begin(src, dst, copy_sems.at[index])
+        begin(src, dst, copy_sems.at[index + 1])
         for index, (src, dst) in enumerate(
             (
-                (part_in, partial), (dn2_hbm, dn2_ref), (h_hbm, h_ref), (cot_hbm, cot_ref),
+                (dn2_hbm, dn2_ref), (h_hbm, h_ref), (cot_hbm, cot_ref),
                 (w0_hbm.at[:, pl.ds(w0_hbm.shape[1] - q_cols, q_cols)], wo), (ctx_hbm, ctx_ref),
             )
         )
     ]
-    place.greet(False, False)
-    put = functools.partial(store_apart, gate_ref, up_ref)
-    scatter = Scatter(place, partial, put, late_share(gate_ref.shape[0], 1 / 6), rest)
-    loads[0].wait()
-    scatter.start()
     sums = scatter.steps()
     g2 = gain_ref[pl.ds(1, 1), :]
-    for load in loads[1:]:
+    for load in loads:
         load.wait()
     small_ref[...] = jnp.zeros_like(small_ref)
 
@@ -1034,14 +1074,17 @@
                 dm_ref[head, rows, :] = jnp.where(lanes // HALF == head // group, keep, 0.0).astype(BF16)
 
     polled(4, back, (sums, {1: 1, 2: 1, 3: 1}))
-    saves = [begin(dh_ref, dh_out, copy_sems.at[6]), begin(dm_ref, dm_out, copy_sems.at[7])]
+    saves = [
+        begin(dh_ref, dh_out, copy_sems.at[7]),
+        begin(dm_ref, dm_out, copy_sems.at[8]),
+    ]
 
     def out_grad(index):
         rows = pl.ds(pl.multiple_of(index * 384, 384), 384)
         dwo_ref[rows, :] = dot_tn(dhb[:, rows], ctx_ref[...]).astype(BF16)
 
     polled(width // 384, out_grad, (sums, {1: 1, 3: 1}))
-    saves.append(begin(dwo_ref, dwo_out, copy_sems.at[8]))
+    saves.append(begin(dwo_ref, dwo_out, copy_sems.at[10]))
     drain(sums)
     for save in saves:
         save.wait()
@@ -1077,7 +1120,7 @@
             pltpu.VMEM((q_cols // HALF, seq, LANES), BF16),
             pltpu.VMEM((width, q_cols), BF16),
             pltpu.VMEM((seq, width), BF16),
-            dma((9,)),
+            dma((11,)),
             *Scatter.scratch(count, rows, part.shape[1], late_share(rows, 1 / 6)),
         ],
         compiler_params=pltpu.CompilerParams(
@@ -1089,10 +1132,10 @@
 def last_kernel(count, *refs):
     (
         part_in, dwo_in, dm_hbm, qm_hbm, kb_hbm, vb_hbm, lse_hbm, qk_hbm, n1_hbm, w0_hbm, x_hbm, dh_hbm,
-        cos_ref, sin_ref, seg_col, seg_row, gain_ref, two_ref,
+        cos_hbm, sin_hbm, seg_row, gain_ref, two_ref,
         grad_out, gate_ref, up_ref, out_ref, qkv_ref, small_ref,
-        partial, partial_o, dm_ref, qm_ref, kb_ref, vb_ref, lse_ref, qk_ref, n1_ref, wqkv, x_ref, dh_ref,
-        partial_qkv, bias, dk, dv, head_sums, dlow, part, dn1_ref, small, slots, head_slots,
+        partial, partial_o, dm_ref, qm_ref, kb_ref, vb_ref, lse_ref, qk_ref, n1_ref, wqkv, x_ref, dh_ref, cos_ref, sin_ref,
+        column, partial_qkv, bias, dk, dv, head_sums, dlow, part, dn1_ref, small, slots, head_slots,
         near, chip, far, sum_sems, small_send, small_recv, copy_sems, *rest,
     ) = refs
     place = Place(count)
@@ -1107,26 +1150,29 @@
     lanes = lane_ids()
     sources = (
         (part_in, partial), (dwo_in, partial_o), (qm_hbm, qm_ref), (kb_hbm, kb_ref), (lse_hbm, lse_ref),
-        (dm_hbm, dm_ref), (vb_hbm, vb_ref), (qk_hbm, qk_ref),
+        (dm_hbm, dm_ref), (vb_hbm, vb_ref), (qk_hbm, qk_ref), (cos_hbm, cos_ref), (sin_hbm, sin_ref),
         (w0_hbm.at[:, pl.ds(0, wqkv.shape[1])], wqkv), (n1_hbm, n1_ref), (x_hbm, x_ref), (dh_hbm, dh_ref),
     )
-    loads = [begin(src, dst, copy_sems.at[index]) for index, (src, dst) in enumerate(sources)]
+    loads = [begin(src, dst, copy_sems.at[index]) for index, (src, dst) in enumerate(sources[:2])]
     place.greet(True, True)
     third = len(rest) // 3
     late = late_share(gate_ref.shape[0], 1 / 6)
-    scatter = Scatter(place, partial, functools.partial(store_apart, gate_ref, up_ref), late, rest[:third])
-    scatter_o = Scatter(place, partial_o, out_ref, late, rest[third : 2 * third])
-    scatter_qkv = Scatter(place, partial_qkv, qkv_ref, late, rest[2 * third :])
+    scatter = Scatter(place, partial, functools.partial(store_apart, gate_ref, up_ref), late, rest[:third], 3, part_in)
+    scatter_o = Scatter(place, partial_o, out_ref, late, rest[third : 2 * third], 8)
+    scatter_qkv = Scatter(place, partial_qkv, qkv_ref, late, rest[2 * third :], 8)
     final = TensorSum(place, part, dn1_ref, 4, (near, chip, far, sum_sems))
-    for load in loads[:2]:
+    scatter.start_near()
+    for load in loads:
         load.wait()
-    scatter.start()
+    scatter.start_far()
+    loads = [begin(src, dst, copy_sems.at[index + 2]) for index, (src, dst) in enumerate(sources[2:])]
+    column_of(seg_row, column)
     sums, sums_o = scatter.steps(), scatter_o.steps()
     dk[...] = jnp.zeros_like(dk)
     dv[...] = jnp.zeros_like(dv)
     gq = gain_ref[pl.ds(2, 1), pl.ds(0, LANES)]
     gk = gain_ref[pl.ds(3, 1), pl.ds(0, LANES)]
-    for load in loads[2:9]:
+    for load in loads[:9]:
         load.wait()
 
     def head_back(grad, raw, cosine, sine, gain):
@@ -1142,7 +1188,7 @@
     for qb in reversed(range(4)):
         last = (qb + 1) * tile
         rows = pl.ds(qb * tile, tile)
-        bias_block(seg_col, seg_row, bias, qb * tile, tile)
+        bias_block(column, seg_row, bias, qb * tile, tile)
 
         def attend_back(pair, last=last, rows=rows):
             keys = pl.ds(0, last)
@@ -1272,14 +1318,14 @@
         each.settle()
 
 
-def last_call(count, part, dwo, dm, qm, kb, vb, lse, qk, n1, w0, x, dh, cosine, sine, seg_col, seg_row, gains, two):
+def last_call(count, part, dwo, dm, qm, kb, vb, lse, qk, n1, w0, x, dh, cosine, sine, seg_row, gains, two):
     seq, width = n1.shape
     rows = width // count
     q_cols = dwo.shape[1]
     low = qk.shape[1] + LANES
     shape = jax.ShapeDtypeStruct
     dma = pltpu.SemaphoreType.DMA
-    loaded = [part, dwo, dm, qm, kb, vb, lse, qk, n1, jax.ShapeDtypeStruct((width, low), BF16), x, dh]
+    loaded = [part, dwo, dm, qm, kb, vb, lse, qk, n1, jax.ShapeDtypeStruct((width, low), BF16), x, dh, cosine, sine]
     small = (8, 2 * LANES)
     return pl.pallas_call(
         functools.partial(last_kernel, count),
@@ -1291,10 +1337,11 @@
             shape((rows, low), F32),
             shape(small, F32),
         ],
-        in_specs=[in_place()] * 12 + [whole_block()] * 6,
+        in_specs=[in_place()] * 14 + [whole_block()] * 3,
         out_specs=[in_place()] + [whole_block()] * 5,
         scratch_shapes=[
             *[pltpu.VMEM(one.shape, one.dtype) for one in loaded],
+            pltpu.VMEM((seq, LANES), F32),
             pltpu.VMEM((width, low), BF16),
             pltpu.VMEM((seq // 4, seq), F32),
             pltpu.VMEM((seq, LANES), F32),
@@ -1309,7 +1356,7 @@
             *TensorSum.scratch(seq, width, 4, BF16),
             dma((count + 3,)),
             dma((count + 3,)),
-            dma((12,)),
+            dma((14,)),
             *Scatter.scratch(count, rows, part.shape[1], late_share(rows, 1 / 6)),
             *Scatter.scratch(count, rows, q_cols, late_share(rows, 1 / 6)),
             *Scatter.scratch(count, rows, low, late_share(rows, 1 / 6)),
@@ -1317,15 +1364,14 @@
         compiler_params=pltpu.CompilerParams(
             collective_id=4, has_side_effects=True, vmem_limit_bytes=61 << 20
         ),
-    )(part, dwo, dm, qm, kb, vb, lse, qk, n1, w0, x, dh, cosine, sine, seg_col, seg_row, gains, two)
-
-
-def rotation_lanes(positions):
+    )(part, dwo, dm, qm, kb, vb, lse, qk, n1, w0, x, dh, cosine, sine, seg_row, gains, two)
+
+
+def rotary_rows():
     lane = np.arange(LANES)
     frequency = ROPE_BASE ** (-(lane % (HALF // 2)) * 2.0 / HALF)
     sign = np.where(lane % HALF < HALF // 2, -1.0, 1.0)
-    angles = positions.astype(F32)[:, None] * frequency.astype(np.float32)[None, :]
-    return jnp.cos(angles), jnp.sin(angles) * sign.astype(np.float32)[None, :]
+    return jnp.asarray(np.concatenate([frequency[None], sign[None], np.zeros((6, LANES))]).astype(np.float32))
 
 
 def shards(
@@ -1351,24 +1397,22 @@
     rows = w_q.shape[0]
     q_cols, kv_cols, ff_cols = w_q.shape[1], w_k.shape[1], w_gate.shape[1]
     small_gain = q_norm_gain.shape[0]
-    seg_col, seg_row = segments[:, None], segments[None, :]
-    gains = jnp.concatenate(
-        [jnp.pad(gain, (0, 2 * LANES - gain.shape[0])) for gain in (norm1_gain, norm2_gain, q_norm_gain, k_norm_gain)]
-        + [jnp.zeros((8 * LANES,), F32)]
-    ).reshape(8, 2 * LANES)
+    seg_row, pos_row = segments[None, :], positions[None, :]
     pack_down = jnp.pad(w_down.T.astype(BF16), ((0, 0), (0, -ff_cols % LANES)))
-    cosine, sine = rotation_lanes(positions)
-    w0, w1, n1, qk, qm, kb, vb, lse, ctx, h, n2, gains = forward_call(
-        n_dp, block_input, w_gate, w_up, seg_col, seg_row, cosine, sine, gains, w_q, w_k, w_v, w_o.T.astype(BF16)
+    w0, w1, n1, qk, qm, kb, vb, lse, ctx, h, n2, cosine, sine, hq, gains = forward_call(
+        n_dp, block_input, w_gate, w_up, seg_row, pos_row, rotary_rows(),
+        norm1_gain[None, :], norm2_gain[None, :], q_norm_gain[None, :], k_norm_gain[None, :],
+        w_q, w_k, w_v, w_o.T.astype(BF16),
     )
-    first, second, dn2, mlp, down = mlp_call(n_dp, n2, cotangent, w1, pack_down)
-    mlp_total = lax.psum(mlp, "tensor")
-    dh, dm, dwo, gate_one, up_one, small_two = middle_call(n_dp, first, dn2, h, cotangent, w0, ctx, gains)
+    first, second, dn2, mlp, down = mlp_call(n_dp, n2, cotangent, w1, hq, pack_down)
+    output_rows = lax.psum(mlp, "tensor")
+    dh, dm, dwo, gate_one, up_one, small_two = middle_call(
+        n_dp, first, dn2, h, cotangent, w0, ctx, gains
+    )
     grad_input, gate_two, up_two, grad_o, grad_qkv, small = last_call(
         n_dp, second, dwo, dm, qm, kb, vb, lse, qk, n1, w0, block_input, dh,
-        cosine, sine, seg_col, seg_row, gains, small_two,
+        cosine, sine, seg_row, gains, small_two,
     )
-    output_rows = (h + mlp_total.astype(F32)).astype(BF16)
     return (
         output_rows,
         grad_input,

time: 507 us -> 492 us (0.970)
  other arithmetic: 16.2 us -> 6.18 us
    convert_element_type x2 -> x0, other arithmetic: 7.08 us -> none  [the longest x1 6.39 us: shards(): output_rows = (h + mlp_total.astype(F32)).astype(BF16)]
    unnamed x18 -> x11, local copies, waits for them, and re-layouts: 9.41 us -> 10.5 us
where the time goes in v5:
time: 492 us; the launch traced here: 482 us
  Pallas kernels  443 us (90%)
  local copies, waits for them, and re-layouts  18.5 us (4%)
  between operations  14.5 us (3%)
  other arithmetic  6.18 us (1%)
    pallas_call x1, Pallas kernels, forward_call(): pl.pallas_call(functools.partial(forward_kernel, count), out_shape=[jax.S...  157 us
    pallas_call x1, Pallas kernels, mlp_call(): pl.pallas_call(functools.partial(mlp_kernel, count, shares), out_shape=[s...  122 us
    pallas_call x1, Pallas kernels, last_call(): pl.pallas_call(functools.partial(last_kernel, count), out_shape=[shape((s...  101 us
    pallas_call x1, Pallas kernels, middle_call(): pl.pallas_call(functools.partial(middle_kernel, count), out_shape=[shape(...  62.8 us
    unnamed x11, local copies, waits for them, and re-layouts  10.5 us
  transfers between devices with their start and end apart: 1, of which 0 were waited for; matrix products, arithmetic and copies ran while one was open for 2% of the time, Pallas kernels for 34%

profile of v5, /device:TPU:0, one launch (start us, length us, event | category | flops | bytes accessed | tf_op | source)
XLA Modules:
  0.0 482.5 jit_solution(1475739719236625936)
XLA Ops:
  7.2 0.0 all-reduce.3.cloned.1.call-start
  7.2 1.6 convert_bitcast_fusion.1.refs_13_
  8.9 1.4 convert_bitcast_fusion
  10.3 0.9 pad.4.refs_4_
  11.2 157.5 %shard_map.255 = (bf16[1536,1024]{1,0:T(8,128)(2,1)}, bf16[1536,3456]{1,0:T(8,128)(2,1)}, bf16[1024,1536]{1,0:T(8,128)(2,1)}, f32[1024,512]{1,0:T(8,128)}, bf16[...) custom-call(bf16[1024,1536]{1,0:T(8,128)(2,1)} %refs_10_.3, ...), custom_call_target="tpu_custom_call" | custom-call | tf_op jit(solution)/shard_map/pallas_call | solution.py:604
  168.7 121.9 %shard_map.256 = (bf16[1536,1792]{1,0:T(8,128)(2,1)}, bf16[1536,1664]{1,0:T(8,128)(2,1)}, bf16[1024,1536]{1,0:T(8,128)(2,1)}, bf16[1024,1536]{1,0:T(8,128)(2,1)}, f32[192,1792]{1,0:T(8,128)}) custom-call(bf16[1024,1536]{1,0:T(8,128)(2,1)} %get-tuple-element.45.refs_0_, bf16[1024,1536]{1,0:T(8,128)(2,1)} %refs_3_.1, ...), custom_call_target="tpu_custom_call" | custom-call | tf_op jit(solution)/shard_map/pallas_call | solution.py:986
  290.6 0.0 all-reduce.3.cloned.1.call-update
  290.6 62.8 %shard_map.257 = (f32[1024,1536]{1,0:T(8,128)}, bf16[6,1024,128]{2,1,0:T(8,128)(2,1)}, bf16[1536,384]{1,0:T(8,128)(2,1)}, f32[192,896]{1,0:T(8,128)}, f32[192,896]{1,0:T(8,128)}, /*index=5*/f32[8,1536]{1,0:T(8,128)}) custom-call(bf16[1536,1792]{1,0:T(8,128)(2,1)} %get-tuple-element.50.refs_0_, bf16[1024,1536]{1,0:T(8,128)(2,1)} %get-tuple-element.51.refs_1_, ...), custom_call_target="tpu_custom_call" | custom-call | tf_op jit(solution)/shard_map/pallas_call | solution.py:1100
  353.4 0.0 copy-start.1
  353.4 0.0 copy-start.2
  353.4 101.1 %shard_map.258 = (f32[1024,1536]{1,0:T(8,128)}, f32[192,832]{1,0:T(8,128)}, f32[192,832]{1,0:T(8,128)}, f32[192,384]{1,0:T(8,128)}, f32[192,640]{1,0:T(8,128)}, /*index=5*/f32[8,256]{1,0:T(8,128)}) custom-call(bf16[1536,1664]{1,0:T(8,128)(2,1)} %get-tuple-element.49.refs_0_, bf16[1536,384]{1,0:T(8,128)(2,1)} %get-tuple-element.56.refs_1_, ...), custom_call_target="tpu_custom_call" | custom-call | tf_op jit(solution)/shard_map/pallas_call | solution.py:1330
  454.5 1.7 slice.27
  456.2 1.3 slice_bitcast_fusion.1
  457.5 1.3 fusion.1
  458.8 1.6 fusion
  460.4 0.0 copy-done.1
  460.4 0.0 copy-done.2
  460.4 0.0 copy-start
  460.4 3.1 pad_maximum_fusion
  463.6 0.0 copy-done
  463.6 1.2 slice_bitcast_fusion
  464.7 0.0 all-reduce.3.cloned.1.call-done
  464.7 3.8 copy.33
  468.5 0.0 copy-start.3
  468.5 6.0 %copy.34 = f32[1024,1536]{1,0:T(8,128)} copy(f32[1024,1536]{1,0:T(8,128)} %get-tuple-element.99) | data formatting | bytes 12582912
  474.5 0.0 copy-done.3
  474.5 0.7 copy.35
Async XLA Ops:
  7.2 457.6 %all-reduce.3.cloned.1.call-start = ((), (), s32[]{:S(2)}) async-start(), calls=%async_computation | async-start | bytes 6291456 | tf_op jit(solution)/shard_map/psum | solution.py:1408
  353.4 107.0 %copy-start.1 = (f32[192,896]{1,0:T(8,128)S(1)}, f32[192,896]{1,0:T(8,128)}, u32[]{:S(2)}) copy-start(f32[192,896]{1,0:T(8,128)} %get-tuple-element.72) | copy-start | bytes 2064388
  353.4 107.0 %copy-start.2 = (f32[192,896]{1,0:T(8,128)S(1)}, f32[192,896]{1,0:T(8,128)}, u32[]{:S(2)}) copy-start(f32[192,896]{1,0:T(8,128)} %get-tuple-element.74) | copy-start | bytes 2064388
  460.4 3.1 copy-start
  468.5 6.0 %copy-start.3 = (f32[192,384]{1,0:T(8,128)S(1)}, f32[192,384]{1,0:T(8,128)}, u32[]{:S(2)}) copy-start(f32[192,384]{1,0:T(8,128)} %get-tuple-element.71) | copy-start | bytes 884740
Sparse Core Ops, SparseCore 0:
  290.7 68.8 all-reduce.2

commit v6 on v5

--- a/solution.py
+++ b/solution.py
@@ -132,7 +132,7 @@
             pl.when(when)(copy.start)
         self.sent.append(make)
 
-    def along(self, way, step, cut, other):
+    def along(self, way, step, cut, other, turn=None):
         place = self.place
         if step >= place.depth - 1:
             return
@@ -145,7 +145,8 @@
                 self.zsend.at[way, step, cut + other], self.zrecv.at[way, step, cut + other],
                 place.me + (NEAR if way == 0 else -NEAR), place.tensor,
             )
-            return copy, more if step == 0 else more & self.valid(way, step)
+            when = more if step == 0 else more & self.valid(way, step)
+            return copy, when if turn is None else when & turn()
 
         self.emit(make)
 
@@ -176,30 +177,44 @@
         self.local().start()
         for cut in reversed(range(len(self.cuts))):
             self.over(0, 0, cut)
-        for cut in range(len(self.cuts)):
-            for way in range(2):
-                self.along(way, 0, cut, 0)
+        for way in range(2):
+            self.along(way, 0, 0, 0)
+            if len(self.cuts) > 1:
+                self.along(way, 0, 1, 0, lambda way=way: jnp.logical_not(self.valid(way, 1)))
+
+    def ends(self, way, step):
+        return self.valid(way, step) & jnp.logical_not(self.valid(way, step + 1))
+
+    def arrive(self, way, step, cut, other):
+        place = self.place
+        spot = self.spot(self.block(way, step, other), cut)
+        copy = remote(
+            spot, spot, self.zsend.at[way, step - 1, cut + other], self.zrecv.at[way, step - 1, cut + other],
+            place.me, place.tensor,
+        )
+        pl.when(self.valid(way, step))(copy.wait_recv)
+        self.along(way, step, cut, other)
 
     def steps(self):
-        place = self.place
-        if len(self.cuts) > 1:
+        late = len(self.cuts) > 1
+        if late:
             self.came_over(0, 0, 1)
             for way in range(2):
-                self.along(way, 0, 1, 1)
+                self.along(way, 0, 1, 1, lambda way=way: jnp.logical_not(self.valid(way, 1)))
             yield
-        for step in range(1, place.depth):
-            for cut in range(len(self.cuts)):
-                for other in range(cut + 1):
+        for step in range(1, self.place.depth):
+            for way in range(2):
+                self.arrive(way, step, 0, 0)
+                self.over(way, step, 0)
+                if late:
+                    for other in range(2):
+                        self.along(way, 0, 1, other, lambda way=way, step=step: self.ends(way, step))
+                yield
+        if late:
+            for step in range(1, self.place.depth):
+                for other in range(2):
                     for way in range(2):
-                        spot = self.spot(self.block(way, step, other), cut)
-                        copy = remote(
-                            spot, spot, self.zsend.at[way, step - 1, cut + other],
-                            self.zrecv.at[way, step - 1, cut + other], place.me, place.tensor,
-                        )
-                        pl.when(self.valid(way, step))(copy.wait_recv)
-                        self.along(way, step, cut, other)
-                        if cut == 0:
-                            self.over(way, step, cut)
+                        self.arrive(way, step, 1, other)
                     yield
 
     def finish(self):
@@ -535,7 +550,8 @@
             return jnp.where(lanes == 2 * pair + 1, sums[1], carry)
 
         lse_ref[rows, :] = lax.fori_loop(0, pairs, attend, jnp.zeros((tile, LANES), F32))
-        next(moves, None)
+        if qb > 1:
+            next(moves, None)
     saves.append(begin(lse_ref, lse_out, copy_sems.at[7]))
     saves.append(begin(ctx_ref, ctx_out, copy_sems.at[8]))
 

time: 492 us -> 483 us (0.982)
  Pallas kernels: 443 us -> 434 us
    pallas_call x1, Pallas kernels: 157 us -> 148 us  [forward_call(): pl.pallas_call(functools.partial(forward_kernel, count), out_shape=[jax.S...]
where the time goes in v6:
time: 483 us; the launch traced here: 474 us
  Pallas kernels  434 us (90%)
  local copies, waits for them, and re-layouts  18.5 us (4%)
  between operations  14.5 us (3%)
  other arithmetic  6.18 us (1%)
    pallas_call x1, Pallas kernels, forward_call(): pl.pallas_call(functools.partial(forward_kernel, count), out_shape=[jax.S...  148 us
    pallas_call x1, Pallas kernels, mlp_call(): pl.pallas_call(functools.partial(mlp_kernel, count, shares), out_shape=[s...  123 us
    pallas_call x1, Pallas kernels, last_call(): pl.pallas_call(functools.partial(last_kernel, count), out_shape=[shape((s...  100 us
    pallas_call x1, Pallas kernels, middle_call(): pl.pallas_call(functools.partial(middle_kernel, count), out_shape=[shape(...  62.8 us
    unnamed x11, local copies, waits for them, and re-layouts  10.5 us
  transfers between devices with their start and end apart: 1, of which 0 were waited for; matrix products, arithmetic and copies ran while one was open for 2% of the time, Pallas kernels for 34%

profile of v6, /device:TPU:0, one launch (start us, length us, event | category | flops | bytes accessed | tf_op | source)
XLA Modules:
  0.0 473.6 jit_solution(11068430693029062295)
XLA Ops:
  7.2 0.0 all-reduce.3.cloned.1.call-start
  7.2 1.6 convert_bitcast_fusion.1.refs_13_
  8.9 1.4 convert_bitcast_fusion
  10.3 0.9 pad.4.refs_4_
  11.2 148.3 %shard_map.255 = (bf16[1536,1024]{1,0:T(8,128)(2,1)}, bf16[1536,3456]{1,0:T(8,128)(2,1)}, bf16[1024,1536]{1,0:T(8,128)(2,1)}, f32[1024,512]{1,0:T(8,128)}, bf16[...) custom-call(bf16[1024,1536]{1,0:T(8,128)(2,1)} %refs_10_.3, ...), custom_call_target="tpu_custom_call" | custom-call | tf_op jit(solution)/shard_map/pallas_call | solution.py:620
  159.5 122.8 %shard_map.256 = (bf16[1536,1792]{1,0:T(8,128)(2,1)}, bf16[1536,1664]{1,0:T(8,128)(2,1)}, bf16[1024,1536]{1,0:T(8,128)(2,1)}, bf16[1024,1536]{1,0:T(8,128)(2,1)}, f32[192,1792]{1,0:T(8,128)}) custom-call(bf16[1024,1536]{1,0:T(8,128)(2,1)} %get-tuple-element.45.refs_0_, bf16[1024,1536]{1,0:T(8,128)(2,1)} %refs_3_.1, ...), custom_call_target="tpu_custom_call" | custom-call | tf_op jit(solution)/shard_map/pallas_call | solution.py:1002
  282.3 0.0 all-reduce.3.cloned.1.call-update
  282.3 62.8 %shard_map.257 = (f32[1024,1536]{1,0:T(8,128)}, bf16[6,1024,128]{2,1,0:T(8,128)(2,1)}, bf16[1536,384]{1,0:T(8,128)(2,1)}, f32[192,896]{1,0:T(8,128)}, f32[192,896]{1,0:T(8,128)}, /*index=5*/f32[8,1536]{1,0:T(8,128)}) custom-call(bf16[1536,1792]{1,0:T(8,128)(2,1)} %get-tuple-element.50.refs_0_, bf16[1024,1536]{1,0:T(8,128)(2,1)} %get-tuple-element.51.refs_1_, ...), custom_call_target="tpu_custom_call" | custom-call | tf_op jit(solution)/shard_map/pallas_call | solution.py:1116
  345.2 0.0 copy-start.1
  345.2 0.0 copy-start.2
  345.2 100.4 %shard_map.258 = (f32[1024,1536]{1,0:T(8,128)}, f32[192,832]{1,0:T(8,128)}, f32[192,832]{1,0:T(8,128)}, f32[192,384]{1,0:T(8,128)}, f32[192,640]{1,0:T(8,128)}, /*index=5*/f32[8,256]{1,0:T(8,128)}) custom-call(bf16[1536,1664]{1,0:T(8,128)(2,1)} %get-tuple-element.49.refs_0_, bf16[1536,384]{1,0:T(8,128)(2,1)} %get-tuple-element.56.refs_1_, ...), custom_call_target="tpu_custom_call" | custom-call | tf_op jit(solution)/shard_map/pallas_call | solution.py:1346
  445.6 1.7 slice.27
  447.3 1.3 slice_bitcast_fusion.1
  448.6 1.3 fusion.1
  449.9 1.6 fusion
  451.6 0.0 copy-done.1
  451.6 0.0 copy-done.2
  451.6 0.0 copy-start
  451.6 3.1 pad_maximum_fusion
  454.7 0.0 copy-done
  454.7 1.2 slice_bitcast_fusion
  455.9 0.0 all-reduce.3.cloned.1.call-done
  455.9 3.8 copy.33
  459.6 0.0 copy-start.3
  459.6 6.0 %copy.34 = f32[1024,1536]{1,0:T(8,128)} copy(f32[1024,1536]{1,0:T(8,128)} %get-tuple-element.99) | data formatting | bytes 12582912
  465.6 0.0 copy-done.3
  465.6 0.7 copy.35
Async XLA Ops:
  7.2 448.7 %all-reduce.3.cloned.1.call-start = ((), (), s32[]{:S(2)}) async-start(), calls=%async_computation | async-start | bytes 6291456 | tf_op jit(solution)/shard_map/psum | solution.py:1424
  345.2 106.4 %copy-start.1 = (f32[192,896]{1,0:T(8,128)S(1)}, f32[192,896]{1,0:T(8,128)}, u32[]{:S(2)}) copy-start(f32[192,896]{1,0:T(8,128)} %get-tuple-element.72) | copy-start | bytes 2064388
  345.2 106.4 %copy-start.2 = (f32[192,896]{1,0:T(8,128)S(1)}, f32[192,896]{1,0:T(8,128)}, u32[]{:S(2)}) copy-start(f32[192,896]{1,0:T(8,128)} %get-tuple-element.74) | copy-start | bytes 2064388
  451.6 3.1 copy-start
  459.6 6.0 %copy-start.3 = (f32[192,384]{1,0:T(8,128)S(1)}, f32[192,384]{1,0:T(8,128)}, u32[]{:S(2)}) copy-start(f32[192,384]{1,0:T(8,128)} %get-tuple-element.71) | copy-start | bytes 884740
Sparse Core Ops, SparseCore 0:
  282.4 67.7 all-reduce.2

commit v7 on v6

--- a/solution.py
+++ b/solution.py
@@ -939,7 +939,7 @@
             cols = pl.ds(pl.multiple_of(index * 4 * LANES + side * 2 * LANES, 2 * LANES), 2 * LANES)
             ab[:, cols] = (ab[:, cols].astype(F32) * jnp.concatenate([piece, piece], axis=1)).astype(BF16)
 
-    polled(even // 2, inner_grad, (sums, {5: 1}))
+    polled(even // 2, inner_grad)
     got = dot_nn(cot_ref[...], w2[:, pl.ds((even - 1) * LANES, 2 * LANES)])
     piece = got[:, :LANES]
     cols = pl.ds(2 * (even - 1) * LANES, 2 * LANES)

time: 483 us -> 479 us (level)
  transfers between devices with their start and end apart: 1 -> 1, of which waited for: 0 -> 0; matrix products, arithmetic and copies ran while one was open for 2% -> 2% of each run, Pallas kernels for 34% -> 35%
where the time goes in v7:
time: 479 us; the launch traced here: 470 us
  Pallas kernels  430 us (90%)
  local copies, waits for them, and re-layouts  18.5 us (4%)
  between operations  14.5 us (3%)
  other arithmetic  6.18 us (1%)
    pallas_call x1, Pallas kernels, forward_call(): pl.pallas_call(functools.partial(forward_kernel, count), out_shape=[jax.S...  148 us
    pallas_call x1, Pallas kernels, mlp_call(): pl.pallas_call(functools.partial(mlp_kernel, count, shares), out_shape=[s...  119 us
    pallas_call x1, Pallas kernels, last_call(): pl.pallas_call(functools.partial(last_kernel, count), out_shape=[shape((s...  101 us
    pallas_call x1, Pallas kernels, middle_call(): pl.pallas_call(functools.partial(middle_kernel, count), out_shape=[shape(...  61.6 us
    unnamed x11, local copies, waits for them, and re-layouts  10.5 us
  transfers between devices with their start and end apart: 1, of which 0 were waited for; matrix products, arithmetic and copies ran while one was open for 2% of the time, Pallas kernels for 35%

profile of v7, /device:TPU:0, one launch (start us, length us, event | category | flops | bytes accessed | tf_op | source)
XLA Modules:
  0.0 469.6 jit_solution(13039602664329936627)
XLA Ops:
  7.2 0.0 all-reduce.3.cloned.1.call-start
  7.2 1.6 convert_bitcast_fusion.1.refs_13_
  8.9 1.4 convert_bitcast_fusion
  10.3 0.9 pad.4.refs_4_
  11.2 148.3 %shard_map.255 = (bf16[1536,1024]{1,0:T(8,128)(2,1)}, bf16[1536,3456]{1,0:T(8,128)(2,1)}, bf16[1024,1536]{1,0:T(8,128)(2,1)}, f32[1024,512]{1,0:T(8,128)}, bf16[...) custom-call(bf16[1024,1536]{1,0:T(8,128)(2,1)} %refs_10_.3, ...), custom_call_target="tpu_custom_call" | custom-call | tf_op jit(solution)/shard_map/pallas_call | solution.py:620
  159.5 119.2 %shard_map.256 = (bf16[1536,1792]{1,0:T(8,128)(2,1)}, bf16[1536,1664]{1,0:T(8,128)(2,1)}, bf16[1024,1536]{1,0:T(8,128)(2,1)}, bf16[1024,1536]{1,0:T(8,128)(2,1)}, f32[192,1792]{1,0:T(8,128)}) custom-call(bf16[1024,1536]{1,0:T(8,128)(2,1)} %get-tuple-element.45.refs_0_, bf16[1024,1536]{1,0:T(8,128)(2,1)} %refs_3_.1, ...), custom_call_target="tpu_custom_call" | custom-call | tf_op jit(solution)/shard_map/pallas_call | solution.py:1002
  278.6 0.0 all-reduce.3.cloned.1.call-update
  278.7 61.6 %shard_map.257 = (f32[1024,1536]{1,0:T(8,128)}, bf16[6,1024,128]{2,1,0:T(8,128)(2,1)}, bf16[1536,384]{1,0:T(8,128)(2,1)}, f32[192,896]{1,0:T(8,128)}, f32[192,896]{1,0:T(8,128)}, /*index=5*/f32[8,1536]{1,0:T(8,128)}) custom-call(bf16[1536,1792]{1,0:T(8,128)(2,1)} %get-tuple-element.50.refs_0_, bf16[1024,1536]{1,0:T(8,128)(2,1)} %get-tuple-element.51.refs_1_, ...), custom_call_target="tpu_custom_call" | custom-call | tf_op jit(solution)/shard_map/pallas_call | solution.py:1116
  340.2 0.0 copy-start.1
  340.2 0.0 copy-start.2
  340.2 101.3 %shard_map.258 = (f32[1024,1536]{1,0:T(8,128)}, f32[192,832]{1,0:T(8,128)}, f32[192,832]{1,0:T(8,128)}, f32[192,384]{1,0:T(8,128)}, f32[192,640]{1,0:T(8,128)}, /*index=5*/f32[8,256]{1,0:T(8,128)}) custom-call(bf16[1536,1664]{1,0:T(8,128)(2,1)} %get-tuple-element.49.refs_0_, bf16[1536,384]{1,0:T(8,128)(2,1)} %get-tuple-element.56.refs_1_, ...), custom_call_target="tpu_custom_call" | custom-call | tf_op jit(solution)/shard_map/pallas_call | solution.py:1346
  441.6 1.7 slice.27
  443.3 1.3 slice_bitcast_fusion.1
  444.5 1.3 fusion.1
  445.9 1.6 fusion
  447.5 0.0 copy-done.1
  447.5 0.0 copy-done.2
  447.5 0.0 copy-start
  447.5 3.1 pad_maximum_fusion
  450.7 0.0 copy-done
  450.7 1.2 slice_bitcast_fusion
  451.8 0.0 all-reduce.3.cloned.1.call-done
  451.8 3.8 copy.33
  455.6 0.0 copy-start.3
  455.6 6.0 %copy.34 = f32[1024,1536]{1,0:T(8,128)} copy(f32[1024,1536]{1,0:T(8,128)} %get-tuple-element.99) | data formatting | bytes 12582912
  461.6 0.0 copy-done.3
  461.6 0.7 copy.35
Async XLA Ops:
  7.2 444.6 %all-reduce.3.cloned.1.call-start = ((), (), s32[]{:S(2)}) async-start(), calls=%async_computation | async-start | bytes 6291456 | tf_op jit(solution)/shard_map/psum | solution.py:1424
  340.2 107.3 %copy-start.1 = (f32[192,896]{1,0:T(8,128)S(1)}, f32[192,896]{1,0:T(8,128)}, u32[]{:S(2)}) copy-start(f32[192,896]{1,0:T(8,128)} %get-tuple-element.72) | copy-start | bytes 2064388
  340.2 107.3 %copy-start.2 = (f32[192,896]{1,0:T(8,128)S(1)}, f32[192,896]{1,0:T(8,128)}, u32[]{:S(2)}) copy-start(f32[192,896]{1,0:T(8,128)} %get-tuple-element.74) | copy-start | bytes 2064388
  447.5 3.1 copy-start
  455.6 6.0 %copy-start.3 = (f32[192,384]{1,0:T(8,128)S(1)}, f32[192,384]{1,0:T(8,128)}, u32[]{:S(2)}) copy-start(f32[192,384]{1,0:T(8,128)} %get-tuple-element.71) | copy-start | bytes 884740
Sparse Core Ops, SparseCore 0:
  278.8 68.1 all-reduce.2
